TPU v7x, 32 devices: a whole 2x2x4 slice. The times are simulated.
32 devices in a mesh: slab: 8 (over z, core), row: 4 (over y, x).
Axes of the slice: x: 2, y: 2, z: 4, core: 2. Of those that a mesh axis runs over, the one named last changes fastest.
Arguments:
- propagator_matrices: float32 [16, 512, 512], P('slab', 'row'), may hold values from -1 to 2
- gain: float32 [512, 128], replicated, may hold values from -0.0546875 to 0.0546875
- obs_matrix: float32 [128, 512], replicated, may hold values from -0.25 to 0.25
- observations: float32 [16, 128], P('slab'), may hold values from -6 to 6
- present: int32 [16], P('slab'), may hold values 0 or 1
- initial: float32 [512], replicated, may hold values from -6 to 6
- smoother_gain: float32 [512, 512], P('row'), may hold values from -1 to 2
Outputs:
- filtered: float32 [16, 512], P('slab')
- smoothed: float32 [16, 512], P('slab')
All inputs are finite; a program needn't handle non-finite values. No bound on the sum of `present` on one device may be relied on, other than what follows from the above.
Results may differ from a plain program's by a relative error of at most 0.00015.
Values sent between devices are 32-bit elements; how exact they have to be, the bound alone decides.
No kernel may reach another device: no remote copies, remote signals or barrier semaphores. Data moves between devices by JAX's collectives and lax.ppermute only.
A program may use at most 192 MiB of HBM per device.

v0:
```python
import jax
import jax.numpy as jnp
from jax import lax
from jax.sharding import PartitionSpec as P


def carried_in(part, axis, combine, identity, reverse):
    count = lax.axis_size(axis)
    place = lax.axis_index(axis)
    ahead = count - 1 - place if reverse else place
    gathered = jax.tree.map(lambda a: lax.all_gather(a, axis), part)
    state = jax.tree.map(lambda a, e: jnp.zeros_like(a) + jnp.asarray(e, a.dtype), part, identity)

    def one(step, state):
        source = count - 1 - step if reverse else step
        return combine(
            state, jax.tree.map(lambda a: lax.dynamic_index_in_dim(a, source, 0, False), gathered)
        )

    return lax.fori_loop(0, ahead, one, state)


def compose(earlier, later):
    greatest_accuracy = lax.Precision.HIGHEST
    return (
        jnp.dot(later[0], earlier[0], precision=greatest_accuracy),
        jnp.dot(later[0], earlier[1], precision=greatest_accuracy) + later[1],
    )


def on_device(propagator_matrices, gain, obs_matrix, observations, present, initial, smoother_gain):
    greatest_accuracy = lax.Precision.HIGHEST
    part_rows = propagator_matrices.shape[1]
    width = propagator_matrices.shape[2]
    epochs_per_group = propagator_matrices.shape[0]
    coupling = jnp.dot(gain, obs_matrix, precision=greatest_accuracy)
    weights = present.astype(jnp.float32)
    drive = jnp.einsum("so,do->sd", observations, gain, precision=greatest_accuracy)
    full_trans, full_smooth = (
        lax.all_gather(propagator_matrices, "row", axis=1, tiled=True),
        lax.all_gather(smoother_gain, "row", axis=0, tiled=True),
    )

    def forward(state, inputs):
        matrix, forced_response, weight = inputs
        pred = jnp.dot(matrix, state, precision=greatest_accuracy)
        new_state = pred + weight * (
            forced_response - jnp.dot(coupling, pred, precision=greatest_accuracy)
        )
        return (new_state, (new_state, new_state - pred))

    def backward(carried, term):
        new_carried = jnp.dot(full_smooth, carried, precision=greatest_accuracy) + term
        return (new_carried, new_carried)

    zeros = jnp.zeros((width,), jnp.float32)
    identity = jnp.eye(width, dtype=jnp.float32)
    local_offset, _ = lax.scan(forward, zeros, (full_trans, drive, weights))
    row_start = lax.axis_index("row") * part_rows
    row_ids = lax.broadcasted_iota(jnp.int32, (part_rows, width), 0) + row_start
    col_ids = lax.broadcasted_iota(jnp.int32, (part_rows, width), 1)
    unit_matrix_lines = (row_ids == col_ids).astype(jnp.float32)

    def postmultiply_operator(carry, inputs):
        matrix, weight = inputs
        mixed = carry - weight * jnp.dot(carry, coupling, precision=greatest_accuracy)
        return (jnp.dot(mixed, matrix, precision=greatest_accuracy), None)

    map_rows, _ = lax.scan(
        postmultiply_operator, unit_matrix_lines, (full_trans, weights), reverse=True
    )
    power_rows = lax.fori_loop(
        0,
        epochs_per_group - 1,
        lambda index, acc: jnp.dot(acc, full_smooth, precision=greatest_accuracy),
        smoother_gain,
    )
    slab_map, power = (
        lax.all_gather(map_rows, "row", axis=0, tiled=True),
        lax.all_gather(power_rows, "row", axis=0, tiled=True),
    )
    prefix_map, prefix_offset = carried_in(
        (slab_map, local_offset), "slab", compose, (identity, zeros), False
    )
    start_state = jnp.dot(prefix_map, initial, precision=greatest_accuracy) + prefix_offset
    _, (filtered, correction) = lax.scan(forward, start_state, (full_trans, drive, weights))
    local_carried, _ = lax.scan(backward, zeros, correction, reverse=True)
    _, next_carried = carried_in((power, local_carried), "slab", compose, (identity, zeros), True)
    _, carried = lax.scan(backward, next_carried, correction, reverse=True)
    smoothed = filtered + carried - correction
    return (filtered, smoothed)


def solution(mesh):
    placed = (P("slab", "row", None), P(), P(), P("slab", None), P("slab"), P(), P("row", None))
    return jax.shard_map(
        on_device,
        mesh=mesh,
        in_specs=placed,
        out_specs=(P("slab", None), P("slab", None)),
        check_vma=False,
    )
```

profile of v0, /device:TPU:0, one launch (start us, length us, event | category | flops | bytes accessed | tf_op | source)
XLA Modules:
  0.0 324.6 jit_solution(9640601542221443507)
XLA Ops:
  7.2 0.7 all-gather.13.cloned.1.call-update
  8.0 0.7 all-gather.17.cloned.1.call-update
  8.7 0.7 convert_element_type.11
  9.5 1.9 fusion.34
  11.4 36.5 %all-gather.13.cloned.1.call-done = f32[2,512,512]{2,1,0:T(8,128)} async-done(((f32[2,128,512]{2,1,0:T(8,128)}), f32[2,512,512]{2,1,0:T(8,128)}) %all-gather.13.cloned.1.call-update) | async-done | bytes 2097168 | tf_op jit(solution)/shard_map/all_gather | solution.py:40
  47.9 7.8 %while.100 = (s32[]{:T(128)}, f32[128,512]{1,0:T(8,128)S(1)}, f32[2]{0:T(128)S(1)}, f32[512,512]{1,0:T(8,128)S(1)}, f32[2,512,512]{2,1,0:T(8,128)}, /*index=5*/s32[]{:T(128)}) while((s32[]{:T(128)}, f32[128,512]{1,0:T(8,128)S(1)}, f32[2]{0:T(128)S(1)}, f32[512,512]{1,0:T(8,128)S(1)}, f32[2,512,512]{2,1,0:T(8,128)}, /*index=5*/s32[]{:T(128)}) %tuple.172), condition=%wide.region_1.2_spmd, body=%wide.region_0.1_spmd.sunk | while | flops 805437440 | bytes 3145829 | solution.py:69
  48.5 1.4 fusion.98
  49.9 1.9 fusion.99
  52.4 1.4 fusion.98
  53.8 1.9 fusion.99
  55.7 0.7 copy-done.2
  56.5 19.9 %all-gather.17.cloned.1.call-done = f32[512,512]{1,0:T(8,128)} async-done(((f32[128,512]{1,0:T(8,128)}), f32[512,512]{1,0:T(8,128)}) %all-gather.17.cloned.1.call-update) | async-done | bytes 1048592 | tf_op jit(solution)/shard_map/all_gather | solution.py:41
  76.4 2.6 fusion.37
  79.1 25.8 %all-gather.15.cloned.1.call-done = f32[512,512]{1,0:T(8,128)} async-done(((f32[128,512]{1,0:T(8,128)}), f32[512,512]{1,0:T(8,128)}) %all-gather.15.cloned.1.call-update) | async-done | bytes 1048592 | tf_op jit(solution)/shard_map/all_gather | solution.py:79
  105.0 28.3 %all-gather.19.cloned.1.call-done = f32[512,512]{1,0:T(8,128)} async-done(((f32[128,512]{1,0:T(8,128)}), f32[512,512]{1,0:T(8,128)}) %all-gather.19.cloned.1.call-update) | async-done | bytes 1048592 | tf_op jit(solution)/shard_map/all_gather | solution.py:80
  133.8 9.1 %while.105 = (s32[]{:T(128)}, f32[512]{0:T(512)S(1)}, f32[2,512,512]{2,1,0:T(8,128)}, f32[2]{0:T(128)S(1)}, f32[2,512]{1,0:T(2,128)S(1)}, /*index=5*/f32[512,512]{1,0:T(8,128)S(1)}, s32[]{:T(128)}, s32[]{:T(128)}) while((s32[]{:T(128)}, f32[512]{0:T(512)S(1)}, f32[2,512,512]{2,1,0:T(8,128)}, f32[2]{0:T(128)S(1)}, ...), condition=%wide.region_3.4_spmd.clone, body=%wide.region_2.3_spmd.clone.sunk | while | flops 6293507 | bytes 2122355 | solution.py:58
  133.8 2.2 fusion.123
  136.0 1.0 fusion.124
  137.6 0.7 multiply_add_fusion.4
  138.3 2.2 fusion.123
  140.6 1.0 fusion.124
  141.6 0.7 dynamic_slice.143
  142.2 0.7 multiply_add_fusion.4
  142.9 12.9 %all-gather.4 = f32[8,1,512]{2,1,0:T(1,128)S(1)} all-gather(f32[1,1,512]{2,1,0:T(1,128)S(1)} %bitcast.205), channel_id=3, replica_groups=mesh['slab'=8,'row'=4] {'slab'}, dimensions={0}, use_global_device_ids=true | all-gather | bytes 18432 | tf_op jit(solution)/shard_map/all_gather | solution.py:11
  155.8 61.1 %all-gather.21.cloned.1.call-done = f32[4096,512]{1,0:T(8,128)} async-done(((f32[512,512]{1,0:T(8,128)}), f32[4096,512]{1,0:T(8,128)}) %all-gather.21.cloned.1.call-update) | async-done | bytes 8388624 | tf_op jit(solution)/shard_map/all_gather | solution.py:11
  216.9 0.7 copy-done.5
  217.6 1.0 fusion.36
  218.6 9.2 %while.102 = (s32[]{:T(128)}, f32[512]{0:T(512)S(1)}, f32[2,512]{1,0:T(2,128)S(1)}, f32[2,512]{1,0:T(2,128)S(1)}, f32[2,512,512]{2,1,0:T(8,128)}, /*index=5*/f32...) while((s32[]{:T(128)}, f32[512]{0:T(512)S(1)}, ...), condition=%wide.region_7.8_spmd, body=%wide.region_6.7_spmd.sunk | while | flops 6293506 | bytes 2128513 | solution.py:86
  218.7 2.2 fusion.110
  220.9 1.0 fusion.111
  223.2 2.3 fusion.110
  225.5 1.0 fusion.111
  227.9 2.1 while.106
  227.9 1.0 fusion.127
  228.9 1.0 fusion.127
  230.0 47.5 %all-gather.5 = f32[8,1,512]{2,1,0:T(1,128)S(1)} all-gather(f32[1,1,512]{2,1,0:T(1,128)S(1)} %bitcast.204), channel_id=5, replica_groups=mesh['slab'=8,'row'=4] {'slab'}, dimensions={0}, use_global_device_ids=true | all-gather | bytes 18432 | tf_op jit(solution)/shard_map/all_gather | solution.py:11
  277.5 21.7 %all-gather.23.cloned.1.call-done = f32[4096,512]{1,0:T(8,128)} async-done(((f32[512,512]{1,0:T(8,128)}), f32[4096,512]{1,0:T(8,128)}) %all-gather.23.cloned.1.call-update) | async-done | bytes 8388624 | tf_op jit(solution)/shard_map/all_gather | solution.py:11
  299.1 15.8 %while.103 = (s32[]{:T(128)}, f32[512]{0:T(512)S(1)}, s32[]{:T(128)}, f32[8,512,512]{2,1,0:T(8,128)}, f32[8,512]{1,0:T(8,128)S(1)}, /*index=5*/s32[]{:T(128)}, s32[]{:T(128)}, s32[]{:T(128)}, s32[]{:T(128)}) while((s32[]{:T(128)}, f32[512]{0:T(512)S(1)}, s32[]{:T(128)}, f32[8,512,512]{2,1,0:T(8,128)}, f32[8,512]{1,0:T(8,128)S(1)}, ...), condition=%wide.region_11.12_spmd, body=%wide.region_10.11_spmd.sunk | while | flops 3146246 | bytes 1063059 | solution.py:20
  299.1 2.2 fusion.115
  301.4 2.2 fusion.115
  303.6 2.2 fusion.115
  305.9 2.2 fusion.115
  308.2 2.2 fusion.115
  310.4 2.2 fusion.115
  312.7 2.2 fusion.115
  315.0 2.1 while.104
  315.0 1.0 fusion.118
  316.1 1.0 fusion.118
  (81 shorter events, 6.4 us)
Async XLA Ops:
  7.2 2.3 copy-start
  7.2 40.7 %all-gather.13.cloned.1.call-start = ((), (), s32[]{:S(2)}) async-start(), calls=%async_computation | async-start | bytes 2621440 | tf_op jit(solution)/shard_map/all_gather | solution.py:40
  7.9 68.5 %all-gather.17.cloned.1.call-start = ((), (), s32[]{:S(2)}) async-start(), calls=%async_computation.2 | async-start | bytes 1310720 | tf_op jit(solution)/shard_map/all_gather | solution.py:41
  8.7 96.3 %all-gather.15.cloned.1.call-start = ((), (), s32[]{:S(2)}) async-start(), calls=%async_computation.1 | async-start | bytes 1310720 | tf_op jit(solution)/shard_map/all_gather | solution.py:79
  11.4 65.0 %copy-start.3 = (f32[128,512]{1,0:T(8,128)S(1)}, f32[128,512]{1,0:T(8,128)}, u32[]{:S(2)}) copy-start(f32[128,512]{1,0:T(8,128)} %param.27) | copy-start | bytes 786436
  47.9 85.5 %copy-start.6 = (f32[2,128]{1,0:T(2,128)S(1)}, f32[2,128]{1,0:T(2,128)}, u32[]{:S(2)}) copy-start(f32[2,128]{1,0:T(2,128)} %param.24) | copy-start | bytes 3076
  55.7 0.7 copy-start.2
  56.5 76.8 %all-gather.19.cloned.1.call-start = ((), (), s32[]{:S(2)}) async-start(), calls=%async_computation.3 | async-start | bytes 1310720 | tf_op jit(solution)/shard_map/all_gather | solution.py:80
  79.1 137.9 %all-gather.21.cloned.1.call-start = ((), (), s32[]{:S(2)}) async-start(), calls=%async_computation.4 | async-start | bytes 9437184 | tf_op jit(solution)/shard_map/all_gather | solution.py:11
  104.9 194.2 %all-gather.23.cloned.1.call-start = ((), (), s32[]{:S(2)}) async-start(), calls=%async_computation.5 | async-start | bytes 9437184 | tf_op jit(solution)/shard_map/all_gather | solution.py:11
  216.9 0.7 copy-start.5
  216.9 10.9 %copy-start.1 = (f32[512,512]{1,0:T(8,128)S(1)}, f32[512,512]{1,0:T(8,128)}, u32[]{:S(2)}) copy-start(f32[512,512]{1,0:T(8,128)} %all-gather.17.cloned.1.call-done) | copy-start | bytes 3145732
  227.8 89.9 %copy-start.4 = (f32[2,512]{1,0:T(2,128)}, f32[2,512]{1,0:T(2,128)S(1)}, u32[]{:S(2)}) copy-start(f32[2,512]{1,0:T(2,128)S(1)} %get-tuple-element.492) | copy-start | bytes 12292
Sparse Core Ops, SparseCore 0:
  9.9 38.0 all-gather.12
  49.7 26.6 all-gather.16
  78.3 26.6 all-gather.14
  106.6 26.6 all-gather.18
  134.7 82.1 all-gather.20
  218.4 80.6 all-gather.22
where the time goes:
time: 326 us; the launch traced here: 325 us
  waiting for transfers between devices  195 us (60%)
  blocking collectives  60.4 us (19%)
  matrix products  44.6 us (14%)
  between operations  14.3 us (4%)
  local copies, waits for them, and re-layouts  5.58 us (2%)
  other arithmetic  4.22 us (1%)
    all_gather x2, waiting for transfers between devices, carried_in(): gathered = jax.tree.map(lambda a: lax.all_gather(a, axis), part)  82.7 us
    all_gather x2, blocking collectives, carried_in(): gathered = jax.tree.map(lambda a: lax.all_gather(a, axis), part)  60.4 us
    all_gather x1, waiting for transfers between devices, on_device(): lax.all_gather(propagator_matrices, 'row', axis=1, tiled=True)  36.5 us
    all_gather x1, waiting for transfers between devices, on_device(): lax.all_gather(power_rows, 'row', axis=0, tiled=True)  28.3 us
    all_gather x1, waiting for transfers between devices, on_device(): lax.all_gather(map_rows, 'row', axis=0, tiled=True)  25.8 us
    all_gather x1, waiting for transfers between devices, on_device(): lax.all_gather(smoother_gain, 'row', axis=0, tiled=True)  19.9 us
    dot_general x7, matrix products, compose(): jnp.dot(later[0], earlier[1], precision=greatest_accuracy) + later[1]  15.4 us
    dot_general x4, matrix products, forward(): pred = jnp.dot(matrix, state, precision=greatest_accuracy)  8.93 us
  transfers between devices with their start and end apart: 6, of which 6 were waited for; matrix products, arithmetic and copies ran while one was open for 11% of the time, Pallas kernels for 0%

commit v1 on v0

v1 whole, which is shorter than its diff:
```python
import jax
import jax.numpy as jnp
from jax import lax
from jax.sharding import PartitionSpec as P

AXES = ("slab", "row")
HIGH = lax.Precision.HIGH


def mm(a, b):
    return jnp.dot(a, b, precision=HIGH)


def by(matrix, rows):
    return lax.dot_general(rows, matrix, (((1,), (1,)), ((), ())), precision=HIGH)


def solution(mesh):
    slabs, parts = mesh.shape["slab"], mesh.shape["row"]
    planes = slabs // 2
    every = [(s, r) for s in range(slabs) for r in range(parts)]

    def send(a, target, which=lambda s: True):
        perm = []
        for s, r in every:
            s_to, r_to = target(s, r)
            if which(s) and 0 <= s_to < slabs:
                perm.append((s * parts + r, s_to * parts + r_to))
        return lax.ppermute(a, AXES, perm)

    def other_core(a):
        return send(a, lambda s, r: (s ^ 1, r))

    def row_parts(block):
        if parts != 4:
            gathered = lax.all_gather(block, "row", axis=0)
            return [gathered[i] for i in range(parts)]
        half = block.shape[0] // 2
        place = lax.axis_index("row")
        from_x = send(block, lambda s, r: (s, r ^ 1))
        from_y = send(block, lambda s, r: (s, r ^ 2))
        far = lax.concatenate(
            [
                send(from_y[:half], lambda s, r: (s, r ^ 1)),
                send(from_x[half:], lambda s, r: (s, r ^ 2)),
            ],
            0,
        )
        x_bit, y_bit = (place & 1) == 1, (place & 2) == 2
        near_0, near_1 = jnp.where(x_bit, from_x, block), jnp.where(x_bit, block, from_x)
        off_0, off_1 = jnp.where(x_bit, far, from_y), jnp.where(x_bit, from_y, far)
        return [
            jnp.where(y_bit, off_0, near_0),
            jnp.where(y_bit, off_1, near_1),
            jnp.where(y_bit, near_0, off_0),
            jnp.where(y_bit, near_1, off_1),
        ]

    def on_device(propagator_matrices, gain, obs_matrix, observations, present, initial, smoother_gain):
        epochs, part_rows, width = propagator_matrices.shape
        place = lax.axis_index("slab")
        plane, odd = place // 2, place % 2 == 1
        weights = present.astype(jnp.float32)
        drive = weights[:, None] * by(gain, observations)
        half = part_rows // 2
        own_half = lax.dynamic_slice_in_dim(smoother_gain, (place % 2) * half, half, 0)
        block = lax.concatenate([propagator_matrices[e] for e in range(epochs)] + [own_half], 0)
        pieces = row_parts(block)
        full = [
            lax.concatenate([p[e * part_rows : (e + 1) * part_rows] for p in pieces], 0)
            for e in range(epochs)
        ]
        smoother_half = jnp.stack([p[epochs * part_rows :] for p in pieces], 0)

        maps, offsets = [], []
        for e in range(epochs):
            step_map = full[e] - weights[e] * mm(gain, mm(obs_matrix, full[e]))
            if e == 0:
                maps.append(step_map)
                offsets.append(drive[0:1])
            else:
                maps.append(mm(step_map, maps[-1]))
                offsets.append(by(step_map, offsets[-1]) + drive[e : e + 1])

        slab_map = lax.concatenate([maps[-1], jnp.pad(offsets[-1], ((0, 7), (0, 0)))], 0)
        else_map = other_core(slab_map)
        first = jnp.where(odd, else_map, slab_map)
        second = jnp.where(odd, slab_map, else_map)
        first_map, first_offset = first[:width], first[width : width + 1]
        second_map, second_offset = second[:width], second[width : width + 1]
        plane_map = mm(second_map, first_map)
        plane_offset = by(second_map, first_offset) + second_offset

        state = initial[None, :]
        for k in range(planes - 1):
            ahead = by(plane_map, state) + plane_offset
            received = send(ahead, lambda s, r: (s + 2, r), lambda s: s // 2 == k)
            state = jnp.where(plane == k + 1, received, state)

        middle = by(first_map, state) + first_offset
        state = jnp.where(odd, middle, state)
        filtered, correction = [], []
        before = state
        for e in range(epochs):
            pred = by(full[e], before)
            before = by(maps[e], state) + offsets[e]
            filtered.append(before)
            correction.append(before - pred)
        filtered = lax.concatenate(filtered, 0)
        correction = lax.concatenate(correction, 0)

        other = other_core(correction)
        own = lax.concatenate(
            [jnp.where(odd, other, correction), jnp.where(odd, correction, other)], 0
        )
        smoother_half, own = lax.optimization_barrier((smoother_half, own))
        terms = [own]
        for k in range(1, planes):
            terms.append(send(own, lambda s, r: (s - 2 * k, r)))

        else_half = other_core(smoother_half)
        smoother = jnp.stack(
            [
                jnp.where(odd, else_half, smoother_half),
                jnp.where(odd, smoother_half, else_half),
            ],
            1,
        ).reshape(width, width)
        count = 2 * epochs * planes
        powers = [smoother]
        while 2 ** len(powers) < count:
            powers.append(mm(powers[-1], powers[-1]))

        carried = lax.concatenate(terms, 0)
        for i, power in enumerate(powers):
            later = jnp.pad(carried[2**i :], ((0, 2**i), (0, 0)))
            carried = carried + by(power, later)
        carried = jnp.where(odd, carried[epochs : 2 * epochs], carried[:epochs])
        return (filtered, filtered + carried - correction)

    placed = (P("slab", "row", None), P(), P(), P("slab", None), P("slab"), P(), P("row", None))
    return jax.shard_map(
        on_device,
        mesh=mesh,
        in_specs=placed,
        out_specs=(P("slab", None), P("slab", None)),
        check_vma=False,
    )
```

time: 326 us -> 85.9 us (0.26)
  waiting for transfers between devices: 195 us -> 34.9 us
  blocking collectives: 60.4 us -> 0 us
  matrix products: 44.6 us -> 16.5 us
  starting transfers between devices: 0.23 us -> 17.2 us
  between operations: 14.3 us -> 1.3 us
  local copies, waits for them, and re-layouts: 5.58 us -> 12.4 us
    all_gather x6 -> x0, waiting for transfers between devices: 193 us -> none  [the longest x2 82.7 us: carried_in(): gathered = jax.tree.map(lambda a: lax.all_gather(a, axis), part)]
    all_gather x2 -> x0, blocking collectives: 60.4 us -> none  [carried_in(): gathered = jax.tree.map(lambda a: lax.all_gather(a, axis), part)]
    ppermute x0 -> x13, waiting for transfers between devices: none -> 34.9 us  [send(): return lax.ppermute(a, AXES, perm)]
    dot_general x27 -> x24, matrix products: 44.6 us -> 16.5 us  [the longest x9 9.62 us: mm(): return jnp.dot(a, b, precision=HIGH)]
    ppermute x0 -> x13, starting transfers between devices: none -> 17.2 us  [send(): return lax.ppermute(a, AXES, perm)]
  transfers between devices with their start and end apart: 6 -> 13, of which waited for: 6 -> 7; matrix products, arithmetic and copies ran while one was open for 11% -> 7% of each run, Pallas kernels for 0% -> 0%
where the time goes in v1:
time: 85.9 us; the launch traced here: 85.5 us
  waiting for transfers between devices  34.9 us (41%)
  starting transfers between devices  17.2 us (20%)
  matrix products  16.5 us (19%)
  local copies, waits for them, and re-layouts  12.4 us (14%)
  other arithmetic  3.21 us (4%)
  between operations  1.3 us (2%)
    ppermute x13, waiting for transfers between devices, send(): return lax.ppermute(a, AXES, perm)  34.9 us
    ppermute x13, starting transfers between devices, send(): return lax.ppermute(a, AXES, perm)  17.2 us
    dot_general x9, matrix products, mm(): return jnp.dot(a, b, precision=HIGH)  9.62 us
    dot_general x15, matrix products, by(): lax.dot_general(rows, matrix, (((1,), (1,)), ((), ())), precision=HIGH)  6.88 us
    unnamed x57, local copies, waits for them, and re-layouts  3.26 us
    another operation x2, local copies, waits for them, and re-layouts, on_device(): smoother_half = jnp.stack([p[epochs * part_rows:] for p in pieces], 0)  2.14 us
    ppermute x3, local copies, waits for them, and re-layouts, send(): return lax.ppermute(a, AXES, perm)  1.94 us
  transfers between devices with their start and end apart: 13, of which 7 were waited for; matrix products, arithmetic and copies ran while one was open for 7% of the time, Pallas kernels for 0%

profile of v1, /device:TPU:0, one launch (start us, length us, event | category | flops | bytes accessed | tf_op | source)
XLA Modules:
  0.0 85.5 jit_solution(1364271390894761540)
XLA Ops:
  0.7 1.0 %constant_dynamic-slice_fusion = f32[64,512]{1,0:T(8,128)S(1)} fusion(f32[128,512]{1,0:T(8,128)} %param.13, s32[]{:T(128)S(6)} %select_n.129), kind=kLoop, calls=%fused_computation.78 | loop fusion | bytes 262148 | tf_op jit(solution)/shard_map/dynamic_slice | solution.py:66
  1.8 1.1 %fusion.41 = (f32[1,128,512]{2,1,0:T(8,128)S(1)}, f32[1,128,512]{2,1,0:T(8,128)S(1)}) fusion(f32[2,128,512]{2,1,0:T(8,128)} %param.7), kind=kLoop, calls=%fused_computation.91 | loop fusion | bytes 1048576 | tf_op jit(solution)/shard_map/slice | solution.py:67
  3.4 3.0 %collective-permute-start.2 = (f32[320,512]{1,0:T(8,128)S(1)}, f32[320,512]{1,0:T(8,128)S(1)}, u32[]{:S(2)}, u32[]{:S(2)}) collective-permute-start(f32[320,512]{1,0:T(8,128)S(1)} %copy.19), channel_id=1, source_target_pairs={{0,1},{1,0},{2,3},{3,2},{4,5},{5,4},{6,7},{7,6},{8,9},{9,8},{10,11... | collective-permute-start | bytes 1966088 | tf_op jit(solution)/shard_map/ppermute | solution.py:29
  6.4 1.5 %collective-permute-start = (f32[320,512]{1,0:T(8,128)S(1)}, f32[320,512]{1,0:T(8,128)}, u32[]{:S(2)}, u32[]{:S(2)}) collective-permute-start(f32[320,512]{1,0:T(8,128)S(1)} %copy.19), channel_id=1, source_target_pairs={{0,2},{1,3},{2,0},{3,1},{4,6},{5,7},{6,4},{7,5},{8,10},{9,11},{10,... | collective-permute-start | bytes 1966088 | tf_op jit(solution)/shard_map/ppermute | solution.py:29
  7.9 13.2 %collective-permute-done.2 = f32[320,512]{1,0:T(8,128)S(1)} collective-permute-done((f32[320,512]{1,0:T(8,128)S(1)}, f32[320,512]{1,0:T(8,128)S(1)}, u32[]{:S(2)}, u32[]{:S(2)}) %collective-permute-start.2) | collective-permute-done | bytes 655392 | tf_op jit(solution)/shard_map/ppermute | solution.py:29
  21.4 1.0 %slice.121 = f32[160,512]{0,1:T(8,128)} slice(f32[320,512]{0,1:T(8,128)S(1)} %copy.22), slice={[160:320], [0:512]} | slice | bytes 655360 | tf_op jit(solution)/shard_map/slice | solution.py:45
  22.5 1.8 %collective-permute-start.3 = (f32[160,512]{0,1:T(8,128)}, f32[160,512]{0,1:T(8,128)S(1)}, u32[]{:S(2)}, u32[]{:S(2)}) collective-permute-start(f32[160,512]{0,1:T(8,128)} %slice.121), channel_id=1, source_target_pairs={{0,2},{1,3},{2,0},{3,1},{4,6},{5,7},{6,4},{7,5},{8,10},{9,11},{10,... | collective-permute-start | bytes 983048 | tf_op jit(solution)/shard_map/ppermute | solution.py:29
  24.2 1.4 %copy.20 = f32[320,512]{0,1:T(8,128)S(1)} copy(f32[320,512]{1,0:T(8,128)} %collective-permute-done) | data formatting | bytes 1310720 | tf_op jit(solution)/shard_map/ppermute | solution.py:29
  25.6 1.6 %collective-permute-start.1 = (f32[160,512]{0,1:T(8,128)S(1)}, f32[160,512]{0,1:T(8,128)S(1)}, u32[]{:S(2)}, u32[]{:S(2)}) collective-permute-start(f32[160,512]{0,1:T(8,128)S(1)} %slice.120), channel_id=1, source_target_pairs={{0,1},{1,0},{2,3},{3,2},{4,5},{5,4},{6,7},{7,6},{8,9},{9,8},{10,11... | collective-permute-start | bytes 983048 | tf_op jit(solution)/shard_map/ppermute | solution.py:29
  27.2 0.6 fusion.42
  28.0 7.9 %collective-permute-done.3 = f32[160,512]{0,1:T(8,128)S(1)} collective-permute-done((f32[160,512]{0,1:T(8,128)}, f32[160,512]{0,1:T(8,128)S(1)}, u32[]{:S(2)}, u32[]{:S(2)}) %collective-permute-start.3) | collective-permute-done | bytes 327712 | tf_op jit(solution)/shard_map/ppermute | solution.py:29
  35.9 2.4 %collective-permute-done.1 = f32[160,512]{0,1:T(8,128)S(1)} collective-permute-done((f32[160,512]{0,1:T(8,128)S(1)}, f32[160,512]{0,1:T(8,128)S(1)}, u32[]{:S(2)}, u32[]{:S(2)}) %collective-permute-start.1) | collective-permute-done | bytes 327712 | tf_op jit(solution)/shard_map/ppermute | solution.py:29
  40.2 0.7 copy-done.25
  40.9 0.6 fusion.14
  41.5 1.3 %fusion.3 = f32[512,512]{0,1:T(8,128)S(1)} fusion(f32[512,128]{1,0:T(8,128)S(1)} %fusion.14, f32[512,128]{1,0:T(8,128)S(1)} %copy-done, f32[]{:T(128)} %bitcast.2, f32[128,512]{0,1:T(8,128)S(1)} %get-tuple-element.35, f32[128,512]{0,1:T(8,128)S(1)} %get-tuple-element.20, f32[128,512]{0,1:T(8,128)S(1)} %get-tuple-element.31, f32[128,512]{0,1:T(8,128)S(1)} %get-tuple-element.16), kind=kOutput, calls=%fused_computation.6 | convolution fusion | flops 202637312 | bytes 2621444 | tf_op jit(solution)/shard_map/dot_general | solution.py:11
  43.2 0.6 fusion.13
  43.8 1.3 %fusion.1 = f32[512,512]{0,1:T(8,128)S(1)} fusion(f32[512,128]{1,0:T(8,128)S(1)} %fusion.13, f32[512,128]{1,0:T(8,128)S(1)} %copy-done, f32[]{:T(128)} %bitcast.4, f32[128,512]{0,1:T(8,128)S(1)} %get-tuple-element.36, f32[128,512]{0,1:T(8,128)S(1)} %get-tuple-element.19, f32[128,512]{0,1:T(8,128)S(1)} %get-tuple-element.32, f32[128,512]{0,1:T(8,128)S(1)} %get-tuple-element.15), kind=kOutput, calls=%fused_computation.3 | convolution fusion | flops 202637312 | bytes 2621444 | tf_op jit(solution)/shard_map/dot_general | solution.py:11
  45.1 1.9 %fusion.43 = f32[512,512]{1,0:T(8,128)S(1)} fusion(f32[512,512]{0,1:T(8,128)S(1)} %fusion.3, f32[512,512]{0,1:T(8,128)S(1)} %fusion.1), kind=kOutput, calls=%fused_computation.93 | convolution fusion | flops 805306368 | bytes 3145728 | tf_op jit(solution)/shard_map/dot_general | solution.py:11
  47.2 2.8 %collective-permute-done.4 = f32[520,512]{1,0:T(8,128)} collective-permute-done((f32[520,512]{1,0:T(8,128)S(1)}, f32[520,512]{1,0:T(8,128)}, u32[]{:S(2)}, u32[]{:S(2)}) %collective-permute-start.4) | collective-permute-done | bytes 1064992 | tf_op jit(solution)/shard_map/ppermute | solution.py:29
  50.0 1.5 %broadcast_select_fusion.1 = (f32[520,512]{1,0:T(8,128)S(1)}, f32[520,512]{1,0:T(8,128)S(1)}) fusion(f32[520,512]{1,0:T(8,128)} %collective-permute-done.4, pred[]{:T(512)S(6)} %eq.21, f32[1,512]{1,0:T(1,128)S(1)} %convolution_add_fusion.11, f32[512,512]{1,0:T(8,128)S(1)} %fusion.43), kind=kLoop, calls=%fused_computation.39 | loop fusion | flops 1331200 | bytes 4245505 | tf_op jit(solution)/shard_map/jit(_where)/select_n | solution.py:88
  51.4 0.5 convolution_add_fusion.9
  52.0 1.0 %fusion.7 = f32[512,512]{1,0:T(8,128)S(1)} fusion(f32[520,512]{1,0:T(8,128)S(1)} %get-tuple-element.12, f32[520,512]{1,0:T(8,128)S(1)} %get-tuple-element.11), kind=kOutput, calls=%fused_computation.32 | convolution fusion | flops 805306368 | bytes 3145728 | tf_op jit(solution)/shard_map/dot_general | solution.py:11
  53.0 0.5 convolution_add_fusion.10
  53.5 3.5 %collective-permute-start.5 = (f32[1,512]{1,0:T(1,128)S(1)}, f32[1,512]{1,0:T(1,128)S(1)}, u32[]{:S(2)}, u32[]{:S(2)}) collective-permute-start(f32[1,512]{1,0:T(1,128)S(1)} %convolution_add_fusion.10), channel_id=1, source_target_pairs={{0,8},{1,9},{2,10},{3,11},{4,12},{5,13},{6,14},{7,15}} | collective-permute-start | bytes 6152 | tf_op jit(solution)/shard_map/ppermute | solution.py:29
  57.0 1.3 %collective-permute-done.5 = f32[1,512]{1,0:T(1,128)S(1)} collective-permute-done((f32[1,512]{1,0:T(1,128)S(1)}, f32[1,512]{1,0:T(1,128)S(1)}, u32[]{:S(2)}, u32[]{:S(2)}) %collective-permute-start.5) | collective-permute-done | bytes 2080 | tf_op jit(solution)/shard_map/ppermute | solution.py:29
  58.3 0.5 convolution_add_fusion.8
  58.8 0.7 collective-permute-start.6
  59.5 1.1 %slice_bitcast_fusion = (f32[1,64,512]{1,2,0:T(8,128)S(1)}, f32[1,64,512]{1,2,0:T(8,128)S(1)}) fusion(f32[320,512]{0,1:T(8,128)} %copy-done.6, f32[320,512]{0,1:T(8,128)} %copy-done.5), kind=kLoop, calls=%fused_computation.48 | loop fusion | bytes 524288 | tf_op jit(solution)/shard_map/stack | solution.py:73
  60.6 0.5 convolution_add_fusion.7
  61.1 1.0 %collective-permute-start.7 = (f32[1,512]{1,0:T(1,128)S(1)}, f32[1,512]{1,0:T(1,128)S(1)}, u32[]{:S(2)}, u32[]{:S(2)}) collective-permute-start(f32[1,512]{1,0:T(1,128)S(1)} %convolution_add_fusion.7), channel_id=1, source_target_pairs={{16,24},{17,25},{18,26},{19,27},{20,28},{21,29},{22,30},{23,31}} | collective-permute-start | bytes 6152 | tf_op jit(solution)/shard_map/ppermute | solution.py:29
  62.1 1.1 %slice_bitcast_fusion.1 = (f32[1,64,512]{1,2,0:T(8,128)S(1)}, f32[1,64,512]{1,2,0:T(8,128)S(1)}) fusion(f32[320,512]{0,1:T(8,128)} %copy-done.4, f32[320,512]{0,1:T(8,128)} %copy-done.3), kind=kLoop, calls=%fused_computation.49 | loop fusion | bytes 524288 | tf_op jit(solution)/shard_map/stack | solution.py:73
  63.2 0.5 fusion.5
  64.1 0.5 convolution_add_fusion.4
  65.3 0.6 copy-done.8
  66.7 1.1 %collective-permute-done.8 = f32[2,512]{1,0:T(2,128)S(1)} collective-permute-done((f32[2,512]{1,0:T(2,128)S(1)}, f32[2,512]{1,0:T(2,128)S(1)}, u32[]{:S(2)}, u32[]{:S(2)}) %collective-permute-start.8) | collective-permute-done | bytes 4128 | tf_op jit(solution)/shard_map/ppermute | solution.py:29
  68.3 1.3 %collective-permute-start.11 = (f32[4,512]{1,0:T(4,128)S(1)}, f32[4,512]{1,0:T(4,128)S(1)}, u32[]{:S(2)}, u32[]{:S(2)}) collective-permute-start(f32[4,512]{1,0:T(4,128)S(1)} %pad_maximum_fusion.11), channel_id=1, source_target_pairs={{24,0},{25,1},{26,2},{27,3},{28,4},{29,5},{30,6},{31,7}} | collective-permute-start | bytes 24584 | tf_op jit(solution)/shard_map/ppermute | solution.py:29
  69.6 1.3 %collective-permute-start.10 = (f32[4,512]{1,0:T(4,128)S(1)}, f32[4,512]{1,0:T(4,128)S(1)}, u32[]{:S(2)}, u32[]{:S(2)}) collective-permute-start(f32[4,512]{1,0:T(4,128)S(1)} %pad_maximum_fusion.11), channel_id=1, source_target_pairs={{16,0},{17,1},{18,2},{19,3},{20,4},{21,5},{22,6},{23,7},{24,8},{25... | collective-permute-start | bytes 24584 | tf_op jit(solution)/shard_map/ppermute | solution.py:29
  70.9 1.3 %collective-permute-start.9 = (f32[4,512]{1,0:T(4,128)S(1)}, f32[4,512]{1,0:T(4,128)S(1)}, u32[]{:S(2)}, u32[]{:S(2)}) collective-permute-start(f32[4,512]{1,0:T(4,128)S(1)} %pad_maximum_fusion.11), channel_id=1, source_target_pairs={{8,0},{9,1},{10,2},{11,3},{12,4},{13,5},{14,6},{15,7},{16,8},{17,9... | collective-permute-start | bytes 24584 | tf_op jit(solution)/shard_map/ppermute | solution.py:29
  72.2 6.2 %collective-permute-done.11 = f32[4,512]{1,0:T(4,128)S(1)} collective-permute-done((f32[4,512]{1,0:T(4,128)S(1)}, f32[4,512]{1,0:T(4,128)S(1)}, u32[]{:S(2)}, u32[]{:S(2)}) %collective-permute-start.11) | collective-permute-done | bytes 8224 | tf_op jit(solution)/shard_map/ppermute | solution.py:29
  79.1 0.6 copy.30
  79.7 1.0 %fusion.44 = f32[512,512]{1,0:T(8,128)S(1)} fusion(f32[512,512]{1,0:T(8,128)S(1)} %bitcast.96), kind=kOutput, calls=%fused_computation.94 | convolution fusion | flops 805306368 | bytes 2097152 | tf_op jit(solution)/shard_map/dot_general | solution.py:11
  80.7 0.5 convolution_add_fusion.3
  81.2 1.0 %fusion.45 = f32[512,512]{1,0:T(8,128)S(1)} fusion(f32[512,512]{1,0:T(8,128)S(1)} %fusion.44), kind=kOutput, calls=%fused_computation.95 | convolution fusion | flops 805306368 | bytes 2097152 | tf_op jit(solution)/shard_map/dot_general | solution.py:11
  82.2 0.5 convolution_add_fusion.2
  82.8 1.0 %fusion.46 = f32[512,512]{1,0:T(8,128)S(1)} fusion(f32[512,512]{1,0:T(8,128)S(1)} %fusion.45), kind=kOutput, calls=%fused_computation.96 | convolution fusion | flops 805306368 | bytes 2097152 | tf_op jit(solution)/shard_map/dot_general | solution.py:11
  83.8 0.5 convolution_add_fusion.1
  84.3 0.5 convolution_add_fusion
  84.9 0.6 fusion.20
  (93 shorter events, 6.6 us)
Async XLA Ops:
  0.6 27.1 %copy-start = (f32[512,128]{1,0:T(8,128)S(1)}, f32[512,128]{1,0:T(8,128)}, u32[]{:S(2)}) copy-start(f32[512,128]{1,0:T(8,128)} %param.8) | copy-start | bytes 786436
  3.2 4.8 %copy-start.26 = (s32[2]{0:T(128)S(1)}, s32[2]{0:T(128)}, u32[]{:S(2)}) copy-start(s32[2]{0:T(128)} %param.11) | copy-start | bytes 28
  3.4 17.7 %collective-permute-start.2 = (f32[320,512]{1,0:T(8,128)S(1)}, f32[320,512]{1,0:T(8,128)S(1)}, u32[]{:S(2)}, u32[]{:S(2)}) collective-permute-start(f32[320,512]{1,0:T(8,128)S(1)} %copy.19), channel_id=1, source_target_pairs={{0,1},{1,0},{2,3},{3,2},{4,5},{5,4},{6,7},{7,6},{8,9},{9,8},{10,11... | collective-permute-start | bytes 1966088 | tf_op jit(solution)/shard_map/ppermute | solution.py:29
  6.4 17.8 %collective-permute-start = (f32[320,512]{1,0:T(8,128)S(1)}, f32[320,512]{1,0:T(8,128)}, u32[]{:S(2)}, u32[]{:S(2)}) collective-permute-start(f32[320,512]{1,0:T(8,128)S(1)} %copy.19), channel_id=1, source_target_pairs={{0,2},{1,3},{2,0},{3,1},{4,6},{5,7},{6,4},{7,5},{8,10},{9,11},{10,... | collective-permute-start | bytes 1966088 | tf_op jit(solution)/shard_map/ppermute | solution.py:29
  22.4 5.3 %copy-start.24 = (f32[2,128]{1,0:T(2,128)S(1)}, f32[2,128]{1,0:T(2,128)}, u32[]{:S(2)}) copy-start(f32[2,128]{1,0:T(2,128)} %param.10) | copy-start | bytes 3076
  22.5 13.4 %collective-permute-start.3 = (f32[160,512]{0,1:T(8,128)}, f32[160,512]{0,1:T(8,128)S(1)}, u32[]{:S(2)}, u32[]{:S(2)}) collective-permute-start(f32[160,512]{0,1:T(8,128)} %slice.121), channel_id=1, source_target_pairs={{0,2},{1,3},{2,0},{3,1},{4,6},{5,7},{6,4},{7,5},{8,10},{9,11},{10,... | collective-permute-start | bytes 983048 | tf_op jit(solution)/shard_map/ppermute | solution.py:29
  25.6 12.7 %collective-permute-start.1 = (f32[160,512]{0,1:T(8,128)S(1)}, f32[160,512]{0,1:T(8,128)S(1)}, u32[]{:S(2)}, u32[]{:S(2)}) collective-permute-start(f32[160,512]{0,1:T(8,128)S(1)} %slice.120), channel_id=1, source_target_pairs={{0,1},{1,0},{2,3},{3,2},{4,5},{5,4},{6,7},{7,6},{8,9},{9,8},{10,11... | collective-permute-start | bytes 983048 | tf_op jit(solution)/shard_map/ppermute | solution.py:29
  38.6 0.9 %copy-start.3 = (f32[320,512]{0,1:T(8,128)}, f32[320,512]{0,1:T(8,128)S(1)}, u32[]{:S(2)}) copy-start(f32[320,512]{0,1:T(8,128)S(1)} %get-tuple-element.9) | copy-start | bytes 1966084
  38.7 1.1 %copy-start.5 = (f32[320,512]{0,1:T(8,128)}, f32[320,512]{0,1:T(8,128)S(1)}, u32[]{:S(2)}) copy-start(f32[320,512]{0,1:T(8,128)S(1)} %get-tuple-element.8) | copy-start | bytes 1966084
  38.7 1.4 %copy-start.4 = (f32[320,512]{0,1:T(8,128)}, f32[320,512]{0,1:T(8,128)S(1)}, u32[]{:S(2)}) copy-start(f32[320,512]{0,1:T(8,128)S(1)} %get-tuple-element.10) | copy-start | bytes 1966084
  38.8 2.8 %copy-start.7 = (f32[128,512]{0,1:T(8,128)}, f32[128,512]{0,1:T(8,128)S(1)}, u32[]{:S(2)}) copy-start(f32[128,512]{0,1:T(8,128)S(1)} %get-tuple-element.16) | copy-start | bytes 786436
  38.8 2.8 %copy-start.9 = (f32[128,512]{0,1:T(8,128)}, f32[128,512]{0,1:T(8,128)S(1)}, u32[]{:S(2)}) copy-start(f32[128,512]{0,1:T(8,128)S(1)} %get-tuple-element.31) | copy-start | bytes 786436
  38.8 5.0 %copy-start.11 = (f32[128,512]{0,1:T(8,128)}, f32[128,512]{0,1:T(8,128)S(1)}, u32[]{:S(2)}) copy-start(f32[128,512]{0,1:T(8,128)S(1)} %get-tuple-element.15) | copy-start | bytes 786436
  38.8 5.0 %copy-start.13 = (f32[128,512]{0,1:T(8,128)}, f32[128,512]{0,1:T(8,128)S(1)}, u32[]{:S(2)}) copy-start(f32[128,512]{0,1:T(8,128)S(1)} %get-tuple-element.32) | copy-start | bytes 786436
  39.8 1.7 %copy-start.6 = (f32[320,512]{0,1:T(8,128)}, f32[320,512]{0,1:T(8,128)S(1)}, u32[]{:S(2)}) copy-start(f32[320,512]{0,1:T(8,128)S(1)} %broadcast_select_fusion.4) | copy-start | bytes 1966084
  39.8 1.1 %copy-start.25 = (f32[128,512]{1,0:T(8,128)S(1)}, f32[128,512]{1,0:T(8,128)}, u32[]{:S(2)}) copy-start(f32[128,512]{1,0:T(8,128)} %param.9) | copy-start | bytes 786436
  40.2 2.6 %copy-start.15 = (f32[128,512]{0,1:T(8,128)}, f32[128,512]{0,1:T(8,128)S(1)}, u32[]{:S(2)}) copy-start(f32[128,512]{0,1:T(8,128)S(1)} %get-tuple-element.20) | copy-start | bytes 786436
  40.2 2.6 %copy-start.17 = (f32[128,512]{0,1:T(8,128)}, f32[128,512]{0,1:T(8,128)S(1)}, u32[]{:S(2)}) copy-start(f32[128,512]{0,1:T(8,128)S(1)} %get-tuple-element.35) | copy-start | bytes 786436
  40.2 3.6 %copy-start.19 = (f32[128,512]{0,1:T(8,128)}, f32[128,512]{0,1:T(8,128)S(1)}, u32[]{:S(2)}) copy-start(f32[128,512]{0,1:T(8,128)S(1)} %get-tuple-element.19) | copy-start | bytes 786436
  40.2 3.6 %copy-start.21 = (f32[128,512]{0,1:T(8,128)}, f32[128,512]{0,1:T(8,128)S(1)}, u32[]{:S(2)}) copy-start(f32[128,512]{0,1:T(8,128)S(1)} %get-tuple-element.36) | copy-start | bytes 786436
  45.1 1.9 %copy-start.1 = (f32[512,512]{0,1:T(8,128)}, f32[512,512]{0,1:T(8,128)S(1)}, u32[]{:S(2)}) copy-start(f32[512,512]{0,1:T(8,128)S(1)} %fusion.1) | copy-start | bytes 3145732
  47.1 2.9 %collective-permute-start.4 = (f32[520,512]{1,0:T(8,128)S(1)}, f32[520,512]{1,0:T(8,128)}, u32[]{:S(2)}, u32[]{:S(2)}) collective-permute-start(f32[520,512]{1,0:T(8,128)S(1)} %select_maximum_fusion), channel_id=1, source_target_pairs={{0,4},{1,5},{2,6},{3,7},{4,0},{5,1},{6,2},{7,3},{8,12},{9,13},{10,... | collective-permute-start | bytes 3194888 | tf_op jit(solution)/shard_map/ppermute | solution.py:29
  52.0 1.0 %copy-start.23 = (f32[512]{0:T(512)S(1)}, f32[512]{0:T(512)}, u32[]{:S(2)}) copy-start(f32[512]{0:T(512)} %param.12) | copy-start | bytes 6148
  53.5 4.8 %collective-permute-start.5 = (f32[1,512]{1,0:T(1,128)S(1)}, f32[1,512]{1,0:T(1,128)S(1)}, u32[]{:S(2)}, u32[]{:S(2)}) collective-permute-start(f32[1,512]{1,0:T(1,128)S(1)} %convolution_add_fusion.10), channel_id=1, source_target_pairs={{0,8},{1,9},{2,10},{3,11},{4,12},{5,13},{6,14},{7,15}} | collective-permute-start | bytes 6152 | tf_op jit(solution)/shard_map/ppermute | solution.py:29
  58.8 1.8 %collective-permute-start.6 = (f32[1,512]{1,0:T(1,128)S(1)}, f32[1,512]{1,0:T(1,128)S(1)}, u32[]{:S(2)}, u32[]{:S(2)}) collective-permute-start(f32[1,512]{1,0:T(1,128)S(1)} %convolution_add_fusion.8), channel_id=1, source_target_pairs={{8,16},{9,17},{10,18},{11,19},{12,20},{13,21},{14,22},{15,23}} | collective-permute-start | bytes 6152 | tf_op jit(solution)/shard_map/ppermute | solution.py:29
  61.1 2.6 %copy-start.2 = (f32[512,512]{0,1:T(8,128)S(1)}, f32[512,512]{0,1:T(8,128)}, u32[]{:S(2)}) copy-start(f32[512,512]{0,1:T(8,128)} %copy-done.1) | copy-start | bytes 3145732
  61.1 2.1 %collective-permute-start.7 = (f32[1,512]{1,0:T(1,128)S(1)}, f32[1,512]{1,0:T(1,128)S(1)}, u32[]{:S(2)}, u32[]{:S(2)}) collective-permute-start(f32[1,512]{1,0:T(1,128)S(1)} %convolution_add_fusion.7), channel_id=1, source_target_pairs={{16,24},{17,25},{18,26},{19,27},{20,28},{21,29},{22,30},{23,31}} | collective-permute-start | bytes 6152 | tf_op jit(solution)/shard_map/ppermute | solution.py:29
  63.7 1.0 %copy-start.12 = (f32[128,512]{0,1:T(8,128)S(1)}, f32[128,512]{0,1:T(8,128)}, u32[]{:S(2)}) copy-start(f32[128,512]{0,1:T(8,128)} %copy-done.11) | copy-start | bytes 786436
  63.7 1.0 %copy-start.14 = (f32[128,512]{0,1:T(8,128)S(1)}, f32[128,512]{0,1:T(8,128)}, u32[]{:S(2)}) copy-start(f32[128,512]{0,1:T(8,128)} %copy-done.13) | copy-start | bytes 786436
  63.7 1.1 %copy-start.20 = (f32[128,512]{0,1:T(8,128)S(1)}, f32[128,512]{0,1:T(8,128)}, u32[]{:S(2)}) copy-start(f32[128,512]{0,1:T(8,128)} %copy-done.19) | copy-start | bytes 786436
  63.7 1.2 %copy-start.22 = (f32[128,512]{0,1:T(8,128)S(1)}, f32[128,512]{0,1:T(8,128)}, u32[]{:S(2)}) copy-start(f32[128,512]{0,1:T(8,128)} %copy-done.21) | copy-start | bytes 786436
  64.9 0.9 %copy-start.8 = (f32[128,512]{0,1:T(8,128)S(1)}, f32[128,512]{0,1:T(8,128)}, u32[]{:S(2)}) copy-start(f32[128,512]{0,1:T(8,128)} %copy-done.7) | copy-start | bytes 786436
  64.9 1.0 %copy-start.10 = (f32[128,512]{0,1:T(8,128)S(1)}, f32[128,512]{0,1:T(8,128)}, u32[]{:S(2)}) copy-start(f32[128,512]{0,1:T(8,128)} %copy-done.9) | copy-start | bytes 786436
  64.9 1.1 %copy-start.16 = (f32[128,512]{0,1:T(8,128)S(1)}, f32[128,512]{0,1:T(8,128)}, u32[]{:S(2)}) copy-start(f32[128,512]{0,1:T(8,128)} %copy-done.15) | copy-start | bytes 786436
  64.9 1.2 %copy-start.18 = (f32[128,512]{0,1:T(8,128)S(1)}, f32[128,512]{0,1:T(8,128)}, u32[]{:S(2)}) copy-start(f32[128,512]{0,1:T(8,128)} %copy-done.17) | copy-start | bytes 786436
  66.5 1.2 %collective-permute-start.8 = (f32[2,512]{1,0:T(2,128)S(1)}, f32[2,512]{1,0:T(2,128)S(1)}, u32[]{:S(2)}, u32[]{:S(2)}) collective-permute-start(f32[2,512]{1,0:T(2,128)S(1)} %pad_maximum_fusion.13), channel_id=1, source_target_pairs={{0,4},{1,5},{2,6},{3,7},{4,0},{5,1},{6,2},{7,3},{8,12},{9,13},{10,... | collective-permute-start | bytes 12296 | tf_op jit(solution)/shard_map/ppermute | solution.py:29
  68.1 10.4 %collective-permute-start.12 = (f32[4,64,512]{2,1,0:T(8,128)S(1)}, f32[4,64,512]{2,1,0:T(8,128)S(1)}, u32[]{:S(2)}, u32[]{:S(2)}) collective-permute-start(f32[4,64,512]{2,1,0:T(8,128)S(1)} %copy.27), channel_id=1, source_target_pairs={{0,4},{1,5},{2,6},{3,7},{4,0},{5,1},{6,2},{7,3},{8,12},{9,13},{10,... | collective-permute-start | bytes 1572872 | tf_op jit(solution)/shard_map/ppermute | solution.py:29
  68.3 10.1 %collective-permute-start.11 = (f32[4,512]{1,0:T(4,128)S(1)}, f32[4,512]{1,0:T(4,128)S(1)}, u32[]{:S(2)}, u32[]{:S(2)}) collective-permute-start(f32[4,512]{1,0:T(4,128)S(1)} %pad_maximum_fusion.11), channel_id=1, source_target_pairs={{24,0},{25,1},{26,2},{27,3},{28,4},{29,5},{30,6},{31,7}} | collective-permute-start | bytes 24584 | tf_op jit(solution)/shard_map/ppermute | solution.py:29
  69.6 8.8 %collective-permute-start.10 = (f32[4,512]{1,0:T(4,128)S(1)}, f32[4,512]{1,0:T(4,128)S(1)}, u32[]{:S(2)}, u32[]{:S(2)}) collective-permute-start(f32[4,512]{1,0:T(4,128)S(1)} %pad_maximum_fusion.11), channel_id=1, source_target_pairs={{16,0},{17,1},{18,2},{19,3},{20,4},{21,5},{22,6},{23,7},{24,8},{25... | collective-permute-start | bytes 24584 | tf_op jit(solution)/shard_map/ppermute | solution.py:29
  70.9 7.5 %collective-permute-start.9 = (f32[4,512]{1,0:T(4,128)S(1)}, f32[4,512]{1,0:T(4,128)S(1)}, u32[]{:S(2)}, u32[]{:S(2)}) collective-permute-start(f32[4,512]{1,0:T(4,128)S(1)} %pad_maximum_fusion.11), channel_id=1, source_target_pairs={{8,0},{9,1},{10,2},{11,3},{12,4},{13,5},{14,6},{15,7},{16,8},{17,9... | collective-permute-start | bytes 24584 | tf_op jit(solution)/shard_map/ppermute | solution.py:29

commit v2 on v1

v2 whole, which is shorter than its diff:
```python
import jax
import jax.numpy as jnp
from jax import lax
from jax.sharding import PartitionSpec as P

AXES = ("slab", "row")
HIGH = lax.Precision.HIGH


def mm(a, b):
    return jnp.dot(a, b, precision=HIGH)


def by(matrix, rows):
    return lax.dot_general(rows, matrix, (((1,), (1,)), ((), ())), precision=HIGH)


def in_order(pieces, place):
    bit = 1
    while bit < len(pieces):
        crossed = (place & bit) != 0
        pieces = [jnp.where(crossed, pieces[i ^ bit], pieces[i]) for i in range(len(pieces))]
        bit *= 2
    return pieces


def after(value, *others):
    return lax.optimization_barrier((value, others))[0]


def solution(mesh):
    slabs, parts = mesh.shape["slab"], mesh.shape["row"]
    planes = slabs // 2
    every = [(s, r) for s in range(slabs) for r in range(parts)]

    def send(a, target, which=lambda s: True):
        perm = []
        for s, r in every:
            s_to, r_to = target(s, r)
            if which(s) and 0 <= s_to < slabs:
                perm.append((s * parts + r, s_to * parts + r_to))
        return lax.ppermute(a, AXES, perm)

    def other_core(a):
        return send(a, lambda s, r: (s ^ 1, r))

    def along(a, bit):
        return send(a, lambda s, r: (s, r ^ bit))

    def over_planes(a):
        return [a] + [send(a, lambda s, r: (s ^ (2 * k), r)) for k in range(1, planes)]

    def on_device(propagator_matrices, gain, obs_matrix, observations, present, initial, smoother_gain):
        epochs, part_rows, width = propagator_matrices.shape
        place, part = lax.axis_index("slab"), lax.axis_index("row")
        plane, odd = place // 2, place % 2 == 1

        share = part_rows // slabs
        own_share = lax.dynamic_slice_in_dim(smoother_gain, place * share, share, 0)

        if parts == 4:
            from_x, from_y = along(propagator_matrices, 1), along(propagator_matrices, 2)
            shares = [own_share] + [along(own_share, bit) for bit in (1, 2, 3)]
            shares = jnp.stack(in_order(shares, part), 0)
            plane_shares = over_planes(shares)
            mid = epochs // 2
            next_x, next_y = after((from_x[mid:], from_y[:mid]), shares)
            far = lax.concatenate([along(next_y, 1), along(next_x, 2)], 0)
            plane_shares, far = lax.optimization_barrier((plane_shares, far))
            pieces = [propagator_matrices, from_x, from_y, far]
            full = lax.concatenate(in_order(pieces, part), 1)
        else:
            full = lax.all_gather(propagator_matrices, "row", axis=1, tiled=True)
            plane_shares = over_planes(lax.all_gather(own_share, "row", axis=0))

        weights = present.astype(jnp.float32)
        drive = weights[:, None] * by(gain, observations)
        taken = [-weights[e] * gain for e in range(epochs)]
        unit = jnp.eye(width, dtype=jnp.float32)
        update = [unit + mm(taken[e], obs_matrix) for e in range(epochs)]

        reach, maps = [], []
        for e in range(epochs):
            reach.append(mm(full[e], maps[-1]) if e else full[e])
            maps.append(mm(update[e], reach[e]))
        slab_map = maps[-1]
        else_map = other_core(slab_map)

        reach = after(reach, slab_map)
        offsets, seen, seen_0 = [], [], []
        for e in range(epochs):
            if e == 0:
                seen_0.append(jnp.zeros((1, obs_matrix.shape[0]), jnp.float32))
                offsets.append(drive[0:1])
            else:
                reach_0 = by(full[e], offsets[-1])
                seen_0.append(by(obs_matrix, reach_0))
                offsets.append(reach_0 + by(taken[e], seen_0[e]) + drive[e : e + 1])
            seen.append(mm(obs_matrix, reach[e]))
        slab_offset = offsets[-1]

        else_offset = other_core(slab_offset)
        plane_map = mm(jnp.where(odd, slab_map, else_map), jnp.where(odd, else_map, slab_map))
        plane_offset = jnp.where(
            odd, by(slab_map, else_offset) + slab_offset, by(else_map, slab_offset) + else_offset
        )

        state = initial[None, :]
        for k in range(planes - 1):
            ahead = by(plane_map, state) + plane_offset
            received = send(ahead, lambda s, r: (s + 2, r), lambda s: s // 2 == k)
            state = jnp.where(plane == k + 1, received, state)

        state = jnp.where(odd, by(else_map, state) + else_offset, state)
        correction = lax.concatenate(
            [
                by(taken[e], by(seen[e], state) + seen_0[e]) + drive[e : e + 1]
                for e in range(epochs)
            ],
            0,
        )
        other = other_core(correction)
        own = lax.concatenate(
            [jnp.where(odd, other, correction), jnp.where(odd, correction, other)], 0
        )
        terms = [own]
        for k in range(1, planes):
            terms.append(send(own, lambda s, r: (s - 2 * k, r)))

        state = after(state, own)
        filtered = lax.concatenate([by(maps[e], state) + offsets[e] for e in range(epochs)], 0)

        mine = after(jnp.stack(in_order(plane_shares, plane), 0), own)
        theirs = other_core(mine)
        smoother = jnp.stack(in_order([mine, theirs], place % 2), 1)
        smoother = smoother.transpose(2, 0, 1, 3, 4).reshape(width, width)
        count = 2 * epochs * planes
        powers = [smoother]
        while 2 ** len(powers) < count:
            powers.append(mm(powers[-1], powers[-1]))
        terms, powers = lax.optimization_barrier((terms, powers))

        carried = lax.concatenate(terms, 0)
        for i, power in enumerate(powers):
            later = jnp.pad(carried[2**i :], ((0, 2**i), (0, 0)))
            carried = carried + by(power, later)
        carried = jnp.where(odd, carried[epochs : 2 * epochs], carried[:epochs])
        return (filtered, filtered + carried - correction)

    placed = (P("slab", "row", None), P(), P(), P("slab", None), P("slab"), P(), P("row", None))
    return jax.shard_map(
        on_device,
        mesh=mesh,
        in_specs=placed,
        out_specs=(P("slab", None), P("slab", None)),
        check_vma=False,
    )
```

time: 85.9 us -> 72.1 us (0.84)
  the two profiles are of different devices: /device:TPU:0 before, /device:TPU:25 now
where the time goes in v2:
time: 72.1 us; the launch traced here: 71.7 us
  starting transfers between devices  23.6 us (33%)
  matrix products  20.6 us (29%)
  waiting for transfers between devices  16.6 us (23%)
  other arithmetic  6.07 us (8%)
  local copies, waits for them, and re-layouts  2.49 us (3%)
  between operations  2.36 us (3%)
    ppermute x20, starting transfers between devices, send(): return lax.ppermute(a, AXES, perm)  23.6 us
    ppermute x20, waiting for transfers between devices, send(): return lax.ppermute(a, AXES, perm)  16.6 us
    dot_general x11, matrix products, mm(): return jnp.dot(a, b, precision=HIGH)  12.3 us
    dot_general x20, matrix products, by(): lax.dot_general(rows, matrix, (((1,), (1,)), ((), ())), precision=HIGH)  8.28 us
  transfers between devices with their start and end apart: 20, of which 7 were waited for; matrix products, arithmetic and copies ran while one was open for 22% of the time, Pallas kernels for 0%

profile of v2, /device:TPU:25, one launch (start us, length us, event | category | flops | bytes accessed | tf_op | source)
XLA Modules:
  0.0 71.7 jit_solution(5894669327300130822)
XLA Ops:
  0.7 0.8 %constant_dynamic-slice_fusion = f32[16,512]{1,0:T(8,128)S(1)} fusion(f32[128,512]{1,0:T(8,128)} %param.13, s32[]{:T(128)S(6)} %select_n.211), kind=kLoop, calls=%fused_computation.106 | loop fusion | bytes 65540 | tf_op jit(solution)/shard_map/dynamic_slice | solution.py:59
  1.5 1.2 %collective-permute-start.2 = (f32[16,512]{1,0:T(8,128)S(1)}, f32[16,512]{1,0:T(8,128)S(1)}, u32[]{:S(2)}, u32[]{:S(2)}) collective-permute-start(f32[16,512]{1,0:T(8,128)S(1)} %constant_dynamic-slice_fusion), channel_id=1, source_target_pairs={{0,1},{1,0},{2,3},{3,2},{4,5},{5,4},{6,7},{7,6},{8,9},{9,8},{10,11... | collective-permute-start | bytes 98312 | tf_op jit(solution)/shard_map/ppermute | solution.py:42
  2.7 1.2 %collective-permute-start.1 = (f32[16,512]{1,0:T(8,128)S(1)}, f32[16,512]{1,0:T(8,128)S(1)}, u32[]{:S(2)}, u32[]{:S(2)}) collective-permute-start(f32[16,512]{1,0:T(8,128)S(1)} %constant_dynamic-slice_fusion), channel_id=1, source_target_pairs={{0,2},{1,3},{2,0},{3,1},{4,6},{5,7},{6,4},{7,5},{8,10},{9,11},{10,... | collective-permute-start | bytes 98312 | tf_op jit(solution)/shard_map/ppermute | solution.py:42
  4.1 1.2 %collective-permute-start.6 = (f32[2,128,512]{2,1,0:T(8,128)}, f32[2,128,512]{2,1,0:T(8,128)S(1)}, u32[]{:S(2)}, u32[]{:S(2)}) collective-permute-start(f32[2,128,512]{2,1,0:T(8,128)} %param.7), channel_id=1, source_target_pairs={{0,1},{1,0},{2,3},{3,2},{4,5},{5,4},{6,7},{7,6},{8,9},{9,8},{10,11... | collective-permute-start | bytes 1572872 | tf_op jit(solution)/shard_map/ppermute | solution.py:42
  5.3 1.2 %collective-permute-start.7 = (f32[2,128,512]{2,1,0:T(8,128)}, f32[2,128,512]{2,1,0:T(8,128)S(1)}, u32[]{:S(2)}, u32[]{:S(2)}) collective-permute-start(f32[2,128,512]{2,1,0:T(8,128)} %param.7), channel_id=1, source_target_pairs={{0,2},{1,3},{2,0},{3,1},{4,6},{5,7},{6,4},{7,5},{8,10},{9,11},{10,... | collective-permute-start | bytes 1572872 | tf_op jit(solution)/shard_map/ppermute | solution.py:42
  6.6 0.7 convert_element_type.17
  7.2 0.6 fusion.46
  8.5 2.5 %convert_add_fusion.1 = f32[512,512]{1,0:T(8,128)} fusion(f32[128,512]{1,0:T(8,128)S(1)} %copy-done, f32[512,128]{1,0:T(8,128)} %param.8, f32[]{:T(128)} %bitcast), kind=kOutput, calls=%fused_computation.2 | convolution fusion | flops 202178560 | bytes 1572868 | tf_op jit(solution)/shard_map/dot_general | solution.py:11
  11.7 0.8 %select_bitcast_fusion.9 = (f32[1,16,512]{2,1,0:T(8,128)S(1)}, f32[1,16,512]{2,1,0:T(8,128)S(1)}, f32[1,16,512]{2,1,0:T(8,128)S(1)}, f32[1,16,512]{2,1,0:T(8,128)S(1)}) fusion(pred[]{:T(512)S(6)} %ne.33, f32[16,512]{1,0:T(8,128)S(1)} %collective-permute-done, f32[16,512]{1,0:T(8,128)S(1)} %collective-permute-done.1, pred[]{:T(512)S(6)} %ne.34, ...), kind=kLoop, calls=%fused_computation.76 | loop fusion | flops 65536 | bytes 262150 | tf_op jit(solution)/shard_map/stack | solution.py:64
  12.5 4.4 %collective-permute-done.6 = f32[2,128,512]{2,1,0:T(8,128)S(1)} collective-permute-done((f32[2,128,512]{2,1,0:T(8,128)}, f32[2,128,512]{2,1,0:T(8,128)S(1)}, u32[]{:S(2)}, u32[]{:S(2)}) %collective-permute-start.6) | collective-permute-done | bytes 524320 | tf_op jit(solution)/shard_map/ppermute | solution.py:42
  17.0 0.9 %collective-permute-done.7 = f32[2,128,512]{2,1,0:T(8,128)S(1)} collective-permute-done((f32[2,128,512]{2,1,0:T(8,128)}, f32[2,128,512]{2,1,0:T(8,128)S(1)}, u32[]{:S(2)}, u32[]{:S(2)}) %collective-permute-start.7) | collective-permute-done | bytes 524320 | tf_op jit(solution)/shard_map/ppermute | solution.py:42
  17.9 0.7 %slice.60 = f32[1,128,512]{2,1,0:T(8,128)} slice(f32[2,128,512]{2,1,0:T(8,128)S(1)} %collective-permute-done.7), slice={[0:1], [0:128], [0:512]} | slice | bytes 524288 | tf_op jit(solution)/shard_map/slice | solution.py:67
  18.9 1.2 %collective-permute-start.9 = (f32[1,128,512]{2,1,0:T(8,128)S(1)}, f32[1,128,512]{2,1,0:T(8,128)}, u32[]{:S(2)}, u32[]{:S(2)}) collective-permute-start(f32[1,128,512]{2,1,0:T(8,128)S(1)} %slice.59), channel_id=1, source_target_pairs={{0,2},{1,3},{2,0},{3,1},{4,6},{5,7},{6,4},{7,5},{8,10},{9,11},{10,... | collective-permute-start | bytes 786440 | tf_op jit(solution)/shard_map/ppermute | solution.py:42
  20.2 0.6 convert_add_fusion
  20.8 1.3 %collective-permute-start.4 = (f32[4,16,512]{2,1,0:T(8,128)S(1)}, f32[4,16,512]{2,1,0:T(8,128)}, u32[]{:S(2)}, u32[]{:S(2)}) collective-permute-start(f32[4,16,512]{2,1,0:T(8,128)S(1)} %pad_maximum_fusion.4), channel_id=1, source_target_pairs={{0,16},{1,17},{2,18},{3,19},{4,20},{5,21},{6,22},{7,23},{8,24},{9,... | collective-permute-start | bytes 393224 | tf_op jit(solution)/shard_map/ppermute | solution.py:42
  22.1 2.2 %collective-permute-start.3 = (f32[4,16,512]{2,1,0:T(8,128)S(1)}, f32[4,16,512]{2,1,0:T(8,128)}, u32[]{:S(2)}, u32[]{:S(2)}) collective-permute-start(f32[4,16,512]{2,1,0:T(8,128)S(1)} %pad_maximum_fusion.4), channel_id=1, source_target_pairs={{0,8},{1,9},{2,10},{3,11},{4,12},{5,13},{6,14},{7,15},{8,0},{9,1},... | collective-permute-start | bytes 393224 | tf_op jit(solution)/shard_map/ppermute | solution.py:42
  24.6 1.1 %pad_maximum_fusion.2 = f32[2,128,512]{2,1,0:T(8,128)S(1)} fusion(f32[1,128,512]{2,1,0:T(8,128)} %collective-permute-done.9, f32[1,128,512]{2,1,0:T(8,128)} %collective-permute-done.8), kind=kLoop, calls=%fused_computation.35 | loop fusion | flops 131072 | bytes 1048576 | tf_op jit(solution)/shard_map/concatenate | solution.py:68
  25.6 1.1 %collective-permute-done.5 = f32[4,16,512]{2,1,0:T(8,128)} collective-permute-done((f32[4,16,512]{2,1,0:T(8,128)S(1)}, f32[4,16,512]{2,1,0:T(8,128)}, u32[]{:S(2)}, u32[]{:S(2)}) %collective-permute-start.5) | collective-permute-done | bytes 131104 | tf_op jit(solution)/shard_map/ppermute | solution.py:42
  26.7 5.6 %collective-permute-done.4 = f32[4,16,512]{2,1,0:T(8,128)} collective-permute-done((f32[4,16,512]{2,1,0:T(8,128)S(1)}, f32[4,16,512]{2,1,0:T(8,128)}, u32[]{:S(2)}, u32[]{:S(2)}) %collective-permute-start.4) | collective-permute-done | bytes 131104 | tf_op jit(solution)/shard_map/ppermute | solution.py:42
  32.8 1.0 %fusion.45 = f32[512,512]{1,0:T(8,128)S(1)} fusion(f32[512,512]{1,0:T(8,128)S(1)} %convert_add_fusion, f32[2,512,512]{2,1,0:T(8,128)S(1)} %pad_maximum_fusion), kind=kOutput, calls=%fused_computation.112 | convolution fusion | flops 805306368 | bytes 3145728 | tf_op jit(solution)/shard_map/dot_general | solution.py:11
  33.9 1.0 %fusion.8 = f32[512,512]{1,0:T(8,128)S(1)} fusion(f32[512,512]{1,0:T(8,128)S(1)} %fusion.45, f32[2,512,512]{2,1,0:T(8,128)S(1)} %pad_maximum_fusion), kind=kOutput, calls=%fused_computation.34 | convolution fusion | flops 805306368 | bytes 3145728 | tf_op jit(solution)/shard_map/dot_general | solution.py:11
  35.1 1.0 %fusion.47 = f32[512,512]{1,0:T(8,128)S(1)} fusion(f32[512,512]{1,0:T(8,128)S(1)} %copy-done.2, f32[512,512]{1,0:T(8,128)S(1)} %fusion.8), kind=kOutput, calls=%fused_computation.114 | convolution fusion | flops 805306368 | bytes 3145728 | tf_op jit(solution)/shard_map/dot_general | solution.py:11
  36.2 2.8 %collective-permute-start.10 = (f32[512,512]{1,0:T(8,128)S(1)}, f32[512,512]{1,0:T(8,128)S(1)}, u32[]{:S(2)}, u32[]{:S(2)}) collective-permute-start(f32[512,512]{1,0:T(8,128)S(1)} %fusion.47), channel_id=1, source_target_pairs={{0,4},{1,5},{2,6},{3,7},{4,0},{5,1},{6,2},{7,3},{8,12},{9,13},{10,... | collective-permute-start | bytes 3145736 | tf_op jit(solution)/shard_map/ppermute | solution.py:42
  40.2 1.1 %collective-permute-done.11 = f32[1,512]{1,0:T(1,128)S(1)} collective-permute-done((f32[1,512]{1,0:T(1,128)S(1)}, f32[1,512]{1,0:T(1,128)S(1)}, u32[]{:S(2)}, u32[]{:S(2)}) %collective-permute-start.11) | collective-permute-done | bytes 2080 | tf_op jit(solution)/shard_map/ppermute | solution.py:42
  41.3 0.5 convolution_add_fusion.11
  41.8 1.1 %fusion.4 = f32[512,512]{1,0:T(8,128)S(1)} fusion(f32[512,512]{1,0:T(8,128)S(1)} %collective-permute-done.10, f32[512,512]{1,0:T(8,128)S(1)} %fusion.47, pred[]{:T(512)S(6)} %eq.20), kind=kOutput, calls=%fused_computation.29 | convolution fusion | flops 805830656 | bytes 3145729 | tf_op jit(solution)/shard_map/dot_general | solution.py:11
  43.4 0.5 convolution_add_fusion.13
  44.0 0.7 collective-permute-start.12
  44.6 1.0 %convolution_bitcast_fusion.1 = f32[128,512]{0,1:T(8,128)S(1)} fusion(f32[512,512]{1,0:T(8,128)S(1)} %slice_bitcast_fusion, f32[128,512]{1,0:T(8,128)S(1)} %copy-done), kind=kOutput, calls=%fused_computation.4 | convolution fusion | flops 201326592 | bytes 1572864 | tf_op jit(solution)/shard_map/dot_general | solution.py:11
  45.7 0.5 convolution_add_fusion.10
  46.2 0.7 collective-permute-start.13
  46.9 1.0 %convolution_bitcast_fusion = f32[128,512]{0,1:T(8,128)S(1)} fusion(f32[512,512]{1,0:T(8,128)S(1)} %fusion.8, f32[128,512]{1,0:T(8,128)S(1)} %copy-done), kind=kOutput, calls=%fused_computation.3 | convolution fusion | flops 201326592 | bytes 1572864 | tf_op jit(solution)/shard_map/dot_general | solution.py:11
  47.9 0.5 convolution_add_fusion.9
  48.4 1.5 %collective-permute-start.14 = (f32[1,512]{1,0:T(1,128)S(1)}, f32[1,512]{1,0:T(1,128)S(1)}, u32[]{:S(2)}, u32[]{:S(2)}) collective-permute-start(f32[1,512]{1,0:T(1,128)S(1)} %convolution_add_fusion.9), channel_id=1, source_target_pairs={{16,24},{17,25},{18,26},{19,27},{20,28},{21,29},{22,30},{23,31}} | collective-permute-start | bytes 6152 | tf_op jit(solution)/shard_map/ppermute | solution.py:42
  49.9 1.1 %select_bitcast_fusion.5 = (f32[1,4,16,512]{3,2,0,1:T(8,128)S(1)}, f32[1,4,16,512]{3,2,0,1:T(8,128)S(1)}, f32[1,4,16,512]{3,2,0,1:T(8,128)S(1)}, f32[1,4,16,512]{3,2,0,1:T(8,128)S(1)}) fusion(pred[]{:T(512)S(6)} %ne.36, f32[4,16,512]{2,1,0:T(8,128)} %collective-permute-done.5, f32[4,16,512]{2,1,0:T(8,128)} %collective-permute-done.4, pred[]{:T(512)S(6)} %ne.37, ...), kind=kLoop, calls=%fused_computation.58 | loop fusion | flops 262144 | bytes 1048578 | tf_op jit(solution)/shard_map/stack | solution.py:133
  51.0 2.6 %collective-permute-done.14 = f32[1,512]{1,0:T(1,128)S(1)} collective-permute-done((f32[1,512]{1,0:T(1,128)S(1)}, f32[1,512]{1,0:T(1,128)S(1)}, u32[]{:S(2)}, u32[]{:S(2)}) %collective-permute-start.14) | collective-permute-done | bytes 2080 | tf_op jit(solution)/shard_map/ppermute | solution.py:42
  53.6 0.5 fusion
  55.0 3.3 %collective-permute-start.15 = (f32[2,512]{1,0:T(2,128)S(1)}, f32[2,512]{1,0:T(2,128)S(1)}, u32[]{:S(2)}, u32[]{:S(2)}) collective-permute-start(f32[2,512]{1,0:T(2,128)S(1)} %pad_maximum_fusion.7), channel_id=1, source_target_pairs={{0,4},{1,5},{2,6},{3,7},{4,0},{5,1},{6,2},{7,3},{8,12},{9,13},{10,... | collective-permute-start | bytes 12296 | tf_op jit(solution)/shard_map/ppermute | solution.py:42
  58.4 0.8 %collective-permute-done.15 = f32[2,512]{1,0:T(2,128)S(1)} collective-permute-done((f32[2,512]{1,0:T(2,128)S(1)}, f32[2,512]{1,0:T(2,128)S(1)}, u32[]{:S(2)}, u32[]{:S(2)}) %collective-permute-start.15) | collective-permute-done | bytes 4128 | tf_op jit(solution)/shard_map/ppermute | solution.py:42
  59.6 1.3 %collective-permute-start.18 = (f32[4,512]{1,0:T(4,128)S(1)}, f32[4,512]{1,0:T(4,128)S(1)}, u32[]{:S(2)}, u32[]{:S(2)}) collective-permute-start(f32[4,512]{1,0:T(4,128)S(1)} %pad_maximum_fusion.6), channel_id=1, source_target_pairs={{24,0},{25,1},{26,2},{27,3},{28,4},{29,5},{30,6},{31,7}} | collective-permute-start | bytes 24584 | tf_op jit(solution)/shard_map/ppermute | solution.py:42
  60.9 1.3 %collective-permute-start.17 = (f32[4,512]{1,0:T(4,128)S(1)}, f32[4,512]{1,0:T(4,128)S(1)}, u32[]{:S(2)}, u32[]{:S(2)}) collective-permute-start(f32[4,512]{1,0:T(4,128)S(1)} %pad_maximum_fusion.6), channel_id=1, source_target_pairs={{16,0},{17,1},{18,2},{19,3},{20,4},{21,5},{22,6},{23,7},{24,8},{25... | collective-permute-start | bytes 24584 | tf_op jit(solution)/shard_map/ppermute | solution.py:42
  62.2 1.3 %collective-permute-start.16 = (f32[4,512]{1,0:T(4,128)S(1)}, f32[4,512]{1,0:T(4,128)S(1)}, u32[]{:S(2)}, u32[]{:S(2)}) collective-permute-start(f32[4,512]{1,0:T(4,128)S(1)} %pad_maximum_fusion.6), channel_id=1, source_target_pairs={{8,0},{9,1},{10,2},{11,3},{12,4},{13,5},{14,6},{15,7},{16,8},{17,9... | collective-permute-start | bytes 24584 | tf_op jit(solution)/shard_map/ppermute | solution.py:42
  64.0 0.5 convolution_add_fusion.5
  64.5 1.2 %select_bitcast_fusion.1 = (f32[4,1,4,16,512]{4,3,1,0,2:T(8,128)S(1)}, f32[4,1,4,16,512]{4,3,1,0,2:T(8,128)S(1)}) fusion(f32[4,4,16,512]{3,2,0,1:T(8,128)} %collective-permute-done.19, f32[4,4,16,512]{3,2,0,1:T(8,128)S(1)} %pad_maximum_fusion.3, pred[]{:T(512)S(6)} %ne.35), kind=kLoop, calls=%fused_computation.38 | loop fusion | flops 262144 | bytes 2097153 | tf_op jit(solution)/shard_map/stack | solution.py:135
  65.8 1.0 %fusion.48 = f32[512,512]{1,0:T(8,128)S(1)} fusion(f32[512,512]{1,0:T(8,128)S(1)} %bitcast.152), kind=kOutput, calls=%fused_computation.115 | convolution fusion | flops 805306368 | bytes 2097152 | tf_op jit(solution)/shard_map/dot_general | solution.py:11
  66.8 1.0 %fusion.49 = f32[512,512]{1,0:T(8,128)S(1)} fusion(f32[512,512]{1,0:T(8,128)S(1)} %fusion.48), kind=kOutput, calls=%fused_computation.116 | convolution fusion | flops 805306368 | bytes 2097152 | tf_op jit(solution)/shard_map/dot_general | solution.py:11
  67.8 1.0 %fusion.50 = f32[512,512]{1,0:T(8,128)S(1)} fusion(f32[512,512]{1,0:T(8,128)S(1)} %fusion.49), kind=kOutput, calls=%fused_computation.117 | convolution fusion | flops 805306368 | bytes 2097152 | tf_op jit(solution)/shard_map/dot_general | solution.py:11
  71.0 0.6 fusion.26
  (62 shorter events, 7.2 us)
Async XLA Ops:
  0.6 7.9 %copy-start = (f32[128,512]{1,0:T(8,128)S(1)}, f32[128,512]{1,0:T(8,128)}, u32[]{:S(2)}) copy-start(f32[128,512]{1,0:T(8,128)} %param.9) | copy-start | bytes 786436
  0.6 19.5 %copy-start.1 = (f32[512,128]{1,0:T(8,128)S(1)}, f32[512,128]{1,0:T(8,128)}, u32[]{:S(2)}) copy-start(f32[512,128]{1,0:T(8,128)} %param.8) | copy-start | bytes 786436
  1.5 10.2 %collective-permute-start.2 = (f32[16,512]{1,0:T(8,128)S(1)}, f32[16,512]{1,0:T(8,128)S(1)}, u32[]{:S(2)}, u32[]{:S(2)}) collective-permute-start(f32[16,512]{1,0:T(8,128)S(1)} %constant_dynamic-slice_fusion), channel_id=1, source_target_pairs={{0,1},{1,0},{2,3},{3,2},{4,5},{5,4},{6,7},{7,6},{8,9},{9,8},{10,11... | collective-permute-start | bytes 98312 | tf_op jit(solution)/shard_map/ppermute | solution.py:42
  2.7 9.0 %collective-permute-start.1 = (f32[16,512]{1,0:T(8,128)S(1)}, f32[16,512]{1,0:T(8,128)S(1)}, u32[]{:S(2)}, u32[]{:S(2)}) collective-permute-start(f32[16,512]{1,0:T(8,128)S(1)} %constant_dynamic-slice_fusion), channel_id=1, source_target_pairs={{0,2},{1,3},{2,0},{3,1},{4,6},{5,7},{6,4},{7,5},{8,10},{9,11},{10,... | collective-permute-start | bytes 98312 | tf_op jit(solution)/shard_map/ppermute | solution.py:42
  3.9 7.7 %collective-permute-start = (f32[16,512]{1,0:T(8,128)S(1)}, f32[16,512]{1,0:T(8,128)S(1)}, u32[]{:S(2)}, u32[]{:S(2)}) collective-permute-start(f32[16,512]{1,0:T(8,128)S(1)} %constant_dynamic-slice_fusion), channel_id=1, source_target_pairs={{0,3},{1,2},{2,1},{3,0},{4,7},{5,6},{6,5},{7,4},{8,11},{9,10},{10,... | collective-permute-start | bytes 98312 | tf_op jit(solution)/shard_map/ppermute | solution.py:42
  4.1 12.8 %collective-permute-start.6 = (f32[2,128,512]{2,1,0:T(8,128)}, f32[2,128,512]{2,1,0:T(8,128)S(1)}, u32[]{:S(2)}, u32[]{:S(2)}) collective-permute-start(f32[2,128,512]{2,1,0:T(8,128)} %param.7), channel_id=1, source_target_pairs={{0,1},{1,0},{2,3},{3,2},{4,5},{5,4},{6,7},{7,6},{8,9},{9,8},{10,11... | collective-permute-start | bytes 1572872 | tf_op jit(solution)/shard_map/ppermute | solution.py:42
  5.3 12.5 %collective-permute-start.7 = (f32[2,128,512]{2,1,0:T(8,128)}, f32[2,128,512]{2,1,0:T(8,128)S(1)}, u32[]{:S(2)}, u32[]{:S(2)}) collective-permute-start(f32[2,128,512]{2,1,0:T(8,128)} %param.7), channel_id=1, source_target_pairs={{0,2},{1,3},{2,0},{3,1},{4,6},{5,7},{6,4},{7,5},{8,10},{9,11},{10,... | collective-permute-start | bytes 1572872 | tf_op jit(solution)/shard_map/ppermute | solution.py:42
  8.5 15.9 %copy-start.5 = (f32[2,128]{1,0:T(2,128)S(1)}, f32[2,128]{1,0:T(2,128)}, u32[]{:S(2)}) copy-start(f32[2,128]{1,0:T(2,128)} %param.10) | copy-start | bytes 3076
  12.5 19.9 %copy-start.3 = (f32[2,128,512]{2,1,0:T(8,128)S(1)}, f32[2,128,512]{2,1,0:T(8,128)}, u32[]{:S(2)}) copy-start(f32[2,128,512]{2,1,0:T(8,128)} %param.7) | copy-start | bytes 1572868
  18.6 6.0 %collective-permute-start.8 = (f32[1,128,512]{2,1,0:T(8,128)}, f32[1,128,512]{2,1,0:T(8,128)}, u32[]{:S(2)}, u32[]{:S(2)}) collective-permute-start(f32[1,128,512]{2,1,0:T(8,128)} %slice.60), channel_id=1, source_target_pairs={{0,1},{1,0},{2,3},{3,2},{4,5},{5,4},{6,7},{7,6},{8,9},{9,8},{10,11... | collective-permute-start | bytes 786440 | tf_op jit(solution)/shard_map/ppermute | solution.py:42
  18.9 5.7 %collective-permute-start.9 = (f32[1,128,512]{2,1,0:T(8,128)S(1)}, f32[1,128,512]{2,1,0:T(8,128)}, u32[]{:S(2)}, u32[]{:S(2)}) collective-permute-start(f32[1,128,512]{2,1,0:T(8,128)S(1)} %slice.59), channel_id=1, source_target_pairs={{0,2},{1,3},{2,0},{3,1},{4,6},{5,7},{6,4},{7,5},{8,10},{9,11},{10,... | collective-permute-start | bytes 786440 | tf_op jit(solution)/shard_map/ppermute | solution.py:42
  20.7 6.0 %collective-permute-start.5 = (f32[4,16,512]{2,1,0:T(8,128)S(1)}, f32[4,16,512]{2,1,0:T(8,128)}, u32[]{:S(2)}, u32[]{:S(2)}) collective-permute-start(f32[4,16,512]{2,1,0:T(8,128)S(1)} %pad_maximum_fusion.4), channel_id=1, source_target_pairs={{0,24},{1,25},{2,26},{3,27},{4,28},{5,29},{6,30},{7,31},{8,16},{9,... | collective-permute-start | bytes 393224 | tf_op jit(solution)/shard_map/ppermute | solution.py:42
  20.8 11.5 %collective-permute-start.4 = (f32[4,16,512]{2,1,0:T(8,128)S(1)}, f32[4,16,512]{2,1,0:T(8,128)}, u32[]{:S(2)}, u32[]{:S(2)}) collective-permute-start(f32[4,16,512]{2,1,0:T(8,128)S(1)} %pad_maximum_fusion.4), channel_id=1, source_target_pairs={{0,16},{1,17},{2,18},{3,19},{4,20},{5,21},{6,22},{7,23},{8,24},{9,... | collective-permute-start | bytes 393224 | tf_op jit(solution)/shard_map/ppermute | solution.py:42
  22.1 10.2 %collective-permute-start.3 = (f32[4,16,512]{2,1,0:T(8,128)S(1)}, f32[4,16,512]{2,1,0:T(8,128)}, u32[]{:S(2)}, u32[]{:S(2)}) collective-permute-start(f32[4,16,512]{2,1,0:T(8,128)S(1)} %pad_maximum_fusion.4), channel_id=1, source_target_pairs={{0,8},{1,9},{2,10},{3,11},{4,12},{5,13},{6,14},{7,15},{8,0},{9,1},... | collective-permute-start | bytes 393224 | tf_op jit(solution)/shard_map/ppermute | solution.py:42
  33.9 1.2 %copy-start.2 = (f32[512,512]{1,0:T(8,128)S(1)}, f32[512,512]{1,0:T(8,128)}, u32[]{:S(2)}) copy-start(f32[512,512]{1,0:T(8,128)} %convert_add_fusion.1) | copy-start | bytes 3145732
  36.2 5.1 %collective-permute-start.10 = (f32[512,512]{1,0:T(8,128)S(1)}, f32[512,512]{1,0:T(8,128)S(1)}, u32[]{:S(2)}, u32[]{:S(2)}) collective-permute-start(f32[512,512]{1,0:T(8,128)S(1)} %fusion.47), channel_id=1, source_target_pairs={{0,4},{1,5},{2,6},{3,7},{4,0},{5,1},{6,2},{7,3},{8,12},{9,13},{10,... | collective-permute-start | bytes 3145736 | tf_op jit(solution)/shard_map/ppermute | solution.py:42
  40.0 1.3 %collective-permute-start.11 = (f32[1,512]{1,0:T(1,128)S(1)}, f32[1,512]{1,0:T(1,128)S(1)}, u32[]{:S(2)}, u32[]{:S(2)}) collective-permute-start(f32[1,512]{1,0:T(1,128)S(1)} %slice_add_fusion), channel_id=1, source_target_pairs={{0,4},{1,5},{2,6},{3,7},{4,0},{5,1},{6,2},{7,3},{8,12},{9,13},{10,... | collective-permute-start | bytes 6152 | tf_op jit(solution)/shard_map/ppermute | solution.py:42
  41.8 1.6 %copy-start.4 = (f32[512]{0:T(512)S(1)}, f32[512]{0:T(512)}, u32[]{:S(2)}) copy-start(f32[512]{0:T(512)} %param.12) | copy-start | bytes 6148
  44.0 1.7 %collective-permute-start.12 = (f32[1,512]{1,0:T(1,128)S(1)}, f32[1,512]{1,0:T(1,128)S(1)}, u32[]{:S(2)}, u32[]{:S(2)}) collective-permute-start(f32[1,512]{1,0:T(1,128)S(1)} %convolution_add_fusion.13), channel_id=1, source_target_pairs={{0,8},{1,9},{2,10},{3,11},{4,12},{5,13},{6,14},{7,15}} | collective-permute-start | bytes 6152 | tf_op jit(solution)/shard_map/ppermute | solution.py:42
  46.2 1.7 %collective-permute-start.13 = (f32[1,512]{1,0:T(1,128)S(1)}, f32[1,512]{1,0:T(1,128)S(1)}, u32[]{:S(2)}, u32[]{:S(2)}) collective-permute-start(f32[1,512]{1,0:T(1,128)S(1)} %convolution_add_fusion.10), channel_id=1, source_target_pairs={{8,16},{9,17},{10,18},{11,19},{12,20},{13,21},{14,22},{15,23}} | collective-permute-start | bytes 6152 | tf_op jit(solution)/shard_map/ppermute | solution.py:42
  48.4 5.2 %collective-permute-start.14 = (f32[1,512]{1,0:T(1,128)S(1)}, f32[1,512]{1,0:T(1,128)S(1)}, u32[]{:S(2)}, u32[]{:S(2)}) collective-permute-start(f32[1,512]{1,0:T(1,128)S(1)} %convolution_add_fusion.9), channel_id=1, source_target_pairs={{16,24},{17,25},{18,26},{19,27},{20,28},{21,29},{22,30},{23,31}} | collective-permute-start | bytes 6152 | tf_op jit(solution)/shard_map/ppermute | solution.py:42
  55.0 4.1 %collective-permute-start.15 = (f32[2,512]{1,0:T(2,128)S(1)}, f32[2,512]{1,0:T(2,128)S(1)}, u32[]{:S(2)}, u32[]{:S(2)}) collective-permute-start(f32[2,512]{1,0:T(2,128)S(1)} %pad_maximum_fusion.7), channel_id=1, source_target_pairs={{0,4},{1,5},{2,6},{3,7},{4,0},{5,1},{6,2},{7,3},{8,12},{9,13},{10,... | collective-permute-start | bytes 12296 | tf_op jit(solution)/shard_map/ppermute | solution.py:42
  59.2 5.3 %collective-permute-start.19 = (f32[4,4,16,512]{3,2,0,1:T(8,128)S(1)}, f32[4,4,16,512]{3,2,0,1:T(8,128)}, u32[]{:S(2)}, u32[]{:S(2)}) collective-permute-start(f32[4,4,16,512]{3,2,0,1:T(8,128)S(1)} %pad_maximum_fusion.3), channel_id=1, source_target_pairs={{0,4},{1,5},{2,6},{3,7},{4,0},{5,1},{6,2},{7,3},{8,12},{9,13},{10,... | collective-permute-start | bytes 1572872 | tf_op jit(solution)/shard_map/ppermute | solution.py:42
  59.6 9.2 %collective-permute-start.18 = (f32[4,512]{1,0:T(4,128)S(1)}, f32[4,512]{1,0:T(4,128)S(1)}, u32[]{:S(2)}, u32[]{:S(2)}) collective-permute-start(f32[4,512]{1,0:T(4,128)S(1)} %pad_maximum_fusion.6), channel_id=1, source_target_pairs={{24,0},{25,1},{26,2},{27,3},{28,4},{29,5},{30,6},{31,7}} | collective-permute-start | bytes 24584 | tf_op jit(solution)/shard_map/ppermute | solution.py:42
  60.9 8.0 %collective-permute-start.17 = (f32[4,512]{1,0:T(4,128)S(1)}, f32[4,512]{1,0:T(4,128)S(1)}, u32[]{:S(2)}, u32[]{:S(2)}) collective-permute-start(f32[4,512]{1,0:T(4,128)S(1)} %pad_maximum_fusion.6), channel_id=1, source_target_pairs={{16,0},{17,1},{18,2},{19,3},{20,4},{21,5},{22,6},{23,7},{24,8},{25... | collective-permute-start | bytes 24584 | tf_op jit(solution)/shard_map/ppermute | solution.py:42
  62.2 6.7 %collective-permute-start.16 = (f32[4,512]{1,0:T(4,128)S(1)}, f32[4,512]{1,0:T(4,128)S(1)}, u32[]{:S(2)}, u32[]{:S(2)}) collective-permute-start(f32[4,512]{1,0:T(4,128)S(1)} %pad_maximum_fusion.6), channel_id=1, source_target_pairs={{8,0},{9,1},{10,2},{11,3},{12,4},{13,5},{14,6},{15,7},{16,8},{17,9... | collective-permute-start | bytes 24584 | tf_op jit(solution)/shard_map/ppermute | solution.py:42

commit v3 on v2

v3 whole, which is shorter than its diff:
```python
import jax
import jax.numpy as jnp
from jax import lax
from jax.sharding import PartitionSpec as P

AXES = ("slab", "row")
HIGH = lax.Precision.HIGH


def mm(a, b):
    return jnp.dot(a, b, precision=HIGH)


def by(matrix, rows):
    return lax.dot_general(rows, matrix, (((1,), (1,)), ((), ())), precision=HIGH)


def in_order(pieces, place):
    bit = 1
    while bit < len(pieces):
        crossed = (place & bit) != 0
        pieces = [jnp.where(crossed, pieces[i ^ bit], pieces[i]) for i in range(len(pieces))]
        bit *= 2
    return pieces


def after(value, *others):
    return lax.optimization_barrier((value, others))[0]


def solution(mesh):
    slabs, parts = mesh.shape["slab"], mesh.shape["row"]
    planes = slabs // 2
    every = [(s, r) for s in range(slabs) for r in range(parts)]

    def send(a, target, which=lambda s: True):
        perm = []
        for s, r in every:
            s_to, r_to = target(s, r)
            if which(s) and 0 <= s_to < slabs:
                perm.append((s * parts + r, s_to * parts + r_to))
        return lax.ppermute(a, AXES, perm)

    def other_core(a):
        return send(a, lambda s, r: (s ^ 1, r))

    def along(a, bit):
        return send(a, lambda s, r: (s, r ^ bit))

    def on_device(propagator_matrices, gain, obs_matrix, observations, present, initial, smoother_gain):
        epochs, part_rows, width = propagator_matrices.shape
        place, part = lax.axis_index("slab"), lax.axis_index("row")
        plane, odd = place // 2, place % 2 == 1

        weights = present.astype(jnp.float32)
        drive = weights[:, None] * by(gain, observations)
        taken = [-weights[e] * gain for e in range(epochs)]
        unit = jnp.eye(width, dtype=jnp.float32)
        update = [unit + mm(taken[e], obs_matrix) for e in range(epochs)]

        share = part_rows // 4
        own_share = lax.dynamic_slice_in_dim(smoother_gain, place % 4 * share, share, 0)
        own_share = after(own_share, update)

        if parts == 4:
            from_x, from_y = along(propagator_matrices, 1), along(propagator_matrices, 2)
            shares = [own_share] + [along(own_share, bit) for bit in (1, 2, 3)]
            shares = jnp.stack(in_order(shares, part), 0)
            mid = epochs // 2
            next_x, next_y = after((from_x[mid:], from_y[:mid]), shares)
            far = lax.concatenate([along(next_y, 1), along(next_x, 2)], 0)
            pieces = [propagator_matrices, from_x, from_y, far]
            full = lax.concatenate(in_order(pieces, part), 1)
        else:
            full = lax.all_gather(propagator_matrices, "row", axis=1, tiled=True)
            shares = lax.all_gather(own_share, "row", axis=0)
        next_shares = send(shares, lambda s, r: (s ^ 2, r))

        reach, maps = [], []
        for e in range(epochs):
            reach.append(mm(full[e], maps[-1]) if e else full[e])
            maps.append(mm(update[e], reach[e]))
        slab_map, shares, next_shares = lax.optimization_barrier((maps[-1], shares, next_shares))
        maps[-1] = slab_map
        else_map = other_core(slab_map)
        mine = jnp.stack(in_order([shares, next_shares], plane % 2), 0)
        theirs = other_core(mine)

        offsets, reach_0 = [drive[0:1]], [None]
        for e in range(1, epochs):
            reach_0.append(by(full[e], offsets[-1]))
            offsets.append(by(update[e], reach_0[e]) + drive[e : e + 1])
        slab_offset = offsets[-1]

        else_offset = other_core(slab_offset)
        plane_map = mm(jnp.where(odd, slab_map, else_map), jnp.where(odd, else_map, slab_map))
        plane_offset = jnp.where(
            odd, by(slab_map, else_offset) + slab_offset, by(else_map, slab_offset) + else_offset
        )

        powers, seen, seen_0 = [], [], []
        count = 2 * epochs * planes

        def smoother_rows(ahead):
            smoother = jnp.stack(in_order(after([mine, theirs], ahead), place % 2), 1)
            powers.append(smoother.transpose(2, 0, 1, 3, 4).reshape(width, width))
            powers.append(mm(powers[0], powers[0]))

        def smoother_powers(ahead):
            powers[-1] = after(powers[-1], ahead)
            while 2 ** len(powers) < count:
                powers.append(mm(powers[-1], powers[-1]))

        def observed_maps(ahead):
            for e, a in enumerate(after(reach, ahead)):
                seen.append(mm(obs_matrix, a))
                seen_0.append(by(obs_matrix, reach_0[e]) if e else jnp.zeros((1, obs_matrix.shape[0])))

        works = [smoother_rows, smoother_powers, observed_maps]
        state = initial[None, :]
        for k in range(planes - 1):
            ahead = by(plane_map, state) + plane_offset
            received = send(ahead, lambda s, r: (s + 2, r), lambda s: s // 2 == k)
            if works:
                works.pop(0)(ahead)
                received, powers, seen, seen_0 = lax.optimization_barrier(
                    (received, powers, seen, seen_0)
                )
            state = jnp.where(plane == k + 1, received, state)
        for work in works:
            work(state)

        state = jnp.where(odd, by(else_map, state) + else_offset, state)
        correction = lax.concatenate(
            [
                by(taken[e], by(seen[e], state) + seen_0[e]) + drive[e : e + 1]
                for e in range(epochs)
            ],
            0,
        )
        other = other_core(correction)
        own = lax.concatenate(
            [jnp.where(odd, other, correction), jnp.where(odd, correction, other)], 0
        )
        terms = [own]
        for k in range(1, planes):
            terms.append(send(own, lambda s, r: (s - 2 * k, r)))

        state = after(state, own)
        filtered = lax.concatenate([by(maps[e], state) + offsets[e] for e in range(epochs)], 0)

        carried = lax.concatenate(terms, 0)
        for i, power in enumerate(powers):
            later = jnp.pad(carried[2**i :], ((0, 2**i), (0, 0)))
            carried = carried + by(power, later)
        carried = jnp.where(odd, carried[epochs : 2 * epochs], carried[:epochs])
        return (filtered, filtered + carried - correction)

    placed = (P("slab", "row", None), P(), P(), P("slab", None), P("slab"), P(), P("row", None))
    return jax.shard_map(
        on_device,
        mesh=mesh,
        in_specs=placed,
        out_specs=(P("slab", None), P("slab", None)),
        check_vma=False,
    )
```

time: 72.1 us -> 68.3 us (0.947)
  the two profiles are of different devices: /device:TPU:25 before, /device:TPU:0 now
where the time goes in v3:
time: 68.3 us; the launch traced here: 67.8 us
  matrix products  21.9 us (32%)
  starting transfers between devices  21.3 us (31%)
  waiting for transfers between devices  13.9 us (20%)
  local copies, waits for them, and re-layouts  5.12 us (7%)
  other arithmetic  3.33 us (5%)
  between operations  2.32 us (3%)
    ppermute x18, starting transfers between devices, send(): return lax.ppermute(a, AXES, perm)  21.3 us
    ppermute x18, waiting for transfers between devices, send(): return lax.ppermute(a, AXES, perm)  13.9 us
    dot_general x11, matrix products, mm(): return jnp.dot(a, b, precision=HIGH)  13.3 us
    dot_general x20, matrix products, by(): lax.dot_general(rows, matrix, (((1,), (1,)), ((), ())), precision=HIGH)  8.6 us
    slice x2, local copies, waits for them, and re-layouts, on_device(): next_x, next_y = after((from_x[mid:], from_y[:mid]), shares)  2.43 us
    select_n x1, other arithmetic, in_order(): jnp.where(crossed, pieces[i ^ bit], pieces[i])  1.5 us
  transfers between devices with their start and end apart: 18, of which 9 were waited for; matrix products, arithmetic and copies ran while one was open for 34% of the time, Pallas kernels for 0%

profile of v3, /device:TPU:0, one launch (start us, length us, event | category | flops | bytes accessed | tf_op | source)
XLA Modules:
  0.0 67.8 jit_solution(2101341363883581631)
XLA Ops:
  0.6 3.0 %collective-permute-start = (f32[2,128,512]{2,1,0:T(8,128)}, f32[2,128,512]{2,1,0:T(8,128)S(1)}, u32[]{:S(2)}, u32[]{:S(2)}) collective-permute-start(f32[2,128,512]{2,1,0:T(8,128)} %param.7), channel_id=1, source_target_pairs={{0,1},{1,0},{2,3},{3,2},{4,5},{5,4},{6,7},{7,6},{8,9},{9,8},{10,11... | collective-permute-start | bytes 1572872 | tf_op jit(solution)/shard_map/ppermute | solution.py:42
  3.6 1.5 %collective-permute-start.1 = (f32[2,128,512]{2,1,0:T(8,128)}, f32[2,128,512]{2,1,0:T(8,128)}, u32[]{:S(2)}, u32[]{:S(2)}) collective-permute-start(f32[2,128,512]{2,1,0:T(8,128)} %param.7), channel_id=1, source_target_pairs={{0,2},{1,3},{2,0},{3,1},{4,6},{5,7},{6,4},{7,5},{8,10},{9,11},{10,... | collective-permute-start | bytes 1572872 | tf_op jit(solution)/shard_map/ppermute | solution.py:42
  5.2 0.7 convert_element_type.17
  5.8 0.6 fusion.39
  7.7 1.5 %convert_add_fusion.1 = f32[512,512]{1,0:T(8,128)S(1)} fusion(f32[128,512]{1,0:T(8,128)S(1)} %copy-done, f32[512,128]{1,0:T(8,128)} %param.8, f32[]{:T(128)} %bitcast), kind=kOutput, calls=%fused_computation.2 | convolution fusion | flops 202178560 | bytes 1572868 | tf_op jit(solution)/shard_map/dot_general | solution.py:11
  9.3 1.6 %convert_add_fusion = f32[512,512]{1,0:T(8,128)S(1)} fusion(f32[128,512]{1,0:T(8,128)S(1)} %copy-done, f32[512,128]{1,0:T(8,128)} %param.8, f32[]{:T(128)} %bitcast.1), kind=kOutput, calls=%fused_computation.1 | convolution fusion | flops 202178560 | bytes 1572868 | tf_op jit(solution)/shard_map/dot_general | solution.py:11
  10.8 0.8 %constant_dynamic-slice_fusion = f32[32,512]{1,0:T(8,128)S(1)} fusion(f32[128,512]{1,0:T(8,128)} %param.13, s32[]{:T(128)S(6)} %select_n.194), kind=kLoop, calls=%fused_computation.94 | loop fusion | bytes 131076 | tf_op jit(solution)/shard_map/dynamic_slice | solution.py:62
  11.7 0.5 collective-permute-start.4
  12.3 2.9 %collective-permute-start.2 = (f32[32,512]{1,0:T(8,128)S(1)}, f32[32,512]{1,0:T(8,128)S(1)}, u32[]{:S(2)}, u32[]{:S(2)}) collective-permute-start(f32[32,512]{1,0:T(8,128)S(1)} %constant_dynamic-slice_fusion), channel_id=1, source_target_pairs={{0,3},{1,2},{2,1},{3,0},{4,7},{5,6},{6,5},{7,4},{8,11},{9,10},{10,... | collective-permute-start | bytes 196616 | tf_op jit(solution)/shard_map/ppermute | solution.py:42
  15.2 2.7 %collective-permute-done.4 = f32[32,512]{1,0:T(8,128)S(1)} collective-permute-done((f32[32,512]{1,0:T(8,128)S(1)}, f32[32,512]{1,0:T(8,128)S(1)}, u32[]{:S(2)}, u32[]{:S(2)}) %collective-permute-start.4) | collective-permute-done | bytes 65568 | tf_op jit(solution)/shard_map/ppermute | solution.py:42
  17.9 2.2 %collective-permute-done.3 = f32[32,512]{1,0:T(8,128)S(1)} collective-permute-done((f32[32,512]{1,0:T(8,128)S(1)}, f32[32,512]{1,0:T(8,128)S(1)}, u32[]{:S(2)}, u32[]{:S(2)}) %collective-permute-start.3) | collective-permute-done | bytes 65568 | tf_op jit(solution)/shard_map/ppermute | solution.py:42
  20.1 0.7 %slice.59 = f32[1,128,512]{2,1,0:T(8,128)} slice(f32[2,128,512]{2,1,0:T(8,128)S(1)} %collective-permute-done), slice={[1:2], [0:128], [0:512]} | slice | bytes 524288 | tf_op jit(solution)/shard_map/slice | solution.py:70
  20.9 1.7 %slice.60 = f32[1,128,512]{2,1,0:T(8,128)} slice(f32[2,128,512]{2,1,0:T(8,128)} %collective-permute-done.1), slice={[0:1], [0:128], [0:512]} | slice | bytes 524288 | tf_op jit(solution)/shard_map/slice | solution.py:70
  22.6 1.2 %collective-permute-start.5 = (f32[1,128,512]{2,1,0:T(8,128)}, f32[1,128,512]{2,1,0:T(8,128)}, u32[]{:S(2)}, u32[]{:S(2)}) collective-permute-start(f32[1,128,512]{2,1,0:T(8,128)} %slice.60), channel_id=1, source_target_pairs={{0,1},{1,0},{2,3},{3,2},{4,5},{5,4},{6,7},{7,6},{8,9},{9,8},{10,11... | collective-permute-start | bytes 786440 | tf_op jit(solution)/shard_map/ppermute | solution.py:42
  23.8 0.8 %collective-permute-start.6 = (f32[1,128,512]{2,1,0:T(8,128)}, f32[1,128,512]{2,1,0:T(8,128)S(1)}, u32[]{:S(2)}, u32[]{:S(2)}) collective-permute-start(f32[1,128,512]{2,1,0:T(8,128)} %slice.59), channel_id=1, source_target_pairs={{0,2},{1,3},{2,0},{3,1},{4,6},{5,7},{6,4},{7,5},{8,10},{9,11},{10,... | collective-permute-start | bytes 786440 | tf_op jit(solution)/shard_map/ppermute | solution.py:42
  24.8 1.6 %collective-permute-start.7 = (f32[4,32,512]{2,1,0:T(8,128)S(1)}, f32[4,32,512]{2,1,0:T(8,128)S(1)}, u32[]{:S(2)}, u32[]{:S(2)}) collective-permute-start(f32[4,32,512]{2,1,0:T(8,128)S(1)} %pad_maximum_fusion.3), channel_id=1, source_target_pairs={{0,8},{1,9},{2,10},{3,11},{4,12},{5,13},{6,14},{7,15},{8,0},{9,1},... | collective-permute-start | bytes 786440 | tf_op jit(solution)/shard_map/ppermute | solution.py:42
  26.4 3.1 %collective-permute-done.5 = f32[1,128,512]{2,1,0:T(8,128)} collective-permute-done((f32[1,128,512]{2,1,0:T(8,128)}, f32[1,128,512]{2,1,0:T(8,128)}, u32[]{:S(2)}, u32[]{:S(2)}) %collective-permute-start.5) | collective-permute-done | bytes 262176 | tf_op jit(solution)/shard_map/ppermute | solution.py:42
  29.5 1.0 %constant_dynamic-update-slice_fusion.1 = f32[2,128,512]{2,1,0:T(8,128)S(1)} fusion(f32[1,128,512]{2,1,0:T(8,128)} %collective-permute-done.5), kind=kLoop, calls=%fused_computation.73 | loop fusion | bytes 524288
  30.6 1.5 %broadcast_select_fusion.7 = (f32[2,128,512]{2,1,0:T(8,128)S(1)}, f32[2,128,512]{2,1,0:T(8,128)S(1)}, f32[2,128,512]{2,1,0:T(8,128)S(1)}, f32[2,128,512]{2,1,0:T(8,128)S(1)}) fusion(pred[]{:T(512)S(6)} %ne.38, f32[2,128,512]{2,1,0:T(8,128)S(1)} %constant_dynamic-update-slice_fusion, f32[2,128,512]{2,1,0:T(8,128)} %collective-permute-done.1, pred[]{:T(512)S(6)} %ne.39, ...), kind=kLoop, calls=%fused_computation.50 | loop fusion | flops 1048576 | bytes 4194306 | tf_op jit(solution)/shard_map/jit(_where)/select_n | solution.py:22
  32.3 1.0 %fusion.38 = f32[512,512]{1,0:T(8,128)S(1)} fusion(f32[512,512]{1,0:T(8,128)S(1)} %convert_add_fusion, f32[2,512,512]{2,1,0:T(8,128)S(1)} %pad_maximum_fusion), kind=kOutput, calls=%fused_computation.100 | convolution fusion | flops 805306368 | bytes 3145728 | tf_op jit(solution)/shard_map/dot_general | solution.py:11
  33.4 1.0 %fusion.7 = f32[512,512]{1,0:T(8,128)S(1)} fusion(f32[512,512]{1,0:T(8,128)S(1)} %fusion.38, f32[2,512,512]{2,1,0:T(8,128)S(1)} %pad_maximum_fusion), kind=kOutput, calls=%fused_computation.35 | convolution fusion | flops 805306368 | bytes 3145728 | tf_op jit(solution)/shard_map/dot_general | solution.py:11
  34.4 1.0 %fusion.40 = f32[512,512]{1,0:T(8,128)S(1)} fusion(f32[512,512]{1,0:T(8,128)S(1)} %convert_add_fusion.1, f32[512,512]{1,0:T(8,128)S(1)} %fusion.7), kind=kOutput, calls=%fused_computation.102 | convolution fusion | flops 805306368 | bytes 3145728 | tf_op jit(solution)/shard_map/dot_general | solution.py:11
  37.5 1.2 %collective-permute-done.8 = f32[512,512]{1,0:T(8,128)S(1)} collective-permute-done((f32[512,512]{1,0:T(8,128)S(1)}, f32[512,512]{1,0:T(8,128)S(1)}, u32[]{:S(2)}, u32[]{:S(2)}) %collective-permute-start.8) | collective-permute-done | bytes 1048608 | tf_op jit(solution)/shard_map/ppermute | solution.py:42
  38.7 1.0 %fusion.4 = f32[512,512]{1,0:T(8,128)S(1)} fusion(f32[512,512]{1,0:T(8,128)S(1)} %collective-permute-done.8, f32[512,512]{1,0:T(8,128)S(1)} %fusion.40, pred[]{:T(512)S(6)} %eq.22), kind=kOutput, calls=%fused_computation.31 | convolution fusion | flops 805830656 | bytes 3145729 | tf_op jit(solution)/shard_map/dot_general | solution.py:11
  39.8 0.5 convolution_add_fusion.11
  40.3 0.6 fusion.1
  40.8 0.5 convolution_add_fusion.14
  41.4 3.5 %collective-permute-start.10 = (f32[1,512]{1,0:T(1,128)S(1)}, f32[1,512]{1,0:T(1,128)S(1)}, u32[]{:S(2)}, u32[]{:S(2)}) collective-permute-start(f32[1,512]{1,0:T(1,128)S(1)} %convolution_add_fusion.14), channel_id=1, source_target_pairs={{0,8},{1,9},{2,10},{3,11},{4,12},{5,13},{6,14},{7,15}} | collective-permute-start | bytes 6152 | tf_op jit(solution)/shard_map/ppermute | solution.py:42
  45.1 1.0 %fusion.41 = f32[512,512]{1,0:T(8,128)S(1)} fusion(f32[512,512]{1,0:T(8,128)S(1)} %bitcast.139), kind=kOutput, calls=%fused_computation.103 | convolution fusion | flops 805306368 | bytes 2097152 | tf_op jit(solution)/shard_map/dot_general | solution.py:11
  46.2 0.5 convolution_add_fusion.10
  46.7 0.8 %collective-permute-start.12 = (f32[1,512]{1,0:T(1,128)S(1)}, f32[1,512]{1,0:T(1,128)S(1)}, u32[]{:S(2)}, u32[]{:S(2)}) collective-permute-start(f32[1,512]{1,0:T(1,128)S(1)} %convolution_add_fusion.10), channel_id=1, source_target_pairs={{8,16},{9,17},{10,18},{11,19},{12,20},{13,21},{14,22},{15,23}} | collective-permute-start | bytes 6152 | tf_op jit(solution)/shard_map/ppermute | solution.py:42
  47.6 1.0 %fusion.42 = f32[512,512]{1,0:T(8,128)S(1)} fusion(f32[512,512]{1,0:T(8,128)S(1)} %fusion.41), kind=kOutput, calls=%fused_computation.104 | convolution fusion | flops 805306368 | bytes 2097152 | tf_op jit(solution)/shard_map/dot_general | solution.py:11
  48.6 2.0 %fusion.43 = f32[512,512]{1,0:T(8,128)} fusion(f32[512,512]{1,0:T(8,128)S(1)} %fusion.42), kind=kOutput, calls=%fused_computation.105 | convolution fusion | flops 805306368 | bytes 2097152 | tf_op jit(solution)/shard_map/dot_general | solution.py:11
  50.6 0.5 convolution_add_fusion.9
  51.1 0.8 %collective-permute-start.13 = (f32[1,512]{1,0:T(1,128)S(1)}, f32[1,512]{1,0:T(1,128)S(1)}, u32[]{:S(2)}, u32[]{:S(2)}) collective-permute-start(f32[1,512]{1,0:T(1,128)S(1)} %convolution_add_fusion.9), channel_id=1, source_target_pairs={{16,24},{17,25},{18,26},{19,27},{20,28},{21,29},{22,30},{23,31}} | collective-permute-start | bytes 6152 | tf_op jit(solution)/shard_map/ppermute | solution.py:42
  51.9 1.0 %convolution_bitcast_fusion.1 = f32[128,512]{0,1:T(8,128)S(1)} fusion(f32[512,512]{1,0:T(8,128)S(1)} %slice_bitcast_fusion, f32[128,512]{1,0:T(8,128)S(1)} %copy-done), kind=kOutput, calls=%fused_computation.4 | convolution fusion | flops 201326592 | bytes 1572864 | tf_op jit(solution)/shard_map/dot_general | solution.py:11
  52.9 1.0 %convolution_bitcast_fusion = f32[128,512]{0,1:T(8,128)S(1)} fusion(f32[512,512]{1,0:T(8,128)S(1)} %fusion.7, f32[128,512]{1,0:T(8,128)S(1)} %copy-done), kind=kOutput, calls=%fused_computation.3 | convolution fusion | flops 201326592 | bytes 1572864 | tf_op jit(solution)/shard_map/dot_general | solution.py:11
  53.9 0.5 fusion
  55.4 1.2 %collective-permute-done.14 = f32[2,512]{1,0:T(2,128)S(1)} collective-permute-done((f32[2,512]{1,0:T(2,128)S(1)}, f32[2,512]{1,0:T(2,128)S(1)}, u32[]{:S(2)}, u32[]{:S(2)}) %collective-permute-start.14) | collective-permute-done | bytes 4128 | tf_op jit(solution)/shard_map/ppermute | solution.py:42
  56.6 1.3 %collective-permute-start.17 = (f32[4,512]{1,0:T(4,128)S(1)}, f32[4,512]{1,0:T(4,128)S(1)}, u32[]{:S(2)}, u32[]{:S(2)}) collective-permute-start(f32[4,512]{1,0:T(4,128)S(1)} %pad_maximum_fusion.4), channel_id=1, source_target_pairs={{24,0},{25,1},{26,2},{27,3},{28,4},{29,5},{30,6},{31,7}} | collective-permute-start | bytes 24584 | tf_op jit(solution)/shard_map/ppermute | solution.py:42
  57.9 1.3 %collective-permute-start.16 = (f32[4,512]{1,0:T(4,128)S(1)}, f32[4,512]{1,0:T(4,128)S(1)}, u32[]{:S(2)}, u32[]{:S(2)}) collective-permute-start(f32[4,512]{1,0:T(4,128)S(1)} %pad_maximum_fusion.4), channel_id=1, source_target_pairs={{16,0},{17,1},{18,2},{19,3},{20,4},{21,5},{22,6},{23,7},{24,8},{25... | collective-permute-start | bytes 24584 | tf_op jit(solution)/shard_map/ppermute | solution.py:42
  59.2 1.3 %collective-permute-start.15 = (f32[4,512]{1,0:T(4,128)S(1)}, f32[4,512]{1,0:T(4,128)S(1)}, u32[]{:S(2)}, u32[]{:S(2)}) collective-permute-start(f32[4,512]{1,0:T(4,128)S(1)} %pad_maximum_fusion.4), channel_id=1, source_target_pairs={{8,0},{9,1},{10,2},{11,3},{12,4},{13,5},{14,6},{15,7},{16,8},{17,9... | collective-permute-start | bytes 24584 | tf_op jit(solution)/shard_map/ppermute | solution.py:42
  60.5 0.5 convolution_add_fusion.5
  61.0 0.6 convolution_add_fusion.4
  61.5 2.4 %collective-permute-done.17 = f32[4,512]{1,0:T(4,128)S(1)} collective-permute-done((f32[4,512]{1,0:T(4,128)S(1)}, f32[4,512]{1,0:T(4,128)S(1)}, u32[]{:S(2)}, u32[]{:S(2)}) %collective-permute-start.17) | collective-permute-done | bytes 8224 | tf_op jit(solution)/shard_map/ppermute | solution.py:42
  64.3 0.7 collective-permute-done.15
  66.7 0.5 convolution_add_fusion
  67.2 0.6 fusion.22
  (58 shorter events, 5.9 us)
Async XLA Ops:
  0.6 7.1 %copy-start = (f32[128,512]{1,0:T(8,128)S(1)}, f32[128,512]{1,0:T(8,128)}, u32[]{:S(2)}) copy-start(f32[128,512]{1,0:T(8,128)} %param.9) | copy-start | bytes 786436
  0.6 19.5 %collective-permute-start = (f32[2,128,512]{2,1,0:T(8,128)}, f32[2,128,512]{2,1,0:T(8,128)S(1)}, u32[]{:S(2)}, u32[]{:S(2)}) collective-permute-start(f32[2,128,512]{2,1,0:T(8,128)} %param.7), channel_id=1, source_target_pairs={{0,1},{1,0},{2,3},{3,2},{4,5},{5,4},{6,7},{7,6},{8,9},{9,8},{10,11... | collective-permute-start | bytes 1572872 | tf_op jit(solution)/shard_map/ppermute | solution.py:42
  3.6 17.2 %collective-permute-start.1 = (f32[2,128,512]{2,1,0:T(8,128)}, f32[2,128,512]{2,1,0:T(8,128)}, u32[]{:S(2)}, u32[]{:S(2)}) collective-permute-start(f32[2,128,512]{2,1,0:T(8,128)} %param.7), channel_id=1, source_target_pairs={{0,2},{1,3},{2,0},{3,1},{4,6},{5,7},{6,4},{7,5},{8,10},{9,11},{10,... | collective-permute-start | bytes 1572872 | tf_op jit(solution)/shard_map/ppermute | solution.py:42
  9.2 15.4 %copy-start.1 = (f32[512,128]{1,0:T(8,128)S(1)}, f32[512,128]{1,0:T(8,128)}, u32[]{:S(2)}) copy-start(f32[512,128]{1,0:T(8,128)} %param.8) | copy-start | bytes 786436
  9.3 15.4 %copy-start.5 = (f32[2,128]{1,0:T(2,128)S(1)}, f32[2,128]{1,0:T(2,128)}, u32[]{:S(2)}) copy-start(f32[2,128]{1,0:T(2,128)} %param.10) | copy-start | bytes 3076
  11.7 6.2 %collective-permute-start.4 = (f32[32,512]{1,0:T(8,128)S(1)}, f32[32,512]{1,0:T(8,128)S(1)}, u32[]{:S(2)}, u32[]{:S(2)}) collective-permute-start(f32[32,512]{1,0:T(8,128)S(1)} %constant_dynamic-slice_fusion), channel_id=1, source_target_pairs={{0,1},{1,0},{2,3},{3,2},{4,5},{5,4},{6,7},{7,6},{8,9},{9,8},{10,11... | collective-permute-start | bytes 196616 | tf_op jit(solution)/shard_map/ppermute | solution.py:42
  12.2 7.8 %collective-permute-start.3 = (f32[32,512]{1,0:T(8,128)S(1)}, f32[32,512]{1,0:T(8,128)S(1)}, u32[]{:S(2)}, u32[]{:S(2)}) collective-permute-start(f32[32,512]{1,0:T(8,128)S(1)} %constant_dynamic-slice_fusion), channel_id=1, source_target_pairs={{0,2},{1,3},{2,0},{3,1},{4,6},{5,7},{6,4},{7,5},{8,10},{9,11},{10,... | collective-permute-start | bytes 196616 | tf_op jit(solution)/shard_map/ppermute | solution.py:42
  12.3 7.8 %collective-permute-start.2 = (f32[32,512]{1,0:T(8,128)S(1)}, f32[32,512]{1,0:T(8,128)S(1)}, u32[]{:S(2)}, u32[]{:S(2)}) collective-permute-start(f32[32,512]{1,0:T(8,128)S(1)} %constant_dynamic-slice_fusion), channel_id=1, source_target_pairs={{0,3},{1,2},{2,1},{3,0},{4,7},{5,6},{6,5},{7,4},{8,11},{9,10},{10,... | collective-permute-start | bytes 196616 | tf_op jit(solution)/shard_map/ppermute | solution.py:42
  22.6 6.9 %collective-permute-start.5 = (f32[1,128,512]{2,1,0:T(8,128)}, f32[1,128,512]{2,1,0:T(8,128)}, u32[]{:S(2)}, u32[]{:S(2)}) collective-permute-start(f32[1,128,512]{2,1,0:T(8,128)} %slice.60), channel_id=1, source_target_pairs={{0,1},{1,0},{2,3},{3,2},{4,5},{5,4},{6,7},{7,6},{8,9},{9,8},{10,11... | collective-permute-start | bytes 786440 | tf_op jit(solution)/shard_map/ppermute | solution.py:42
  23.8 6.8 %collective-permute-start.6 = (f32[1,128,512]{2,1,0:T(8,128)}, f32[1,128,512]{2,1,0:T(8,128)S(1)}, u32[]{:S(2)}, u32[]{:S(2)}) collective-permute-start(f32[1,128,512]{2,1,0:T(8,128)} %slice.59), channel_id=1, source_target_pairs={{0,2},{1,3},{2,0},{3,1},{4,6},{5,7},{6,4},{7,5},{8,10},{9,11},{10,... | collective-permute-start | bytes 786440 | tf_op jit(solution)/shard_map/ppermute | solution.py:42
  24.8 11.2 %collective-permute-start.7 = (f32[4,32,512]{2,1,0:T(8,128)S(1)}, f32[4,32,512]{2,1,0:T(8,128)S(1)}, u32[]{:S(2)}, u32[]{:S(2)}) collective-permute-start(f32[4,32,512]{2,1,0:T(8,128)S(1)} %pad_maximum_fusion.3), channel_id=1, source_target_pairs={{0,8},{1,9},{2,10},{3,11},{4,12},{5,13},{6,14},{7,15},{8,0},{9,1},... | collective-permute-start | bytes 786440 | tf_op jit(solution)/shard_map/ppermute | solution.py:42
  36.0 2.7 %collective-permute-start.8 = (f32[512,512]{1,0:T(8,128)S(1)}, f32[512,512]{1,0:T(8,128)S(1)}, u32[]{:S(2)}, u32[]{:S(2)}) collective-permute-start(f32[512,512]{1,0:T(8,128)S(1)} %fusion.40), channel_id=1, source_target_pairs={{0,4},{1,5},{2,6},{3,7},{4,0},{5,1},{6,2},{7,3},{8,12},{9,13},{10,... | collective-permute-start | bytes 3145736 | tf_op jit(solution)/shard_map/ppermute | solution.py:42
  36.5 3.2 %collective-permute-start.9 = (f32[1,512]{1,0:T(1,128)S(1)}, f32[1,512]{1,0:T(1,128)S(1)}, u32[]{:S(2)}, u32[]{:S(2)}) collective-permute-start(f32[1,512]{1,0:T(1,128)S(1)} %convolution_add_fusion.13), channel_id=1, source_target_pairs={{0,4},{1,5},{2,6},{3,7},{4,0},{5,1},{6,2},{7,3},{8,12},{9,13},{10,... | collective-permute-start | bytes 6152 | tf_op jit(solution)/shard_map/ppermute | solution.py:42
  37.2 7.7 %collective-permute-start.11 = (f32[2,4,32,512]{3,2,0,1:T(8,128)S(1)}, f32[2,4,32,512]{3,2,0,1:T(8,128)S(1)}, u32[]{:S(2)}, u32[]{:S(2)}) collective-permute-start(f32[2,4,32,512]{3,2,0,1:T(8,128)S(1)} %pad_maximum_fusion.2), channel_id=1, source_target_pairs={{0,4},{1,5},{2,6},{3,7},{4,0},{5,1},{6,2},{7,3},{8,12},{9,13},{10,... | collective-permute-start | bytes 1572872 | tf_op jit(solution)/shard_map/ppermute | solution.py:42
  39.7 1.1 %copy-start.4 = (f32[512]{0:T(512)S(1)}, f32[512]{0:T(512)}, u32[]{:S(2)}) copy-start(f32[512]{0:T(512)} %param.12) | copy-start | bytes 6148
  41.4 4.8 %collective-permute-start.10 = (f32[1,512]{1,0:T(1,128)S(1)}, f32[1,512]{1,0:T(1,128)S(1)}, u32[]{:S(2)}, u32[]{:S(2)}) collective-permute-start(f32[1,512]{1,0:T(1,128)S(1)} %convolution_add_fusion.14), channel_id=1, source_target_pairs={{0,8},{1,9},{2,10},{3,11},{4,12},{5,13},{6,14},{7,15}} | collective-permute-start | bytes 6152 | tf_op jit(solution)/shard_map/ppermute | solution.py:42
  46.7 3.9 %collective-permute-start.12 = (f32[1,512]{1,0:T(1,128)S(1)}, f32[1,512]{1,0:T(1,128)S(1)}, u32[]{:S(2)}, u32[]{:S(2)}) collective-permute-start(f32[1,512]{1,0:T(1,128)S(1)} %convolution_add_fusion.10), channel_id=1, source_target_pairs={{8,16},{9,17},{10,18},{11,19},{12,20},{13,21},{14,22},{15,23}} | collective-permute-start | bytes 6152 | tf_op jit(solution)/shard_map/ppermute | solution.py:42
  51.1 3.6 %copy-start.2 = (f32[512,128]{1,0:T(8,128)S(1)}, f32[512,128]{1,0:T(8,128)}, u32[]{:S(2)}) copy-start(f32[512,128]{1,0:T(8,128)} %param.8) | copy-start | bytes 786436
  51.1 2.8 %collective-permute-start.13 = (f32[1,512]{1,0:T(1,128)S(1)}, f32[1,512]{1,0:T(1,128)S(1)}, u32[]{:S(2)}, u32[]{:S(2)}) collective-permute-start(f32[1,512]{1,0:T(1,128)S(1)} %convolution_add_fusion.9), channel_id=1, source_target_pairs={{16,24},{17,25},{18,26},{19,27},{20,28},{21,29},{22,30},{23,31}} | collective-permute-start | bytes 6152 | tf_op jit(solution)/shard_map/ppermute | solution.py:42
  55.3 1.2 %collective-permute-start.14 = (f32[2,512]{1,0:T(2,128)S(1)}, f32[2,512]{1,0:T(2,128)S(1)}, u32[]{:S(2)}, u32[]{:S(2)}) collective-permute-start(f32[2,512]{1,0:T(2,128)S(1)} %pad_maximum_fusion.5), channel_id=1, source_target_pairs={{0,4},{1,5},{2,6},{3,7},{4,0},{5,1},{6,2},{7,3},{8,12},{9,13},{10,... | collective-permute-start | bytes 12296 | tf_op jit(solution)/shard_map/ppermute | solution.py:42
  56.6 7.3 %collective-permute-start.17 = (f32[4,512]{1,0:T(4,128)S(1)}, f32[4,512]{1,0:T(4,128)S(1)}, u32[]{:S(2)}, u32[]{:S(2)}) collective-permute-start(f32[4,512]{1,0:T(4,128)S(1)} %pad_maximum_fusion.4), channel_id=1, source_target_pairs={{24,0},{25,1},{26,2},{27,3},{28,4},{29,5},{30,6},{31,7}} | collective-permute-start | bytes 24584 | tf_op jit(solution)/shard_map/ppermute | solution.py:42
  57.9 6.4 %collective-permute-start.16 = (f32[4,512]{1,0:T(4,128)S(1)}, f32[4,512]{1,0:T(4,128)S(1)}, u32[]{:S(2)}, u32[]{:S(2)}) collective-permute-start(f32[4,512]{1,0:T(4,128)S(1)} %pad_maximum_fusion.4), channel_id=1, source_target_pairs={{16,0},{17,1},{18,2},{19,3},{20,4},{21,5},{22,6},{23,7},{24,8},{25... | collective-permute-start | bytes 24584 | tf_op jit(solution)/shard_map/ppermute | solution.py:42
  59.2 5.8 %collective-permute-start.15 = (f32[4,512]{1,0:T(4,128)S(1)}, f32[4,512]{1,0:T(4,128)S(1)}, u32[]{:S(2)}, u32[]{:S(2)}) collective-permute-start(f32[4,512]{1,0:T(4,128)S(1)} %pad_maximum_fusion.4), channel_id=1, source_target_pairs={{8,0},{9,1},{10,2},{11,3},{12,4},{13,5},{14,6},{15,7},{16,8},{17,9... | collective-permute-start | bytes 24584 | tf_op jit(solution)/shard_map/ppermute | solution.py:42
  65.0 1.7 %copy-start.3 = (f32[512,512]{1,0:T(8,128)S(1)}, f32[512,512]{1,0:T(8,128)}, u32[]{:S(2)}) copy-start(f32[512,512]{1,0:T(8,128)} %fusion.43) | copy-start | bytes 3145732

commit v4 on v3

--- a/solution.py
+++ b/solution.py
@@ -67,8 +67,8 @@
             shares = [own_share] + [along(own_share, bit) for bit in (1, 2, 3)]
             shares = jnp.stack(in_order(shares, part), 0)
             mid = epochs // 2
-            next_x, next_y = after((from_x[mid:], from_y[:mid]), shares)
-            far = lax.concatenate([along(next_y, 1), along(next_x, 2)], 0)
+            far = lax.concatenate([along(from_y[:mid], 1), along(from_x[mid:], 2)], 0)
+            far = after(far, shares)
             pieces = [propagator_matrices, from_x, from_y, far]
             full = lax.concatenate(in_order(pieces, part), 1)
         else:

time: 68.3 us -> 63.9 us (0.936)
  waiting for transfers between devices: 13.9 us -> 10.8 us
  local copies, waits for them, and re-layouts: 5.12 us -> 2.68 us
  starting transfers between devices: 21.3 us -> 22.5 us
    ppermute x18, waiting for transfers between devices: 13.9 us -> 10.8 us  [send(): return lax.ppermute(a, AXES, perm)]
    slice x2, local copies, waits for them, and re-layouts: 2.43 us -> 0.99 us  [on_device(): far = lax.concatenate([along(from_y[:mid], 1), along(from_x[mid:], 2)], 0)]
    ppermute x18, starting transfers between devices: 21.3 us -> 22.5 us  [send(): return lax.ppermute(a, AXES, perm)]
    unnamed x13 -> x12, local copies, waits for them, and re-layouts: 1 us -> 0.03 us
  transfers between devices with their start and end apart: 18 -> 18, of which waited for: 9 -> 10; matrix products, arithmetic and copies ran while one was open for 34% -> 36% of each run, Pallas kernels for 0% -> 0%
where the time goes in v4:
time: 63.9 us; the launch traced here: 63.5 us
  starting transfers between devices  22.5 us (35%)
  matrix products  21.8 us (34%)
  waiting for transfers between devices  10.8 us (17%)
  other arithmetic  3.37 us (5%)
  local copies, waits for them, and re-layouts  2.68 us (4%)
  between operations  2.31 us (4%)
    ppermute x18, starting transfers between devices, send(): return lax.ppermute(a, AXES, perm)  22.5 us
    dot_general x11, matrix products, mm(): return jnp.dot(a, b, precision=HIGH)  13.2 us
    ppermute x18, waiting for transfers between devices, send(): return lax.ppermute(a, AXES, perm)  10.8 us
    dot_general x20, matrix products, by(): lax.dot_general(rows, matrix, (((1,), (1,)), ((), ())), precision=HIGH)  8.6 us
    select_n x1, other arithmetic, in_order(): jnp.where(crossed, pieces[i ^ bit], pieces[i])  1.5 us
  transfers between devices with their start and end apart: 18, of which 10 were waited for; matrix products, arithmetic and copies ran while one was open for 36% of the time, Pallas kernels for 0%

profile of v4, /device:TPU:0, one launch (start us, length us, event | category | flops | bytes accessed | tf_op | source)
XLA Modules:
  0.0 63.5 jit_solution(16970428852412887094)
XLA Ops:
  0.7 3.0 %collective-permute-start = (f32[2,128,512]{2,1,0:T(8,128)}, f32[2,128,512]{2,1,0:T(8,128)S(1)}, u32[]{:S(2)}, u32[]{:S(2)}) collective-permute-start(f32[2,128,512]{2,1,0:T(8,128)} %param.7), channel_id=1, source_target_pairs={{0,2},{1,3},{2,0},{3,1},{4,6},{5,7},{6,4},{7,5},{8,10},{9,11},{10,... | collective-permute-start | bytes 1572872 | tf_op jit(solution)/shard_map/ppermute | solution.py:42
  3.7 1.5 %collective-permute-start.2 = (f32[2,128,512]{2,1,0:T(8,128)}, f32[2,128,512]{2,1,0:T(8,128)}, u32[]{:S(2)}, u32[]{:S(2)}) collective-permute-start(f32[2,128,512]{2,1,0:T(8,128)} %param.7), channel_id=1, source_target_pairs={{0,1},{1,0},{2,3},{3,2},{4,5},{5,4},{6,7},{7,6},{8,9},{9,8},{10,11... | collective-permute-start | bytes 1572872 | tf_op jit(solution)/shard_map/ppermute | solution.py:42
  5.2 0.7 %convert_element_type.17 = f32[2]{0:T(128)S(1)} convert(s32[2]{0:T(128)} %param.11) | non-fusion elementwise | flops 2 | bytes 16 | tf_op jit(solution)/shard_map/convert_element_type | solution.py:55
  5.8 0.6 fusion.39
  7.1 1.5 %convert_add_fusion.1 = f32[512,512]{1,0:T(8,128)S(1)} fusion(f32[128,512]{1,0:T(8,128)S(1)} %copy-done, f32[512,128]{1,0:T(8,128)} %param.8, f32[]{:T(128)} %bitcast), kind=kOutput, calls=%fused_computation.2 | convolution fusion | flops 202178560 | bytes 1572868 | tf_op jit(solution)/shard_map/dot_general | solution.py:11
  8.6 0.9 %constant_dynamic-slice_fusion = f32[32,512]{1,0:T(8,128)S(1)} fusion(f32[128,512]{1,0:T(8,128)} %param.13, s32[]{:T(128)S(6)} %select_n.194), kind=kLoop, calls=%fused_computation.93 | loop fusion | bytes 131076 | tf_op jit(solution)/shard_map/dynamic_slice | solution.py:62
  10.1 1.5 %convert_add_fusion = f32[512,512]{1,0:T(8,128)S(1)} fusion(f32[128,512]{1,0:T(8,128)S(1)} %copy-done, f32[512,128]{1,0:T(8,128)} %param.8, f32[]{:T(128)} %bitcast.1), kind=kOutput, calls=%fused_computation.1 | convolution fusion | flops 202178560 | bytes 1572868 | tf_op jit(solution)/shard_map/dot_general | solution.py:11
  11.6 0.6 collective-permute-start.6
  12.3 2.9 %collective-permute-start.4 = (f32[32,512]{1,0:T(8,128)S(1)}, f32[32,512]{1,0:T(8,128)S(1)}, u32[]{:S(2)}, u32[]{:S(2)}) collective-permute-start(f32[32,512]{1,0:T(8,128)S(1)} %constant_dynamic-slice_fusion), channel_id=1, source_target_pairs={{0,3},{1,2},{2,1},{3,0},{4,7},{5,6},{6,5},{7,4},{8,11},{9,10},{10,... | collective-permute-start | bytes 196616 | tf_op jit(solution)/shard_map/ppermute | solution.py:42
  15.4 1.1 %collective-permute-done = f32[2,128,512]{2,1,0:T(8,128)S(1)} collective-permute-done((f32[2,128,512]{2,1,0:T(8,128)}, f32[2,128,512]{2,1,0:T(8,128)S(1)}, u32[]{:S(2)}, u32[]{:S(2)}) %collective-permute-start) | collective-permute-done | bytes 524320 | tf_op jit(solution)/shard_map/ppermute | solution.py:42
  16.6 1.8 %collective-permute-start.1 = (f32[1,128,512]{2,1,0:T(8,128)S(1)}, f32[1,128,512]{2,1,0:T(8,128)S(1)}, u32[]{:S(2)}, u32[]{:S(2)}) collective-permute-start(f32[1,128,512]{2,1,0:T(8,128)S(1)} %slice.59), channel_id=1, source_target_pairs={{0,1},{1,0},{2,3},{3,2},{4,5},{5,4},{6,7},{7,6},{8,9},{9,8},{10,11... | collective-permute-start | bytes 786440 | tf_op jit(solution)/shard_map/ppermute | solution.py:42
  18.3 0.5 collective-permute-done.2
  18.9 1.0 %slice.60 = f32[1,128,512]{2,1,0:T(8,128)S(1)} slice(f32[2,128,512]{2,1,0:T(8,128)} %collective-permute-done.2), slice={[1:2], [0:128], [0:512]} | slice | bytes 524288 | tf_op jit(solution)/shard_map/slice | solution.py:70
  19.8 1.1 %collective-permute-start.3 = (f32[1,128,512]{2,1,0:T(8,128)S(1)}, f32[1,128,512]{2,1,0:T(8,128)S(1)}, u32[]{:S(2)}, u32[]{:S(2)}) collective-permute-start(f32[1,128,512]{2,1,0:T(8,128)S(1)} %slice.60), channel_id=1, source_target_pairs={{0,2},{1,3},{2,0},{3,1},{4,6},{5,7},{6,4},{7,5},{8,10},{9,11},{10,... | collective-permute-start | bytes 786440 | tf_op jit(solution)/shard_map/ppermute | solution.py:42
  21.0 1.9 %collective-permute-start.7 = (f32[4,32,512]{2,1,0:T(8,128)S(1)}, f32[4,32,512]{2,1,0:T(8,128)S(1)}, u32[]{:S(2)}, u32[]{:S(2)}) collective-permute-start(f32[4,32,512]{2,1,0:T(8,128)S(1)} %pad_maximum_fusion.4), channel_id=1, source_target_pairs={{0,8},{1,9},{2,10},{3,11},{4,12},{5,13},{6,14},{7,15},{8,0},{9,1},... | collective-permute-start | bytes 786440 | tf_op jit(solution)/shard_map/ppermute | solution.py:42
  23.0 2.8 %collective-permute-done.1 = f32[1,128,512]{2,1,0:T(8,128)S(1)} collective-permute-done((f32[1,128,512]{2,1,0:T(8,128)S(1)}, f32[1,128,512]{2,1,0:T(8,128)S(1)}, u32[]{:S(2)}, u32[]{:S(2)}) %collective-permute-start.1) | collective-permute-done | bytes 262176 | tf_op jit(solution)/shard_map/ppermute | solution.py:42
  25.7 0.6 collective-permute-done.3
  26.3 1.5 %broadcast_select_fusion.7 = (f32[2,128,512]{2,1,0:T(8,128)S(1)}, f32[2,128,512]{2,1,0:T(8,128)S(1)}, f32[2,128,512]{2,1,0:T(8,128)S(1)}, f32[2,128,512]{2,1,0:T(8,128)S(1)}) fusion(pred[]{:T(512)S(6)} %ne.38, f32[2,128,512]{2,1,0:T(8,128)S(1)} %pad_maximum_fusion.2, f32[2,128,512]{2,1,0:T(8,128)S(1)} %collective-permute-done, pred[]{:T(512)S(6)} %ne.39, ...), kind=kLoop, calls=%fused_computation.51 | loop fusion | flops 1048576 | bytes 4194306 | tf_op jit(solution)/shard_map/jit(_where)/select_n | solution.py:22
  28.0 1.0 %fusion.38 = f32[512,512]{1,0:T(8,128)S(1)} fusion(f32[512,512]{1,0:T(8,128)S(1)} %convert_add_fusion, f32[2,512,512]{2,1,0:T(8,128)S(1)} %pad_maximum_fusion), kind=kOutput, calls=%fused_computation.99 | convolution fusion | flops 805306368 | bytes 3145728 | tf_op jit(solution)/shard_map/dot_general | solution.py:11
  29.1 1.0 %fusion.7 = f32[512,512]{1,0:T(8,128)S(1)} fusion(f32[512,512]{1,0:T(8,128)S(1)} %fusion.38, f32[2,512,512]{2,1,0:T(8,128)S(1)} %pad_maximum_fusion), kind=kOutput, calls=%fused_computation.35 | convolution fusion | flops 805306368 | bytes 3145728 | tf_op jit(solution)/shard_map/dot_general | solution.py:11
  30.1 1.0 %fusion.40 = f32[512,512]{1,0:T(8,128)S(1)} fusion(f32[512,512]{1,0:T(8,128)S(1)} %convert_add_fusion.1, f32[512,512]{1,0:T(8,128)S(1)} %fusion.7), kind=kOutput, calls=%fused_computation.101 | convolution fusion | flops 805306368 | bytes 3145728 | tf_op jit(solution)/shard_map/dot_general | solution.py:11
  31.2 0.5 convolution_bitcast_fusion.2
  33.2 1.1 %collective-permute-done.8 = f32[512,512]{1,0:T(8,128)S(1)} collective-permute-done((f32[512,512]{1,0:T(8,128)S(1)}, f32[512,512]{1,0:T(8,128)S(1)}, u32[]{:S(2)}, u32[]{:S(2)}) %collective-permute-start.8) | collective-permute-done | bytes 1048608 | tf_op jit(solution)/shard_map/ppermute | solution.py:42
  34.4 1.0 %fusion.4 = f32[512,512]{1,0:T(8,128)S(1)} fusion(f32[512,512]{1,0:T(8,128)S(1)} %collective-permute-done.8, f32[512,512]{1,0:T(8,128)S(1)} %fusion.40, pred[]{:T(512)S(6)} %eq.22), kind=kOutput, calls=%fused_computation.31 | convolution fusion | flops 805830656 | bytes 3145729 | tf_op jit(solution)/shard_map/dot_general | solution.py:11
  35.4 0.5 convolution_add_fusion.11
  36.0 0.6 fusion.1
  36.5 0.5 convolution_add_fusion.14
  37.1 3.5 %collective-permute-start.10 = (f32[1,512]{1,0:T(1,128)S(1)}, f32[1,512]{1,0:T(1,128)S(1)}, u32[]{:S(2)}, u32[]{:S(2)}) collective-permute-start(f32[1,512]{1,0:T(1,128)S(1)} %convolution_add_fusion.14), channel_id=1, source_target_pairs={{0,8},{1,9},{2,10},{3,11},{4,12},{5,13},{6,14},{7,15}} | collective-permute-start | bytes 6152 | tf_op jit(solution)/shard_map/ppermute | solution.py:42
  40.8 1.0 %fusion.41 = f32[512,512]{1,0:T(8,128)S(1)} fusion(f32[512,512]{1,0:T(8,128)S(1)} %bitcast.139), kind=kOutput, calls=%fused_computation.102 | convolution fusion | flops 805306368 | bytes 2097152 | tf_op jit(solution)/shard_map/dot_general | solution.py:11
  41.9 0.5 convolution_add_fusion.10
  42.4 0.8 %collective-permute-start.12 = (f32[1,512]{1,0:T(1,128)S(1)}, f32[1,512]{1,0:T(1,128)S(1)}, u32[]{:S(2)}, u32[]{:S(2)}) collective-permute-start(f32[1,512]{1,0:T(1,128)S(1)} %convolution_add_fusion.10), channel_id=1, source_target_pairs={{8,16},{9,17},{10,18},{11,19},{12,20},{13,21},{14,22},{15,23}} | collective-permute-start | bytes 6152 | tf_op jit(solution)/shard_map/ppermute | solution.py:42
  43.2 1.0 %fusion.42 = f32[512,512]{1,0:T(8,128)S(1)} fusion(f32[512,512]{1,0:T(8,128)S(1)} %fusion.41), kind=kOutput, calls=%fused_computation.103 | convolution fusion | flops 805306368 | bytes 2097152 | tf_op jit(solution)/shard_map/dot_general | solution.py:11
  44.3 2.0 %fusion.43 = f32[512,512]{1,0:T(8,128)} fusion(f32[512,512]{1,0:T(8,128)S(1)} %fusion.42), kind=kOutput, calls=%fused_computation.104 | convolution fusion | flops 805306368 | bytes 2097152 | tf_op jit(solution)/shard_map/dot_general | solution.py:11
  46.3 0.5 convolution_add_fusion.9
  46.8 0.8 %collective-permute-start.13 = (f32[1,512]{1,0:T(1,128)S(1)}, f32[1,512]{1,0:T(1,128)S(1)}, u32[]{:S(2)}, u32[]{:S(2)}) collective-permute-start(f32[1,512]{1,0:T(1,128)S(1)} %convolution_add_fusion.9), channel_id=1, source_target_pairs={{16,24},{17,25},{18,26},{19,27},{20,28},{21,29},{22,30},{23,31}} | collective-permute-start | bytes 6152 | tf_op jit(solution)/shard_map/ppermute | solution.py:42
  47.6 1.0 %convolution_bitcast_fusion.1 = f32[128,512]{0,1:T(8,128)S(1)} fusion(f32[512,512]{1,0:T(8,128)S(1)} %slice_bitcast_fusion, f32[128,512]{1,0:T(8,128)S(1)} %copy-done), kind=kOutput, calls=%fused_computation.4 | convolution fusion | flops 201326592 | bytes 1572864 | tf_op jit(solution)/shard_map/dot_general | solution.py:11
  48.6 1.0 %convolution_bitcast_fusion = f32[128,512]{0,1:T(8,128)S(1)} fusion(f32[512,512]{1,0:T(8,128)S(1)} %fusion.7, f32[128,512]{1,0:T(8,128)S(1)} %copy-done), kind=kOutput, calls=%fused_computation.3 | convolution fusion | flops 201326592 | bytes 1572864 | tf_op jit(solution)/shard_map/dot_general | solution.py:11
  49.6 0.5 fusion
  51.1 1.2 %collective-permute-done.14 = f32[2,512]{1,0:T(2,128)S(1)} collective-permute-done((f32[2,512]{1,0:T(2,128)S(1)}, f32[2,512]{1,0:T(2,128)S(1)}, u32[]{:S(2)}, u32[]{:S(2)}) %collective-permute-start.14) | collective-permute-done | bytes 4128 | tf_op jit(solution)/shard_map/ppermute | solution.py:42
  52.3 1.3 %collective-permute-start.17 = (f32[4,512]{1,0:T(4,128)S(1)}, f32[4,512]{1,0:T(4,128)S(1)}, u32[]{:S(2)}, u32[]{:S(2)}) collective-permute-start(f32[4,512]{1,0:T(4,128)S(1)} %pad_maximum_fusion.5), channel_id=1, source_target_pairs={{24,0},{25,1},{26,2},{27,3},{28,4},{29,5},{30,6},{31,7}} | collective-permute-start | bytes 24584 | tf_op jit(solution)/shard_map/ppermute | solution.py:42
  53.6 1.3 %collective-permute-start.16 = (f32[4,512]{1,0:T(4,128)S(1)}, f32[4,512]{1,0:T(4,128)S(1)}, u32[]{:S(2)}, u32[]{:S(2)}) collective-permute-start(f32[4,512]{1,0:T(4,128)S(1)} %pad_maximum_fusion.5), channel_id=1, source_target_pairs={{16,0},{17,1},{18,2},{19,3},{20,4},{21,5},{22,6},{23,7},{24,8},{25... | collective-permute-start | bytes 24584 | tf_op jit(solution)/shard_map/ppermute | solution.py:42
  54.9 1.3 %collective-permute-start.15 = (f32[4,512]{1,0:T(4,128)S(1)}, f32[4,512]{1,0:T(4,128)S(1)}, u32[]{:S(2)}, u32[]{:S(2)}) collective-permute-start(f32[4,512]{1,0:T(4,128)S(1)} %pad_maximum_fusion.5), channel_id=1, source_target_pairs={{8,0},{9,1},{10,2},{11,3},{12,4},{13,5},{14,6},{15,7},{16,8},{17,9... | collective-permute-start | bytes 24584 | tf_op jit(solution)/shard_map/ppermute | solution.py:42
  56.2 0.5 convolution_add_fusion.5
  56.7 0.6 convolution_add_fusion.4
  57.2 2.4 %collective-permute-done.17 = f32[4,512]{1,0:T(4,128)S(1)} collective-permute-done((f32[4,512]{1,0:T(4,128)S(1)}, f32[4,512]{1,0:T(4,128)S(1)}, u32[]{:S(2)}, u32[]{:S(2)}) %collective-permute-start.17) | collective-permute-done | bytes 8224 | tf_op jit(solution)/shard_map/ppermute | solution.py:42
  60.0 0.7 %collective-permute-done.15 = f32[4,512]{1,0:T(4,128)S(1)} collective-permute-done((f32[4,512]{1,0:T(4,128)S(1)}, f32[4,512]{1,0:T(4,128)S(1)}, u32[]{:S(2)}, u32[]{:S(2)}) %collective-permute-start.15) | collective-permute-done | bytes 8224 | tf_op jit(solution)/shard_map/ppermute | solution.py:42
  62.4 0.5 convolution_add_fusion
  62.9 0.6 fusion.22
  (57 shorter events, 5.4 us)
Async XLA Ops:
  0.6 6.5 %copy-start = (f32[128,512]{1,0:T(8,128)S(1)}, f32[128,512]{1,0:T(8,128)}, u32[]{:S(2)}) copy-start(f32[128,512]{1,0:T(8,128)} %param.9) | copy-start | bytes 786436
  0.6 14.6 %copy-start.1 = (f32[512,128]{1,0:T(8,128)S(1)}, f32[512,128]{1,0:T(8,128)}, u32[]{:S(2)}) copy-start(f32[512,128]{1,0:T(8,128)} %param.8) | copy-start | bytes 786436
  0.7 14.5 %copy-start.5 = (f32[2,128]{1,0:T(2,128)S(1)}, f32[2,128]{1,0:T(2,128)}, u32[]{:S(2)}) copy-start(f32[2,128]{1,0:T(2,128)} %param.10) | copy-start | bytes 3076
  0.7 15.9 %collective-permute-start = (f32[2,128,512]{2,1,0:T(8,128)}, f32[2,128,512]{2,1,0:T(8,128)S(1)}, u32[]{:S(2)}, u32[]{:S(2)}) collective-permute-start(f32[2,128,512]{2,1,0:T(8,128)} %param.7), channel_id=1, source_target_pairs={{0,2},{1,3},{2,0},{3,1},{4,6},{5,7},{6,4},{7,5},{8,10},{9,11},{10,... | collective-permute-start | bytes 1572872 | tf_op jit(solution)/shard_map/ppermute | solution.py:42
  3.7 15.2 %collective-permute-start.2 = (f32[2,128,512]{2,1,0:T(8,128)}, f32[2,128,512]{2,1,0:T(8,128)}, u32[]{:S(2)}, u32[]{:S(2)}) collective-permute-start(f32[2,128,512]{2,1,0:T(8,128)} %param.7), channel_id=1, source_target_pairs={{0,1},{1,0},{2,3},{3,2},{4,5},{5,4},{6,7},{7,6},{8,9},{9,8},{10,11... | collective-permute-start | bytes 1572872 | tf_op jit(solution)/shard_map/ppermute | solution.py:42
  11.6 9.3 %collective-permute-start.6 = (f32[32,512]{1,0:T(8,128)S(1)}, f32[32,512]{1,0:T(8,128)S(1)}, u32[]{:S(2)}, u32[]{:S(2)}) collective-permute-start(f32[32,512]{1,0:T(8,128)S(1)} %constant_dynamic-slice_fusion), channel_id=1, source_target_pairs={{0,1},{1,0},{2,3},{3,2},{4,5},{5,4},{6,7},{7,6},{8,9},{9,8},{10,11... | collective-permute-start | bytes 196616 | tf_op jit(solution)/shard_map/ppermute | solution.py:42
  12.3 8.7 %collective-permute-start.5 = (f32[32,512]{1,0:T(8,128)S(1)}, f32[32,512]{1,0:T(8,128)S(1)}, u32[]{:S(2)}, u32[]{:S(2)}) collective-permute-start(f32[32,512]{1,0:T(8,128)S(1)} %constant_dynamic-slice_fusion), channel_id=1, source_target_pairs={{0,2},{1,3},{2,0},{3,1},{4,6},{5,7},{6,4},{7,5},{8,10},{9,11},{10,... | collective-permute-start | bytes 196616 | tf_op jit(solution)/shard_map/ppermute | solution.py:42
  12.3 8.6 %collective-permute-start.4 = (f32[32,512]{1,0:T(8,128)S(1)}, f32[32,512]{1,0:T(8,128)S(1)}, u32[]{:S(2)}, u32[]{:S(2)}) collective-permute-start(f32[32,512]{1,0:T(8,128)S(1)} %constant_dynamic-slice_fusion), channel_id=1, source_target_pairs={{0,3},{1,2},{2,1},{3,0},{4,7},{5,6},{6,5},{7,4},{8,11},{9,10},{10,... | collective-permute-start | bytes 196616 | tf_op jit(solution)/shard_map/ppermute | solution.py:42
  16.6 9.2 %collective-permute-start.1 = (f32[1,128,512]{2,1,0:T(8,128)S(1)}, f32[1,128,512]{2,1,0:T(8,128)S(1)}, u32[]{:S(2)}, u32[]{:S(2)}) collective-permute-start(f32[1,128,512]{2,1,0:T(8,128)S(1)} %slice.59), channel_id=1, source_target_pairs={{0,1},{1,0},{2,3},{3,2},{4,5},{5,4},{6,7},{7,6},{8,9},{9,8},{10,11... | collective-permute-start | bytes 786440 | tf_op jit(solution)/shard_map/ppermute | solution.py:42
  19.8 6.4 %collective-permute-start.3 = (f32[1,128,512]{2,1,0:T(8,128)S(1)}, f32[1,128,512]{2,1,0:T(8,128)S(1)}, u32[]{:S(2)}, u32[]{:S(2)}) collective-permute-start(f32[1,128,512]{2,1,0:T(8,128)S(1)} %slice.60), channel_id=1, source_target_pairs={{0,2},{1,3},{2,0},{3,1},{4,6},{5,7},{6,4},{7,5},{8,10},{9,11},{10,... | collective-permute-start | bytes 786440 | tf_op jit(solution)/shard_map/ppermute | solution.py:42
  21.0 10.7 %collective-permute-start.7 = (f32[4,32,512]{2,1,0:T(8,128)S(1)}, f32[4,32,512]{2,1,0:T(8,128)S(1)}, u32[]{:S(2)}, u32[]{:S(2)}) collective-permute-start(f32[4,32,512]{2,1,0:T(8,128)S(1)} %pad_maximum_fusion.4), channel_id=1, source_target_pairs={{0,8},{1,9},{2,10},{3,11},{4,12},{5,13},{6,14},{7,15},{8,0},{9,1},... | collective-permute-start | bytes 786440 | tf_op jit(solution)/shard_map/ppermute | solution.py:42
  31.7 2.7 %collective-permute-start.8 = (f32[512,512]{1,0:T(8,128)S(1)}, f32[512,512]{1,0:T(8,128)S(1)}, u32[]{:S(2)}, u32[]{:S(2)}) collective-permute-start(f32[512,512]{1,0:T(8,128)S(1)} %fusion.40), channel_id=1, source_target_pairs={{0,4},{1,5},{2,6},{3,7},{4,0},{5,1},{6,2},{7,3},{8,12},{9,13},{10,... | collective-permute-start | bytes 3145736 | tf_op jit(solution)/shard_map/ppermute | solution.py:42
  32.2 3.2 %collective-permute-start.9 = (f32[1,512]{1,0:T(1,128)S(1)}, f32[1,512]{1,0:T(1,128)S(1)}, u32[]{:S(2)}, u32[]{:S(2)}) collective-permute-start(f32[1,512]{1,0:T(1,128)S(1)} %convolution_add_fusion.13), channel_id=1, source_target_pairs={{0,4},{1,5},{2,6},{3,7},{4,0},{5,1},{6,2},{7,3},{8,12},{9,13},{10,... | collective-permute-start | bytes 6152 | tf_op jit(solution)/shard_map/ppermute | solution.py:42
  32.8 7.7 %collective-permute-start.11 = (f32[2,4,32,512]{3,2,0,1:T(8,128)S(1)}, f32[2,4,32,512]{3,2,0,1:T(8,128)S(1)}, u32[]{:S(2)}, u32[]{:S(2)}) collective-permute-start(f32[2,4,32,512]{3,2,0,1:T(8,128)S(1)} %pad_maximum_fusion.3), channel_id=1, source_target_pairs={{0,4},{1,5},{2,6},{3,7},{4,0},{5,1},{6,2},{7,3},{8,12},{9,13},{10,... | collective-permute-start | bytes 1572872 | tf_op jit(solution)/shard_map/ppermute | solution.py:42
  35.4 1.1 %copy-start.4 = (f32[512]{0:T(512)S(1)}, f32[512]{0:T(512)}, u32[]{:S(2)}) copy-start(f32[512]{0:T(512)} %param.12) | copy-start | bytes 6148
  37.1 4.8 %collective-permute-start.10 = (f32[1,512]{1,0:T(1,128)S(1)}, f32[1,512]{1,0:T(1,128)S(1)}, u32[]{:S(2)}, u32[]{:S(2)}) collective-permute-start(f32[1,512]{1,0:T(1,128)S(1)} %convolution_add_fusion.14), channel_id=1, source_target_pairs={{0,8},{1,9},{2,10},{3,11},{4,12},{5,13},{6,14},{7,15}} | collective-permute-start | bytes 6152 | tf_op jit(solution)/shard_map/ppermute | solution.py:42
  42.4 3.9 %collective-permute-start.12 = (f32[1,512]{1,0:T(1,128)S(1)}, f32[1,512]{1,0:T(1,128)S(1)}, u32[]{:S(2)}, u32[]{:S(2)}) collective-permute-start(f32[1,512]{1,0:T(1,128)S(1)} %convolution_add_fusion.10), channel_id=1, source_target_pairs={{8,16},{9,17},{10,18},{11,19},{12,20},{13,21},{14,22},{15,23}} | collective-permute-start | bytes 6152 | tf_op jit(solution)/shard_map/ppermute | solution.py:42
  46.8 3.6 %copy-start.2 = (f32[512,128]{1,0:T(8,128)S(1)}, f32[512,128]{1,0:T(8,128)}, u32[]{:S(2)}) copy-start(f32[512,128]{1,0:T(8,128)} %param.8) | copy-start | bytes 786436
  46.8 2.8 %collective-permute-start.13 = (f32[1,512]{1,0:T(1,128)S(1)}, f32[1,512]{1,0:T(1,128)S(1)}, u32[]{:S(2)}, u32[]{:S(2)}) collective-permute-start(f32[1,512]{1,0:T(1,128)S(1)} %convolution_add_fusion.9), channel_id=1, source_target_pairs={{16,24},{17,25},{18,26},{19,27},{20,28},{21,29},{22,30},{23,31}} | collective-permute-start | bytes 6152 | tf_op jit(solution)/shard_map/ppermute | solution.py:42
  51.0 1.2 %collective-permute-start.14 = (f32[2,512]{1,0:T(2,128)S(1)}, f32[2,512]{1,0:T(2,128)S(1)}, u32[]{:S(2)}, u32[]{:S(2)}) collective-permute-start(f32[2,512]{1,0:T(2,128)S(1)} %pad_maximum_fusion.6), channel_id=1, source_target_pairs={{0,4},{1,5},{2,6},{3,7},{4,0},{5,1},{6,2},{7,3},{8,12},{9,13},{10,... | collective-permute-start | bytes 12296 | tf_op jit(solution)/shard_map/ppermute | solution.py:42
  52.3 7.3 %collective-permute-start.17 = (f32[4,512]{1,0:T(4,128)S(1)}, f32[4,512]{1,0:T(4,128)S(1)}, u32[]{:S(2)}, u32[]{:S(2)}) collective-permute-start(f32[4,512]{1,0:T(4,128)S(1)} %pad_maximum_fusion.5), channel_id=1, source_target_pairs={{24,0},{25,1},{26,2},{27,3},{28,4},{29,5},{30,6},{31,7}} | collective-permute-start | bytes 24584 | tf_op jit(solution)/shard_map/ppermute | solution.py:42
  53.6 6.4 %collective-permute-start.16 = (f32[4,512]{1,0:T(4,128)S(1)}, f32[4,512]{1,0:T(4,128)S(1)}, u32[]{:S(2)}, u32[]{:S(2)}) collective-permute-start(f32[4,512]{1,0:T(4,128)S(1)} %pad_maximum_fusion.5), channel_id=1, source_target_pairs={{16,0},{17,1},{18,2},{19,3},{20,4},{21,5},{22,6},{23,7},{24,8},{25... | collective-permute-start | bytes 24584 | tf_op jit(solution)/shard_map/ppermute | solution.py:42
  54.9 5.8 %collective-permute-start.15 = (f32[4,512]{1,0:T(4,128)S(1)}, f32[4,512]{1,0:T(4,128)S(1)}, u32[]{:S(2)}, u32[]{:S(2)}) collective-permute-start(f32[4,512]{1,0:T(4,128)S(1)} %pad_maximum_fusion.5), channel_id=1, source_target_pairs={{8,0},{9,1},{10,2},{11,3},{12,4},{13,5},{14,6},{15,7},{16,8},{17,9... | collective-permute-start | bytes 24584 | tf_op jit(solution)/shard_map/ppermute | solution.py:42
  60.7 1.7 %copy-start.3 = (f32[512,512]{1,0:T(8,128)S(1)}, f32[512,512]{1,0:T(8,128)}, u32[]{:S(2)}) copy-start(f32[512,512]{1,0:T(8,128)} %fusion.43) | copy-start | bytes 3145732

commit v5 on v4

--- a/solution.py
+++ b/solution.py
@@ -55,12 +55,10 @@
         weights = present.astype(jnp.float32)
         drive = weights[:, None] * by(gain, observations)
         taken = [-weights[e] * gain for e in range(epochs)]
-        unit = jnp.eye(width, dtype=jnp.float32)
-        update = [unit + mm(taken[e], obs_matrix) for e in range(epochs)]
 
         share = part_rows // 4
         own_share = lax.dynamic_slice_in_dim(smoother_gain, place % 4 * share, share, 0)
-        own_share = after(own_share, update)
+        own_share = after(own_share, drive)
 
         if parts == 4:
             from_x, from_y = along(propagator_matrices, 1), along(propagator_matrices, 2)
@@ -76,77 +74,79 @@
             shares = lax.all_gather(own_share, "row", axis=0)
         next_shares = send(shares, lambda s, r: (s ^ 2, r))
 
-        reach, maps = [], []
+        maps, seen = [], []
         for e in range(epochs):
-            reach.append(mm(full[e], maps[-1]) if e else full[e])
-            maps.append(mm(update[e], reach[e]))
+            reach = mm(full[e], maps[-1]) if e else full[e]
+            seen.append(mm(obs_matrix, reach))
+            maps.append(reach + mm(taken[e], seen[e]))
         slab_map, shares, next_shares = lax.optimization_barrier((maps[-1], shares, next_shares))
         maps[-1] = slab_map
         else_map = other_core(slab_map)
         mine = jnp.stack(in_order([shares, next_shares], plane % 2), 0)
         theirs = other_core(mine)
 
-        offsets, reach_0 = [drive[0:1]], [None]
+        offsets = [after(drive, slab_map)[0:1]]
+        seen_0 = [jnp.zeros((1, obs_matrix.shape[0]), jnp.float32)]
         for e in range(1, epochs):
-            reach_0.append(by(full[e], offsets[-1]))
-            offsets.append(by(update[e], reach_0[e]) + drive[e : e + 1])
+            reach_0 = by(full[e], offsets[-1])
+            seen_0.append(by(obs_matrix, reach_0))
+            offsets.append(reach_0 + by(taken[e], seen_0[e]) + drive[e : e + 1])
         slab_offset = offsets[-1]
 
         else_offset = other_core(slab_offset)
         plane_map = mm(jnp.where(odd, slab_map, else_map), jnp.where(odd, else_map, slab_map))
-        plane_offset = jnp.where(
-            odd, by(slab_map, else_offset) + slab_offset, by(else_map, slab_offset) + else_offset
-        )
+        last_offset = by(slab_map, else_offset) + slab_offset
+        else_last = after(other_core(last_offset), plane_map)
+        plane_offset = jnp.where(odd, last_offset, else_last)
 
-        powers, seen, seen_0 = [], [], []
+        powers = []
         count = 2 * epochs * planes
 
-        def smoother_rows(ahead):
+        def first_work(ahead):
             smoother = jnp.stack(in_order(after([mine, theirs], ahead), place % 2), 1)
             powers.append(smoother.transpose(2, 0, 1, 3, 4).reshape(width, width))
             powers.append(mm(powers[0], powers[0]))
+            maps_0, base = after((seen, seen_0), ahead)
+            seen[:] = [
+                lax.concatenate([-weights[e] * maps_0[e] for e in range(epochs)], 0),
+                weights[:, None] * (observations - lax.concatenate(base, 0)),
+            ]
 
-        def smoother_powers(ahead):
-            powers[-1] = after(powers[-1], ahead)
+        def second_work(ahead):
+            powers[-1], seen[:] = after((powers[-1], seen), ahead)
+            powers.append(mm(powers[-1], powers[-1]))
+            moved = [mm(seen[0], else_map), by(seen[0], else_offset).reshape(seen[1].shape) + seen[1]]
+            seen[:] = [jnp.where(odd, a, b) for a, b in zip(moved, seen)]
+
+        def third_work(ahead):
+            powers[-1], seen[:] = after((powers[-1], seen), ahead)
+            seen[:] = [
+                lax.concatenate(in_order([a, other_core(a)], place % 2), 0) for a in seen
+            ]
             while 2 ** len(powers) < count:
                 powers.append(mm(powers[-1], powers[-1]))
 
-        def observed_maps(ahead):
-            for e, a in enumerate(after(reach, ahead)):
-                seen.append(mm(obs_matrix, a))
-                seen_0.append(by(obs_matrix, reach_0[e]) if e else jnp.zeros((1, obs_matrix.shape[0])))
-
-        works = [smoother_rows, smoother_powers, observed_maps]
+        works = [first_work, second_work, third_work]
         state = initial[None, :]
         for k in range(planes - 1):
             ahead = by(plane_map, state) + plane_offset
             received = send(ahead, lambda s, r: (s + 2, r), lambda s: s // 2 == k)
             if works:
                 works.pop(0)(ahead)
-                received, powers, seen, seen_0 = lax.optimization_barrier(
-                    (received, powers, seen, seen_0)
-                )
+                received, powers, seen = lax.optimization_barrier((received, powers, seen))
             state = jnp.where(plane == k + 1, received, state)
         for work in works:
             work(state)
 
-        state = jnp.where(odd, by(else_map, state) + else_offset, state)
-        correction = lax.concatenate(
-            [
-                by(taken[e], by(seen[e], state) + seen_0[e]) + drive[e : e + 1]
-                for e in range(epochs)
-            ],
-            0,
-        )
-        other = other_core(correction)
-        own = lax.concatenate(
-            [jnp.where(odd, other, correction), jnp.where(odd, correction, other)], 0
-        )
+        innovations = by(seen[0], state).reshape(seen[1].shape) + seen[1]
+        own = by(gain, innovations)
         terms = [own]
         for k in range(1, planes):
             terms.append(send(own, lambda s, r: (s - 2 * k, r)))
 
         state = after(state, own)
+        state = jnp.where(odd, by(else_map, state) + else_offset, state)
+        correction = jnp.where(odd, own[epochs:], own[:epochs])
         filtered = lax.concatenate([by(maps[e], state) + offsets[e] for e in range(epochs)], 0)
 
         carried = lax.concatenate(terms, 0)

time: 63.9 us -> 59.9 us (0.937)
  matrix products: 21.8 us -> 18.3 us
  local copies, waits for them, and re-layouts: 2.68 us -> 1.54 us
  other arithmetic: 3.37 us -> 2.51 us
  starting transfers between devices: 22.5 us -> 23.3 us
  waiting for transfers between devices: 10.8 us -> 11.5 us
    dot_general x11 -> x10, matrix products: 13.2 us -> 9.5 us  [mm(): return jnp.dot(a, b, precision=HIGH)]
    select_n x1 -> x3, other arithmetic: 1.5 us -> 0.37 us  [in_order(): jnp.where(crossed, pieces[i ^ bit], pieces[i])]
    slice x2, local copies, waits for them, and re-layouts: 0.99 us -> 0.04 us  [on_device(): far = lax.concatenate([along(from_y[:mid], 1), along(from_x[mid:], 2)], 0)]
    ppermute x18 -> x20, starting transfers between devices: 22.5 us -> 23.3 us  [send(): return lax.ppermute(a, AXES, perm)]
    ppermute x18 -> x20, waiting for transfers between devices: 10.8 us -> 11.5 us  [send(): return lax.ppermute(a, AXES, perm)]
    dot_general x20 -> x18, matrix products: 8.6 us -> 8.82 us  [by(): lax.dot_general(rows, matrix, (((1,), (1,)), ((), ())), precision=HIGH)]
  transfers between devices with their start and end apart: 18 -> 20, of which waited for: 10 -> 10; matrix products, arithmetic and copies ran while one was open for 36% -> 30% of each run, Pallas kernels for 0% -> 0%
where the time goes in v5:
time: 59.9 us; the launch traced here: 59.6 us
  starting transfers between devices  23.3 us (39%)
  matrix products  18.3 us (31%)
  waiting for transfers between devices  11.5 us (19%)
  other arithmetic  2.51 us (4%)
  between operations  2.4 us (4%)
  local copies, waits for them, and re-layouts  1.54 us (3%)
    ppermute x20, starting transfers between devices, send(): return lax.ppermute(a, AXES, perm)  23.3 us
    ppermute x20, waiting for transfers between devices, send(): return lax.ppermute(a, AXES, perm)  11.5 us
    dot_general x10, matrix products, mm(): return jnp.dot(a, b, precision=HIGH)  9.5 us
    dot_general x18, matrix products, by(): lax.dot_general(rows, matrix, (((1,), (1,)), ((), ())), precision=HIGH)  8.82 us
  transfers between devices with their start and end apart: 20, of which 10 were waited for; matrix products, arithmetic and copies ran while one was open for 30% of the time, Pallas kernels for 0%

profile of v5, /device:TPU:0, one launch (start us, length us, event | category | flops | bytes accessed | tf_op | source)
XLA Modules:
  0.0 59.6 jit_solution(622819309023100679)
XLA Ops:
  0.7 3.0 %collective-permute-start = (f32[2,128,512]{2,1,0:T(8,128)}, f32[2,128,512]{2,1,0:T(8,128)S(1)}, u32[]{:S(2)}, u32[]{:S(2)}) collective-permute-start(f32[2,128,512]{2,1,0:T(8,128)} %param.7), channel_id=1, source_target_pairs={{0,2},{1,3},{2,0},{3,1},{4,6},{5,7},{6,4},{7,5},{8,10},{9,11},{10,... | collective-permute-start | bytes 1572872 | tf_op jit(solution)/shard_map/ppermute | solution.py:42
  3.7 1.5 %collective-permute-start.2 = (f32[2,128,512]{2,1,0:T(8,128)}, f32[2,128,512]{2,1,0:T(8,128)S(1)}, u32[]{:S(2)}, u32[]{:S(2)}) collective-permute-start(f32[2,128,512]{2,1,0:T(8,128)} %param.7), channel_id=1, source_target_pairs={{0,1},{1,0},{2,3},{3,2},{4,5},{5,4},{6,7},{7,6},{8,9},{9,8},{10,11... | collective-permute-start | bytes 1572872 | tf_op jit(solution)/shard_map/ppermute | solution.py:42
  5.2 0.7 %convert_element_type.11 = f32[2]{0:T(128)S(1)} convert(s32[2]{0:T(128)} %param.11) | non-fusion elementwise | flops 2 | bytes 16 | tf_op jit(solution)/shard_map/convert_element_type | solution.py:55
  5.8 0.8 %constant_dynamic-slice_fusion = f32[32,512]{1,0:T(8,128)S(1)} fusion(f32[128,512]{1,0:T(8,128)} %param.13, s32[]{:T(128)S(6)} %select_n.230), kind=kLoop, calls=%fused_computation.104 | loop fusion | bytes 131076 | tf_op jit(solution)/shard_map/dynamic_slice | solution.py:60
  6.7 1.2 %convolution_multiply_fusion = f32[2,512]{1,0:T(2,128)S(1)} fusion(f32[2,128]{1,0:T(2,128)} %param.10, f32[512,128]{1,0:T(8,128)} %param.8, f32[2]{0:T(128)S(1)} %convert_element_type.11), kind=kOutput, calls=%fused_computation.8 | convolution fusion | flops 787456 | bytes 267272 | tf_op jit(solution)/shard_map/dot_general | solution.py:15
  7.9 0.6 collective-permute-start.6
  8.5 2.9 %collective-permute-start.4 = (f32[32,512]{1,0:T(8,128)S(1)}, f32[32,512]{1,0:T(8,128)S(1)}, u32[]{:S(2)}, u32[]{:S(2)}) collective-permute-start(f32[32,512]{1,0:T(8,128)S(1)} %constant_dynamic-slice_fusion), channel_id=1, source_target_pairs={{0,3},{1,2},{2,1},{3,0},{4,7},{5,6},{6,5},{7,4},{8,11},{9,10},{10,... | collective-permute-start | bytes 196616 | tf_op jit(solution)/shard_map/ppermute | solution.py:42
  11.4 0.6 fusion.46
  13.3 3.3 %collective-permute-done = f32[2,128,512]{2,1,0:T(8,128)S(1)} collective-permute-done((f32[2,128,512]{2,1,0:T(8,128)}, f32[2,128,512]{2,1,0:T(8,128)S(1)}, u32[]{:S(2)}, u32[]{:S(2)}) %collective-permute-start) | collective-permute-done | bytes 524320 | tf_op jit(solution)/shard_map/ppermute | solution.py:42
  16.5 1.8 %collective-permute-start.1 = (f32[1,128,512]{2,1,0:T(8,128)S(1)}, f32[1,128,512]{2,1,0:T(8,128)S(1)}, u32[]{:S(2)}, u32[]{:S(2)}) collective-permute-start(f32[1,128,512]{2,1,0:T(8,128)S(1)} %slice.67), channel_id=1, source_target_pairs={{0,1},{1,0},{2,3},{3,2},{4,5},{5,4},{6,7},{7,6},{8,9},{9,8},{10,11... | collective-permute-start | bytes 786440 | tf_op jit(solution)/shard_map/ppermute | solution.py:42
  18.8 1.2 %collective-permute-start.3 = (f32[1,128,512]{2,1,0:T(8,128)S(1)}, f32[1,128,512]{2,1,0:T(8,128)S(1)}, u32[]{:S(2)}, u32[]{:S(2)}) collective-permute-start(f32[1,128,512]{2,1,0:T(8,128)S(1)} %slice.68), channel_id=1, source_target_pairs={{0,2},{1,3},{2,0},{3,1},{4,6},{5,7},{6,4},{7,5},{8,10},{9,11},{10,... | collective-permute-start | bytes 786440 | tf_op jit(solution)/shard_map/ppermute | solution.py:42
  20.2 0.9 %collective-permute-done.4 = f32[32,512]{1,0:T(8,128)S(1)} collective-permute-done((f32[32,512]{1,0:T(8,128)S(1)}, f32[32,512]{1,0:T(8,128)S(1)}, u32[]{:S(2)}, u32[]{:S(2)}) %collective-permute-start.4) | collective-permute-done | bytes 65568 | tf_op jit(solution)/shard_map/ppermute | solution.py:42
  21.1 2.0 %collective-permute-start.7 = (f32[4,32,512]{2,1,0:T(8,128)S(1)}, f32[4,32,512]{2,1,0:T(8,128)S(1)}, u32[]{:S(2)}, u32[]{:S(2)}) collective-permute-start(f32[4,32,512]{2,1,0:T(8,128)S(1)} %pad_maximum_fusion.6), channel_id=1, source_target_pairs={{0,8},{1,9},{2,10},{3,11},{4,12},{5,13},{6,14},{7,15},{8,0},{9,1},... | collective-permute-start | bytes 786440 | tf_op jit(solution)/shard_map/ppermute | solution.py:42
  23.1 2.6 %collective-permute-done.1 = f32[1,128,512]{2,1,0:T(8,128)S(1)} collective-permute-done((f32[1,128,512]{2,1,0:T(8,128)S(1)}, f32[1,128,512]{2,1,0:T(8,128)S(1)}, u32[]{:S(2)}, u32[]{:S(2)}) %collective-permute-start.1) | collective-permute-done | bytes 262176 | tf_op jit(solution)/shard_map/ppermute | solution.py:42
  26.3 1.0 %fusion.10 = f32[512,128]{1,0:T(8,128)S(1)} fusion(f32[128,512]{1,0:T(8,128)S(1)} %copy-done, f32[2,512,512]{2,1,0:T(8,128)S(1)} %pad_maximum_fusion), kind=kOutput, calls=%fused_computation.30 | convolution fusion | flops 201326592 | bytes 1572864 | tf_op jit(solution)/shard_map/dot_general | solution.py:11
  27.3 0.6 %convolution_add_fusion.1 = f32[512,512]{1,0:T(8,128)S(1)} fusion(f32[512,128]{1,0:T(8,128)S(1)} %fusion.10, f32[2,512,512]{2,1,0:T(8,128)S(1)} %pad_maximum_fusion, f32[512,128]{1,0:T(8,128)S(1)} %copy-done.1, f32[]{:T(128)} %bitcast.6), kind=kOutput, calls=%fused_computation.2 | convolution fusion | flops 201654272 | bytes 2621444 | tf_op jit(solution)/shard_map/dot_general | solution.py:11
  27.9 1.0 %fusion.9 = f32[512,512]{1,0:T(8,128)S(1)} fusion(f32[512,512]{1,0:T(8,128)S(1)} %convolution_add_fusion.1, f32[2,512,512]{2,1,0:T(8,128)S(1)} %pad_maximum_fusion), kind=kOutput, calls=%fused_computation.29 | convolution fusion | flops 805306368 | bytes 3145728 | tf_op jit(solution)/shard_map/dot_general | solution.py:11
  29.0 1.0 %fusion.47 = f32[512,128]{1,0:T(8,128)S(1)} fusion(f32[512,512]{1,0:T(8,128)S(1)} %fusion.9, f32[128,512]{1,0:T(8,128)S(1)} %copy-done), kind=kOutput, calls=%fused_computation.110 | convolution fusion | flops 201326592 | bytes 1572864 | tf_op jit(solution)/shard_map/dot_general | solution.py:11
  30.0 0.6 %convolution_add_fusion = f32[512,512]{1,0:T(8,128)S(1)} fusion(f32[512,512]{1,0:T(8,128)S(1)} %fusion.9, f32[512,128]{1,0:T(8,128)S(1)} %fusion.47, f32[512,128]{1,0:T(8,128)S(1)} %copy-done.1, f32[]{:T(128)} %bitcast.7), kind=kOutput, calls=%fused_computation.1 | convolution fusion | flops 201654272 | bytes 2621444 | tf_op jit(solution)/shard_map/dot_general | solution.py:11
  30.7 0.5 fusion.8
  31.7 0.6 collective-permute-start.9
  32.4 0.9 %collective-permute-done.9 = f32[1,512]{1,0:T(1,128)S(1)} collective-permute-done((f32[1,512]{1,0:T(1,128)S(1)}, f32[1,512]{1,0:T(1,128)S(1)}, u32[]{:S(2)}, u32[]{:S(2)}) %collective-permute-start.9) | collective-permute-done | bytes 2080 | tf_op jit(solution)/shard_map/ppermute | solution.py:42
  33.3 0.5 convolution_add_fusion.11
  34.0 1.0 %fusion.5 = f32[512,512]{1,0:T(8,128)S(1)} fusion(f32[512,512]{1,0:T(8,128)S(1)} %collective-permute-done.8, f32[512,512]{1,0:T(8,128)S(1)} %convolution_add_fusion, pred[]{:T(512)S(6)} %eq.19), kind=kOutput, calls=%fused_computation.25 | convolution fusion | flops 805830656 | bytes 3145729 | tf_op jit(solution)/shard_map/dot_general | solution.py:11
  35.1 0.5 convolution_add_fusion.12
  35.6 3.5 %collective-permute-start.11 = (f32[1,512]{1,0:T(1,128)S(1)}, f32[1,512]{1,0:T(1,128)S(1)}, u32[]{:S(2)}, u32[]{:S(2)}) collective-permute-start(f32[1,512]{1,0:T(1,128)S(1)} %convolution_add_fusion.12), channel_id=1, source_target_pairs={{0,8},{1,9},{2,10},{3,11},{4,12},{5,13},{6,14},{7,15}} | collective-permute-start | bytes 6152 | tf_op jit(solution)/shard_map/ppermute | solution.py:42
  39.4 1.0 %fusion.48 = f32[512,512]{1,0:T(8,128)S(1)} fusion(f32[512,512]{1,0:T(8,128)S(1)} %bitcast.138), kind=kOutput, calls=%fused_computation.111 | convolution fusion | flops 805306368 | bytes 2097152 | tf_op jit(solution)/shard_map/dot_general | solution.py:11
  40.6 0.5 convolution_add_fusion.10
  41.2 0.8 %collective-permute-start.13 = (f32[1,512]{1,0:T(1,128)S(1)}, f32[1,512]{1,0:T(1,128)S(1)}, u32[]{:S(2)}, u32[]{:S(2)}) collective-permute-start(f32[1,512]{1,0:T(1,128)S(1)} %convolution_add_fusion.10), channel_id=1, source_target_pairs={{8,16},{9,17},{10,18},{11,19},{12,20},{13,21},{14,22},{15,23}} | collective-permute-start | bytes 6152 | tf_op jit(solution)/shard_map/ppermute | solution.py:42
  42.0 1.0 %fusion.49 = f32[512,512]{1,0:T(8,128)S(1)} fusion(f32[512,512]{1,0:T(8,128)S(1)} %fusion.48), kind=kOutput, calls=%fused_computation.112 | convolution fusion | flops 805306368 | bytes 2097152 | tf_op jit(solution)/shard_map/dot_general | solution.py:11
  43.2 1.1 %convolution_select_fusion = f32[256,512]{0,1:T(8,128)S(1)} fusion(f32[256,512]{0,1:T(8,128)S(1)} %pad_maximum_fusion.5, f32[512,512]{1,0:T(8,128)S(1)} %collective-permute-done.8, pred[]{:T(512)S(6)} %eq.19), kind=kOutput, calls=%fused_computation.3 | convolution fusion | flops 402784256 | bytes 2097153 | tf_op jit(solution)/shard_map/dot_general | solution.py:11
  44.3 0.5 convolution_add_fusion.9
  44.9 0.7 %collective-permute-start.14 = (f32[1,512]{1,0:T(1,128)S(1)}, f32[1,512]{1,0:T(1,128)S(1)}, u32[]{:S(2)}, u32[]{:S(2)}) collective-permute-start(f32[1,512]{1,0:T(1,128)S(1)} %convolution_add_fusion.9), channel_id=1, source_target_pairs={{16,24},{17,25},{18,26},{19,27},{20,28},{21,29},{22,30},{23,31}} | collective-permute-start | bytes 6152 | tf_op jit(solution)/shard_map/ppermute | solution.py:42
  46.1 1.0 %fusion.50 = f32[512,512]{1,0:T(8,128)S(1)} fusion(f32[512,512]{1,0:T(8,128)S(1)} %fusion.49), kind=kOutput, calls=%fused_computation.113 | convolution fusion | flops 805306368 | bytes 2097152 | tf_op jit(solution)/shard_map/dot_general | solution.py:11
  47.2 0.5 collective-permute-done.15
  48.5 1.3 %collective-permute-start.19 = (f32[4,512]{1,0:T(4,128)S(1)}, f32[4,512]{1,0:T(4,128)S(1)}, u32[]{:S(2)}, u32[]{:S(2)}) collective-permute-start(f32[4,512]{1,0:T(4,128)S(1)} %fusion.37), channel_id=1, source_target_pairs={{24,0},{25,1},{26,2},{27,3},{28,4},{29,5},{30,6},{31,7}} | collective-permute-start | bytes 24584 | tf_op jit(solution)/shard_map/ppermute | solution.py:42
  49.8 1.3 %collective-permute-start.18 = (f32[4,512]{1,0:T(4,128)S(1)}, f32[4,512]{1,0:T(4,128)S(1)}, u32[]{:S(2)}, u32[]{:S(2)}) collective-permute-start(f32[4,512]{1,0:T(4,128)S(1)} %fusion.37), channel_id=1, source_target_pairs={{16,0},{17,1},{18,2},{19,3},{20,4},{21,5},{22,6},{23,7},{24,8},{25... | collective-permute-start | bytes 24584 | tf_op jit(solution)/shard_map/ppermute | solution.py:42
  51.1 1.3 %collective-permute-start.17 = (f32[4,512]{1,0:T(4,128)S(1)}, f32[4,512]{1,0:T(4,128)S(1)}, u32[]{:S(2)}, u32[]{:S(2)}) collective-permute-start(f32[4,512]{1,0:T(4,128)S(1)} %fusion.37), channel_id=1, source_target_pairs={{8,0},{9,1},{10,2},{11,3},{12,4},{13,5},{14,6},{15,7},{16,8},{17,9... | collective-permute-start | bytes 24584 | tf_op jit(solution)/shard_map/ppermute | solution.py:42
  52.4 0.5 fusion.1
  52.9 0.6 convolution_add_fusion.7
  53.5 0.6 convolution_add_fusion.6
  54.0 1.9 %collective-permute-done.19 = f32[4,512]{1,0:T(4,128)S(1)} collective-permute-done((f32[4,512]{1,0:T(4,128)S(1)}, f32[4,512]{1,0:T(4,128)S(1)}, u32[]{:S(2)}, u32[]{:S(2)}) %collective-permute-start.19) | collective-permute-done | bytes 8224 | tf_op jit(solution)/shard_map/ppermute | solution.py:42
  56.2 0.5 collective-permute-done.17
  56.7 0.5 convolution_add_fusion.5
  57.3 0.5 convolution_add_fusion.4
  57.8 0.5 convolution_add_fusion.3
  58.4 0.5 convolution_add_fusion.2
  58.9 0.6 %fusion.26 = (f32[2,512]{1,0:T(2,128)}, f32[2,512]{1,0:T(2,128)}) fusion(f32[4,512]{1,0:T(4,128)S(1)} %fusion.37, f32[16,512]{1,0:T(8,128)S(1)} %convolution_add_fusion.2, pred[]{:T(512)S(6)} %eq.19, f32[1,512]{1,0:T(1,128)S(1)} %convolution_add_fusion.6, f32[1,512]{1,0:T(1,128)S(1)} %convolution_add_fusion.7), kind=kLoop, calls=%fused_computation.76 | loop fusion | flops 5120 | bytes 28673 | tf_op jit(solution)/shard_map/sub | solution.py:157
  (64 shorter events, 4.5 us)
Async XLA Ops:
  0.6 25.6 %copy-start = (f32[128,512]{1,0:T(8,128)S(1)}, f32[128,512]{1,0:T(8,128)}, u32[]{:S(2)}) copy-start(f32[128,512]{1,0:T(8,128)} %param.9) | copy-start | bytes 786436
  0.6 25.1 %copy-start.2 = (f32[2,128,512]{2,1,0:T(8,128)S(1)}, f32[2,128,512]{2,1,0:T(8,128)}, u32[]{:S(2)}) copy-start(f32[2,128,512]{2,1,0:T(8,128)} %param.7) | copy-start | bytes 1572868
  0.7 15.9 %collective-permute-start = (f32[2,128,512]{2,1,0:T(8,128)}, f32[2,128,512]{2,1,0:T(8,128)S(1)}, u32[]{:S(2)}, u32[]{:S(2)}) collective-permute-start(f32[2,128,512]{2,1,0:T(8,128)} %param.7), channel_id=1, source_target_pairs={{0,2},{1,3},{2,0},{3,1},{4,6},{5,7},{6,4},{7,5},{8,10},{9,11},{10,... | collective-permute-start | bytes 1572872 | tf_op jit(solution)/shard_map/ppermute | solution.py:42
  3.7 15.1 %collective-permute-start.2 = (f32[2,128,512]{2,1,0:T(8,128)}, f32[2,128,512]{2,1,0:T(8,128)S(1)}, u32[]{:S(2)}, u32[]{:S(2)}) collective-permute-start(f32[2,128,512]{2,1,0:T(8,128)} %param.7), channel_id=1, source_target_pairs={{0,1},{1,0},{2,3},{3,2},{4,5},{5,4},{6,7},{7,6},{8,9},{9,8},{10,11... | collective-permute-start | bytes 1572872 | tf_op jit(solution)/shard_map/ppermute | solution.py:42
  7.9 12.3 %collective-permute-start.6 = (f32[32,512]{1,0:T(8,128)S(1)}, f32[32,512]{1,0:T(8,128)S(1)}, u32[]{:S(2)}, u32[]{:S(2)}) collective-permute-start(f32[32,512]{1,0:T(8,128)S(1)} %constant_dynamic-slice_fusion), channel_id=1, source_target_pairs={{0,1},{1,0},{2,3},{3,2},{4,5},{5,4},{6,7},{7,6},{8,9},{9,8},{10,11... | collective-permute-start | bytes 196616 | tf_op jit(solution)/shard_map/ppermute | solution.py:42
  8.4 11.7 %collective-permute-start.5 = (f32[32,512]{1,0:T(8,128)S(1)}, f32[32,512]{1,0:T(8,128)S(1)}, u32[]{:S(2)}, u32[]{:S(2)}) collective-permute-start(f32[32,512]{1,0:T(8,128)S(1)} %constant_dynamic-slice_fusion), channel_id=1, source_target_pairs={{0,2},{1,3},{2,0},{3,1},{4,6},{5,7},{6,4},{7,5},{8,10},{9,11},{10,... | collective-permute-start | bytes 196616 | tf_op jit(solution)/shard_map/ppermute | solution.py:42
  8.5 12.5 %collective-permute-start.4 = (f32[32,512]{1,0:T(8,128)S(1)}, f32[32,512]{1,0:T(8,128)S(1)}, u32[]{:S(2)}, u32[]{:S(2)}) collective-permute-start(f32[32,512]{1,0:T(8,128)S(1)} %constant_dynamic-slice_fusion), channel_id=1, source_target_pairs={{0,3},{1,2},{2,1},{3,0},{4,7},{5,6},{6,5},{7,4},{8,11},{9,10},{10,... | collective-permute-start | bytes 196616 | tf_op jit(solution)/shard_map/ppermute | solution.py:42
  16.5 9.2 %collective-permute-start.1 = (f32[1,128,512]{2,1,0:T(8,128)S(1)}, f32[1,128,512]{2,1,0:T(8,128)S(1)}, u32[]{:S(2)}, u32[]{:S(2)}) collective-permute-start(f32[1,128,512]{2,1,0:T(8,128)S(1)} %slice.67), channel_id=1, source_target_pairs={{0,1},{1,0},{2,3},{3,2},{4,5},{5,4},{6,7},{7,6},{8,9},{9,8},{10,11... | collective-permute-start | bytes 786440 | tf_op jit(solution)/shard_map/ppermute | solution.py:42
  18.8 6.9 %collective-permute-start.3 = (f32[1,128,512]{2,1,0:T(8,128)S(1)}, f32[1,128,512]{2,1,0:T(8,128)S(1)}, u32[]{:S(2)}, u32[]{:S(2)}) collective-permute-start(f32[1,128,512]{2,1,0:T(8,128)S(1)} %slice.68), channel_id=1, source_target_pairs={{0,2},{1,3},{2,0},{3,1},{4,6},{5,7},{6,4},{7,5},{8,10},{9,11},{10,... | collective-permute-start | bytes 786440 | tf_op jit(solution)/shard_map/ppermute | solution.py:42
  21.1 9.5 %collective-permute-start.7 = (f32[4,32,512]{2,1,0:T(8,128)S(1)}, f32[4,32,512]{2,1,0:T(8,128)S(1)}, u32[]{:S(2)}, u32[]{:S(2)}) collective-permute-start(f32[4,32,512]{2,1,0:T(8,128)S(1)} %pad_maximum_fusion.6), channel_id=1, source_target_pairs={{0,8},{1,9},{2,10},{3,11},{4,12},{5,13},{6,14},{7,15},{8,0},{9,1},... | collective-permute-start | bytes 786440 | tf_op jit(solution)/shard_map/ppermute | solution.py:42
  26.1 1.2 %copy-start.1 = (f32[512,128]{1,0:T(8,128)S(1)}, f32[512,128]{1,0:T(8,128)}, u32[]{:S(2)}) copy-start(f32[512,128]{1,0:T(8,128)} %param.8) | copy-start | bytes 786436
  30.6 3.4 %collective-permute-start.8 = (f32[512,512]{1,0:T(8,128)S(1)}, f32[512,512]{1,0:T(8,128)S(1)}, u32[]{:S(2)}, u32[]{:S(2)}) collective-permute-start(f32[512,512]{1,0:T(8,128)S(1)} %convolution_add_fusion), channel_id=1, source_target_pairs={{0,4},{1,5},{2,6},{3,7},{4,0},{5,1},{6,2},{7,3},{8,12},{9,13},{10,... | collective-permute-start | bytes 3145736 | tf_op jit(solution)/shard_map/ppermute | solution.py:42
  31.7 1.6 %collective-permute-start.9 = (f32[1,512]{1,0:T(1,128)S(1)}, f32[1,512]{1,0:T(1,128)S(1)}, u32[]{:S(2)}, u32[]{:S(2)}) collective-permute-start(f32[1,512]{1,0:T(1,128)S(1)} %slice_add_fusion), channel_id=1, source_target_pairs={{0,4},{1,5},{2,6},{3,7},{4,0},{5,1},{6,2},{7,3},{8,12},{9,13},{10,... | collective-permute-start | bytes 6152 | tf_op jit(solution)/shard_map/ppermute | solution.py:42
  32.3 6.8 %collective-permute-start.12 = (f32[2,4,32,512]{3,2,0,1:T(8,128)S(1)}, f32[2,4,32,512]{3,2,0,1:T(8,128)S(1)}, u32[]{:S(2)}, u32[]{:S(2)}) collective-permute-start(f32[2,4,32,512]{3,2,0,1:T(8,128)S(1)} %pad_maximum_fusion.4), channel_id=1, source_target_pairs={{0,4},{1,5},{2,6},{3,7},{4,0},{5,1},{6,2},{7,3},{8,12},{9,13},{10,... | collective-permute-start | bytes 1572872 | tf_op jit(solution)/shard_map/ppermute | solution.py:42
  33.9 1.2 %copy-start.3 = (f32[512]{0:T(512)S(1)}, f32[512]{0:T(512)}, u32[]{:S(2)}) copy-start(f32[512]{0:T(512)} %param.12) | copy-start | bytes 6148
  33.9 1.2 %collective-permute-start.10 = (f32[1,512]{1,0:T(1,128)S(1)}, f32[1,512]{1,0:T(1,128)S(1)}, u32[]{:S(2)}, u32[]{:S(2)}) collective-permute-start(f32[1,512]{1,0:T(1,128)S(1)} %convolution_add_fusion.11), channel_id=1, source_target_pairs={{0,4},{1,5},{2,6},{3,7},{4,0},{5,1},{6,2},{7,3},{8,12},{9,13},{10,... | collective-permute-start | bytes 6152 | tf_op jit(solution)/shard_map/ppermute | solution.py:42
  35.6 5.0 %collective-permute-start.11 = (f32[1,512]{1,0:T(1,128)S(1)}, f32[1,512]{1,0:T(1,128)S(1)}, u32[]{:S(2)}, u32[]{:S(2)}) collective-permute-start(f32[1,512]{1,0:T(1,128)S(1)} %convolution_add_fusion.12), channel_id=1, source_target_pairs={{0,8},{1,9},{2,10},{3,11},{4,12},{5,13},{6,14},{7,15}} | collective-permute-start | bytes 6152 | tf_op jit(solution)/shard_map/ppermute | solution.py:42
  39.4 1.1 %copy-start.4 = (f32[2,128]{1,0:T(2,128)S(1)}, f32[2,128]{1,0:T(2,128)}, u32[]{:S(2)}) copy-start(f32[2,128]{1,0:T(2,128)} %param.10) | copy-start | bytes 3076
  41.2 3.2 %collective-permute-start.13 = (f32[1,512]{1,0:T(1,128)S(1)}, f32[1,512]{1,0:T(1,128)S(1)}, u32[]{:S(2)}, u32[]{:S(2)}) collective-permute-start(f32[1,512]{1,0:T(1,128)S(1)} %convolution_add_fusion.10), channel_id=1, source_target_pairs={{8,16},{9,17},{10,18},{11,19},{12,20},{13,21},{14,22},{15,23}} | collective-permute-start | bytes 6152 | tf_op jit(solution)/shard_map/ppermute | solution.py:42
  44.9 3.0 %collective-permute-start.14 = (f32[1,512]{1,0:T(1,128)S(1)}, f32[1,512]{1,0:T(1,128)S(1)}, u32[]{:S(2)}, u32[]{:S(2)}) collective-permute-start(f32[1,512]{1,0:T(1,128)S(1)} %convolution_add_fusion.9), channel_id=1, source_target_pairs={{16,24},{17,25},{18,26},{19,27},{20,28},{21,29},{22,30},{23,31}} | collective-permute-start | bytes 6152 | tf_op jit(solution)/shard_map/ppermute | solution.py:42
  45.5 1.6 %collective-permute-start.16 = (f32[2,128]{1,0:T(2,128)S(1)}, f32[2,128]{1,0:T(2,128)S(1)}, u32[]{:S(2)}, u32[]{:S(2)}) collective-permute-start(f32[2,128]{1,0:T(2,128)S(1)} %add_select_fusion), channel_id=1, source_target_pairs={{0,4},{1,5},{2,6},{3,7},{4,0},{5,1},{6,2},{7,3},{8,12},{9,13},{10,... | collective-permute-start | bytes 3080 | tf_op jit(solution)/shard_map/ppermute | solution.py:42
  45.7 2.0 %collective-permute-start.15 = (f32[256,512]{0,1:T(8,128)S(1)}, f32[256,512]{0,1:T(8,128)S(1)}, u32[]{:S(2)}, u32[]{:S(2)}) collective-permute-start(f32[256,512]{0,1:T(8,128)S(1)} %convolution_select_fusion), channel_id=1, source_target_pairs={{0,4},{1,5},{2,6},{3,7},{4,0},{5,1},{6,2},{7,3},{8,12},{9,13},{10,... | collective-permute-start | bytes 1572872 | tf_op jit(solution)/shard_map/ppermute | solution.py:42
  48.5 7.4 %collective-permute-start.19 = (f32[4,512]{1,0:T(4,128)S(1)}, f32[4,512]{1,0:T(4,128)S(1)}, u32[]{:S(2)}, u32[]{:S(2)}) collective-permute-start(f32[4,512]{1,0:T(4,128)S(1)} %fusion.37), channel_id=1, source_target_pairs={{24,0},{25,1},{26,2},{27,3},{28,4},{29,5},{30,6},{31,7}} | collective-permute-start | bytes 24584 | tf_op jit(solution)/shard_map/ppermute | solution.py:42
  49.8 6.5 %collective-permute-start.18 = (f32[4,512]{1,0:T(4,128)S(1)}, f32[4,512]{1,0:T(4,128)S(1)}, u32[]{:S(2)}, u32[]{:S(2)}) collective-permute-start(f32[4,512]{1,0:T(4,128)S(1)} %fusion.37), channel_id=1, source_target_pairs={{16,0},{17,1},{18,2},{19,3},{20,4},{21,5},{22,6},{23,7},{24,8},{25... | collective-permute-start | bytes 24584 | tf_op jit(solution)/shard_map/ppermute | solution.py:42
  51.1 5.6 %collective-permute-start.17 = (f32[4,512]{1,0:T(4,128)S(1)}, f32[4,512]{1,0:T(4,128)S(1)}, u32[]{:S(2)}, u32[]{:S(2)}) collective-permute-start(f32[4,512]{1,0:T(4,128)S(1)} %fusion.37), channel_id=1, source_target_pairs={{8,0},{9,1},{10,2},{11,3},{12,4},{13,5},{14,6},{15,7},{16,8},{17,9... | collective-permute-start | bytes 24584 | tf_op jit(solution)/shard_map/ppermute | solution.py:42

commit v6 on v5

--- a/solution.py
+++ b/solution.py
@@ -1,6 +1,7 @@
 import jax
 import jax.numpy as jnp
 from jax import lax
+from jax.experimental.layout import Layout, with_layout_constraint
 from jax.sharding import PartitionSpec as P
 
 AXES = ("slab", "row")
@@ -13,6 +14,10 @@
 
 def by(matrix, rows):
     return lax.dot_general(rows, matrix, (((1,), (1,)), ((), ())), precision=HIGH)
+
+
+def rowwise(a):
+    return with_layout_constraint(a, Layout((0, 1)))
 
 
 def in_order(pieces, place):
@@ -77,7 +82,7 @@
         maps, seen = [], []
         for e in range(epochs):
             reach = mm(full[e], maps[-1]) if e else full[e]
-            seen.append(mm(obs_matrix, reach))
+            seen.append(rowwise(mm(obs_matrix, reach)))
             maps.append(reach + mm(taken[e], seen[e]))
         slab_map, shares, next_shares = lax.optimization_barrier((maps[-1], shares, next_shares))
         maps[-1] = slab_map

time: 59.9 us -> 58.9 us (0.983)
  matrix products: 18.3 us -> 17 us
    dot_general x10, matrix products: 9.5 us -> 7.92 us  [mm(): return jnp.dot(a, b, precision=HIGH)]
  transfers between devices with their start and end apart: 20 -> 20, of which waited for: 10 -> 10; matrix products, arithmetic and copies ran while one was open for 30% -> 28% of each run, Pallas kernels for 0% -> 0%
where the time goes in v6:
time: 58.9 us; the launch traced here: 58.6 us
  starting transfers between devices  23.3 us (40%)
  matrix products  17 us (29%)
  waiting for transfers between devices  11.5 us (20%)
  other arithmetic  2.5 us (4%)
  between operations  2.4 us (4%)
  local copies, waits for them, and re-layouts  1.85 us (3%)
    ppermute x20, starting transfers between devices, send(): return lax.ppermute(a, AXES, perm)  23.3 us
    ppermute x20, waiting for transfers between devices, send(): return lax.ppermute(a, AXES, perm)  11.5 us
    dot_general x18, matrix products, by(): lax.dot_general(rows, matrix, (((1,), (1,)), ((), ())), precision=HIGH)  9.1 us
    dot_general x10, matrix products, mm(): return jnp.dot(a, b, precision=HIGH)  7.92 us
  transfers between devices with their start and end apart: 20, of which 10 were waited for; matrix products, arithmetic and copies ran while one was open for 28% of the time, Pallas kernels for 0%

profile of v6, /device:TPU:0, one launch (start us, length us, event | category | flops | bytes accessed | tf_op | source)
XLA Modules:
  0.0 58.6 jit_solution(10080935118394491526)
XLA Ops:
  0.7 3.0 %collective-permute-start = (f32[2,128,512]{2,1,0:T(8,128)}, f32[2,128,512]{2,1,0:T(8,128)S(1)}, u32[]{:S(2)}, u32[]{:S(2)}) collective-permute-start(f32[2,128,512]{2,1,0:T(8,128)} %param.7), channel_id=1, source_target_pairs={{0,2},{1,3},{2,0},{3,1},{4,6},{5,7},{6,4},{7,5},{8,10},{9,11},{10,... | collective-permute-start | bytes 1572872 | tf_op jit(solution)/shard_map/ppermute | solution.py:47
  3.7 1.5 %collective-permute-start.2 = (f32[2,128,512]{2,1,0:T(8,128)}, f32[2,128,512]{2,1,0:T(8,128)S(1)}, u32[]{:S(2)}, u32[]{:S(2)}) collective-permute-start(f32[2,128,512]{2,1,0:T(8,128)} %param.7), channel_id=1, source_target_pairs={{0,1},{1,0},{2,3},{3,2},{4,5},{5,4},{6,7},{7,6},{8,9},{9,8},{10,11... | collective-permute-start | bytes 1572872 | tf_op jit(solution)/shard_map/ppermute | solution.py:47
  5.2 0.7 %convert_element_type.11 = f32[2]{0:T(128)S(1)} convert(s32[2]{0:T(128)} %param.11) | non-fusion elementwise | flops 2 | bytes 16 | tf_op jit(solution)/shard_map/convert_element_type | solution.py:60
  5.8 0.8 %constant_dynamic-slice_fusion = f32[32,512]{1,0:T(8,128)S(1)} fusion(f32[128,512]{1,0:T(8,128)} %param.13, s32[]{:T(128)S(6)} %select_n.230), kind=kLoop, calls=%fused_computation.101 | loop fusion | bytes 131076 | tf_op jit(solution)/shard_map/dynamic_slice | solution.py:65
  6.7 1.2 %convolution_multiply_fusion = f32[2,512]{1,0:T(2,128)S(1)} fusion(f32[2,128]{1,0:T(2,128)} %param.10, f32[512,128]{1,0:T(8,128)} %param.8, f32[2]{0:T(128)S(1)} %convert_element_type.11), kind=kOutput, calls=%fused_computation.10 | convolution fusion | flops 787456 | bytes 267272 | tf_op jit(solution)/shard_map/dot_general | solution.py:16
  7.9 0.6 collective-permute-start.6
  8.5 2.9 %collective-permute-start.4 = (f32[32,512]{1,0:T(8,128)S(1)}, f32[32,512]{1,0:T(8,128)S(1)}, u32[]{:S(2)}, u32[]{:S(2)}) collective-permute-start(f32[32,512]{1,0:T(8,128)S(1)} %constant_dynamic-slice_fusion), channel_id=1, source_target_pairs={{0,3},{1,2},{2,1},{3,0},{4,7},{5,6},{6,5},{7,4},{8,11},{9,10},{10,... | collective-permute-start | bytes 196616 | tf_op jit(solution)/shard_map/ppermute | solution.py:47
  11.4 0.6 fusion.41
  13.3 3.3 %collective-permute-done = f32[2,128,512]{2,1,0:T(8,128)S(1)} collective-permute-done((f32[2,128,512]{2,1,0:T(8,128)}, f32[2,128,512]{2,1,0:T(8,128)S(1)}, u32[]{:S(2)}, u32[]{:S(2)}) %collective-permute-start) | collective-permute-done | bytes 524320 | tf_op jit(solution)/shard_map/ppermute | solution.py:47
  16.5 1.8 %collective-permute-start.1 = (f32[1,128,512]{2,1,0:T(8,128)S(1)}, f32[1,128,512]{2,1,0:T(8,128)S(1)}, u32[]{:S(2)}, u32[]{:S(2)}) collective-permute-start(f32[1,128,512]{2,1,0:T(8,128)S(1)} %slice.67), channel_id=1, source_target_pairs={{0,1},{1,0},{2,3},{3,2},{4,5},{5,4},{6,7},{7,6},{8,9},{9,8},{10,11... | collective-permute-start | bytes 786440 | tf_op jit(solution)/shard_map/ppermute | solution.py:47
  18.8 1.2 %collective-permute-start.3 = (f32[1,128,512]{2,1,0:T(8,128)S(1)}, f32[1,128,512]{2,1,0:T(8,128)S(1)}, u32[]{:S(2)}, u32[]{:S(2)}) collective-permute-start(f32[1,128,512]{2,1,0:T(8,128)S(1)} %slice.68), channel_id=1, source_target_pairs={{0,2},{1,3},{2,0},{3,1},{4,6},{5,7},{6,4},{7,5},{8,10},{9,11},{10,... | collective-permute-start | bytes 786440 | tf_op jit(solution)/shard_map/ppermute | solution.py:47
  20.2 0.9 %collective-permute-done.4 = f32[32,512]{1,0:T(8,128)S(1)} collective-permute-done((f32[32,512]{1,0:T(8,128)S(1)}, f32[32,512]{1,0:T(8,128)S(1)}, u32[]{:S(2)}, u32[]{:S(2)}) %collective-permute-start.4) | collective-permute-done | bytes 65568 | tf_op jit(solution)/shard_map/ppermute | solution.py:47
  21.1 2.0 %collective-permute-start.7 = (f32[4,32,512]{2,1,0:T(8,128)S(1)}, f32[4,32,512]{2,1,0:T(8,128)S(1)}, u32[]{:S(2)}, u32[]{:S(2)}) collective-permute-start(f32[4,32,512]{2,1,0:T(8,128)S(1)} %pad_maximum_fusion.6), channel_id=1, source_target_pairs={{0,8},{1,9},{2,10},{3,11},{4,12},{5,13},{6,14},{7,15},{8,0},{9,1},... | collective-permute-start | bytes 786440 | tf_op jit(solution)/shard_map/ppermute | solution.py:47
  23.1 2.6 %collective-permute-done.1 = f32[1,128,512]{2,1,0:T(8,128)S(1)} collective-permute-done((f32[1,128,512]{2,1,0:T(8,128)S(1)}, f32[1,128,512]{2,1,0:T(8,128)S(1)}, u32[]{:S(2)}, u32[]{:S(2)}) %collective-permute-start.1) | collective-permute-done | bytes 262176 | tf_op jit(solution)/shard_map/ppermute | solution.py:47
  26.3 0.4 convolution_bitcast_fusion.1
  27.0 0.6 %convolution_add_fusion.1 = f32[512,512]{1,0:T(8,128)S(1)} fusion(f32[128,512]{1,0:T(8,128)S(1)} %convolution_bitcast_fusion.1, f32[2,512,512]{2,1,0:T(8,128)S(1)} %pad_maximum_fusion, f32[512,128]{1,0:T(8,128)S(1)} %copy-done.1, f32[]{:T(128)} %bitcast.6), kind=kOutput, calls=%fused_computation.2 | convolution fusion | flops 201654272 | bytes 2621444 | tf_op jit(solution)/shard_map/dot_general | solution.py:12
  27.7 1.0 %fusion.6 = f32[512,512]{1,0:T(8,128)S(1)} fusion(f32[512,512]{1,0:T(8,128)S(1)} %convolution_add_fusion.1, f32[2,512,512]{2,1,0:T(8,128)S(1)} %pad_maximum_fusion), kind=kOutput, calls=%fused_computation.28 | convolution fusion | flops 805306368 | bytes 3145728 | tf_op jit(solution)/shard_map/dot_general | solution.py:12
  29.2 0.6 convolution_add_fusion
  29.8 0.5 fusion.5
  30.8 0.6 collective-permute-start.9
  31.6 0.9 %collective-permute-done.9 = f32[1,512]{1,0:T(1,128)S(1)} collective-permute-done((f32[1,512]{1,0:T(1,128)S(1)}, f32[1,512]{1,0:T(1,128)S(1)}, u32[]{:S(2)}, u32[]{:S(2)}) %collective-permute-start.9) | collective-permute-done | bytes 2080 | tf_op jit(solution)/shard_map/ppermute | solution.py:47
  32.5 0.5 convolution_add_fusion.11
  33.2 1.0 %fusion.2 = f32[512,512]{1,0:T(8,128)S(1)} fusion(f32[512,512]{1,0:T(8,128)S(1)} %collective-permute-done.8, f32[512,512]{1,0:T(8,128)S(1)} %convolution_add_fusion, pred[]{:T(512)S(6)} %eq.19), kind=kOutput, calls=%fused_computation.24 | convolution fusion | flops 805830656 | bytes 3145729 | tf_op jit(solution)/shard_map/dot_general | solution.py:12
  34.3 0.5 convolution_add_fusion.12
  34.8 3.5 %collective-permute-start.11 = (f32[1,512]{1,0:T(1,128)S(1)}, f32[1,512]{1,0:T(1,128)S(1)}, u32[]{:S(2)}, u32[]{:S(2)}) collective-permute-start(f32[1,512]{1,0:T(1,128)S(1)} %convolution_add_fusion.12), channel_id=1, source_target_pairs={{0,8},{1,9},{2,10},{3,11},{4,12},{5,13},{6,14},{7,15}} | collective-permute-start | bytes 6152 | tf_op jit(solution)/shard_map/ppermute | solution.py:47
  38.5 1.0 %fusion.42 = f32[512,512]{1,0:T(8,128)S(1)} fusion(f32[512,512]{1,0:T(8,128)S(1)} %bitcast.130), kind=kOutput, calls=%fused_computation.107 | convolution fusion | flops 805306368 | bytes 2097152 | tf_op jit(solution)/shard_map/dot_general | solution.py:12
  39.8 0.5 convolution_add_fusion.10
  40.3 0.7 %collective-permute-start.13 = (f32[1,512]{1,0:T(1,128)S(1)}, f32[1,512]{1,0:T(1,128)S(1)}, u32[]{:S(2)}, u32[]{:S(2)}) collective-permute-start(f32[1,512]{1,0:T(1,128)S(1)} %convolution_add_fusion.10), channel_id=1, source_target_pairs={{8,16},{9,17},{10,18},{11,19},{12,20},{13,21},{14,22},{15,23}} | collective-permute-start | bytes 6152 | tf_op jit(solution)/shard_map/ppermute | solution.py:47
  41.0 1.0 %fusion.43 = f32[512,512]{1,0:T(8,128)S(1)} fusion(f32[512,512]{1,0:T(8,128)S(1)} %fusion.42), kind=kOutput, calls=%fused_computation.108 | convolution fusion | flops 805306368 | bytes 2097152 | tf_op jit(solution)/shard_map/dot_general | solution.py:12
  42.0 0.7 %convolution_select_fusion = f32[256,512]{1,0:T(8,128)S(1)} fusion(f32[256,512]{1,0:T(8,128)S(1)} %pad_maximum_fusion.5, f32[512,512]{1,0:T(8,128)S(1)} %collective-permute-done.8, pred[]{:T(512)S(6)} %eq.19), kind=kOutput, calls=%fused_computation.3 | convolution fusion | flops 402784256 | bytes 2097153 | tf_op jit(solution)/shard_map/dot_general | solution.py:12
  43.0 0.5 convolution_add_fusion.9
  43.5 0.8 %collective-permute-start.14 = (f32[1,512]{1,0:T(1,128)S(1)}, f32[1,512]{1,0:T(1,128)S(1)}, u32[]{:S(2)}, u32[]{:S(2)}) collective-permute-start(f32[1,512]{1,0:T(1,128)S(1)} %convolution_add_fusion.9), channel_id=1, source_target_pairs={{16,24},{17,25},{18,26},{19,27},{20,28},{21,29},{22,30},{23,31}} | collective-permute-start | bytes 6152 | tf_op jit(solution)/shard_map/ppermute | solution.py:47
  44.5 0.4 collective-permute-start.15
  45.0 1.0 %fusion.44 = f32[512,512]{1,0:T(8,128)S(1)} fusion(f32[512,512]{1,0:T(8,128)S(1)} %fusion.43), kind=kOutput, calls=%fused_computation.109 | convolution fusion | flops 805306368 | bytes 2097152 | tf_op jit(solution)/shard_map/dot_general | solution.py:12
  46.1 0.5 collective-permute-done.15
  46.7 0.5 fusion.21
  47.5 1.3 %collective-permute-start.19 = (f32[4,512]{1,0:T(4,128)S(1)}, f32[4,512]{1,0:T(4,128)S(1)}, u32[]{:S(2)}, u32[]{:S(2)}) collective-permute-start(f32[4,512]{1,0:T(4,128)S(1)} %fusion.32), channel_id=1, source_target_pairs={{24,0},{25,1},{26,2},{27,3},{28,4},{29,5},{30,6},{31,7}} | collective-permute-start | bytes 24584 | tf_op jit(solution)/shard_map/ppermute | solution.py:47
  48.8 1.3 %collective-permute-start.18 = (f32[4,512]{1,0:T(4,128)S(1)}, f32[4,512]{1,0:T(4,128)S(1)}, u32[]{:S(2)}, u32[]{:S(2)}) collective-permute-start(f32[4,512]{1,0:T(4,128)S(1)} %fusion.32), channel_id=1, source_target_pairs={{16,0},{17,1},{18,2},{19,3},{20,4},{21,5},{22,6},{23,7},{24,8},{25... | collective-permute-start | bytes 24584 | tf_op jit(solution)/shard_map/ppermute | solution.py:47
  50.1 1.3 %collective-permute-start.17 = (f32[4,512]{1,0:T(4,128)S(1)}, f32[4,512]{1,0:T(4,128)S(1)}, u32[]{:S(2)}, u32[]{:S(2)}) collective-permute-start(f32[4,512]{1,0:T(4,128)S(1)} %fusion.32), channel_id=1, source_target_pairs={{8,0},{9,1},{10,2},{11,3},{12,4},{13,5},{14,6},{15,7},{16,8},{17,9... | collective-permute-start | bytes 24584 | tf_op jit(solution)/shard_map/ppermute | solution.py:47
  51.4 0.5 fusion.1
  51.9 0.6 convolution_add_fusion.7
  52.5 0.6 convolution_add_fusion.6
  53.0 2.2 %collective-permute-done.19 = f32[4,512]{1,0:T(4,128)S(1)} collective-permute-done((f32[4,512]{1,0:T(4,128)S(1)}, f32[4,512]{1,0:T(4,128)S(1)}, u32[]{:S(2)}, u32[]{:S(2)}) %collective-permute-start.19) | collective-permute-done | bytes 8224 | tf_op jit(solution)/shard_map/ppermute | solution.py:47
  55.7 0.5 convolution_add_fusion.5
  56.3 0.5 convolution_add_fusion.4
  56.8 0.5 convolution_add_fusion.3
  57.4 0.5 convolution_add_fusion.2
  57.9 0.6 %fusion.19 = (f32[2,512]{1,0:T(2,128)}, f32[2,512]{1,0:T(2,128)}) fusion(f32[4,512]{1,0:T(4,128)S(1)} %fusion.32, f32[16,512]{1,0:T(8,128)S(1)} %convolution_add_fusion.2, pred[]{:T(512)S(6)} %eq.19, f32[1,512]{1,0:T(1,128)S(1)} %convolution_add_fusion.6, f32[1,512]{1,0:T(1,128)S(1)} %convolution_add_fusion.7), kind=kLoop, calls=%fused_computation.71 | loop fusion | flops 5120 | bytes 28673 | tf_op jit(solution)/shard_map/sub | solution.py:162
  (64 shorter events, 4.7 us)
Async XLA Ops:
  0.6 25.6 %copy-start = (f32[128,512]{1,0:T(8,128)S(1)}, f32[128,512]{1,0:T(8,128)}, u32[]{:S(2)}) copy-start(f32[128,512]{1,0:T(8,128)} %param.9) | copy-start | bytes 786436
  0.6 25.1 %copy-start.2 = (f32[2,128,512]{2,1,0:T(8,128)S(1)}, f32[2,128,512]{2,1,0:T(8,128)}, u32[]{:S(2)}) copy-start(f32[2,128,512]{2,1,0:T(8,128)} %param.7) | copy-start | bytes 1572868
  0.7 15.9 %collective-permute-start = (f32[2,128,512]{2,1,0:T(8,128)}, f32[2,128,512]{2,1,0:T(8,128)S(1)}, u32[]{:S(2)}, u32[]{:S(2)}) collective-permute-start(f32[2,128,512]{2,1,0:T(8,128)} %param.7), channel_id=1, source_target_pairs={{0,2},{1,3},{2,0},{3,1},{4,6},{5,7},{6,4},{7,5},{8,10},{9,11},{10,... | collective-permute-start | bytes 1572872 | tf_op jit(solution)/shard_map/ppermute | solution.py:47
  3.7 15.1 %collective-permute-start.2 = (f32[2,128,512]{2,1,0:T(8,128)}, f32[2,128,512]{2,1,0:T(8,128)S(1)}, u32[]{:S(2)}, u32[]{:S(2)}) collective-permute-start(f32[2,128,512]{2,1,0:T(8,128)} %param.7), channel_id=1, source_target_pairs={{0,1},{1,0},{2,3},{3,2},{4,5},{5,4},{6,7},{7,6},{8,9},{9,8},{10,11... | collective-permute-start | bytes 1572872 | tf_op jit(solution)/shard_map/ppermute | solution.py:47
  7.9 12.3 %collective-permute-start.6 = (f32[32,512]{1,0:T(8,128)S(1)}, f32[32,512]{1,0:T(8,128)S(1)}, u32[]{:S(2)}, u32[]{:S(2)}) collective-permute-start(f32[32,512]{1,0:T(8,128)S(1)} %constant_dynamic-slice_fusion), channel_id=1, source_target_pairs={{0,1},{1,0},{2,3},{3,2},{4,5},{5,4},{6,7},{7,6},{8,9},{9,8},{10,11... | collective-permute-start | bytes 196616 | tf_op jit(solution)/shard_map/ppermute | solution.py:47
  8.4 11.7 %collective-permute-start.5 = (f32[32,512]{1,0:T(8,128)S(1)}, f32[32,512]{1,0:T(8,128)S(1)}, u32[]{:S(2)}, u32[]{:S(2)}) collective-permute-start(f32[32,512]{1,0:T(8,128)S(1)} %constant_dynamic-slice_fusion), channel_id=1, source_target_pairs={{0,2},{1,3},{2,0},{3,1},{4,6},{5,7},{6,4},{7,5},{8,10},{9,11},{10,... | collective-permute-start | bytes 196616 | tf_op jit(solution)/shard_map/ppermute | solution.py:47
  8.5 12.5 %collective-permute-start.4 = (f32[32,512]{1,0:T(8,128)S(1)}, f32[32,512]{1,0:T(8,128)S(1)}, u32[]{:S(2)}, u32[]{:S(2)}) collective-permute-start(f32[32,512]{1,0:T(8,128)S(1)} %constant_dynamic-slice_fusion), channel_id=1, source_target_pairs={{0,3},{1,2},{2,1},{3,0},{4,7},{5,6},{6,5},{7,4},{8,11},{9,10},{10,... | collective-permute-start | bytes 196616 | tf_op jit(solution)/shard_map/ppermute | solution.py:47
  16.5 9.2 %collective-permute-start.1 = (f32[1,128,512]{2,1,0:T(8,128)S(1)}, f32[1,128,512]{2,1,0:T(8,128)S(1)}, u32[]{:S(2)}, u32[]{:S(2)}) collective-permute-start(f32[1,128,512]{2,1,0:T(8,128)S(1)} %slice.67), channel_id=1, source_target_pairs={{0,1},{1,0},{2,3},{3,2},{4,5},{5,4},{6,7},{7,6},{8,9},{9,8},{10,11... | collective-permute-start | bytes 786440 | tf_op jit(solution)/shard_map/ppermute | solution.py:47
  18.8 6.9 %collective-permute-start.3 = (f32[1,128,512]{2,1,0:T(8,128)S(1)}, f32[1,128,512]{2,1,0:T(8,128)S(1)}, u32[]{:S(2)}, u32[]{:S(2)}) collective-permute-start(f32[1,128,512]{2,1,0:T(8,128)S(1)} %slice.68), channel_id=1, source_target_pairs={{0,2},{1,3},{2,0},{3,1},{4,6},{5,7},{6,4},{7,5},{8,10},{9,11},{10,... | collective-permute-start | bytes 786440 | tf_op jit(solution)/shard_map/ppermute | solution.py:47
  21.1 8.7 %collective-permute-start.7 = (f32[4,32,512]{2,1,0:T(8,128)S(1)}, f32[4,32,512]{2,1,0:T(8,128)S(1)}, u32[]{:S(2)}, u32[]{:S(2)}) collective-permute-start(f32[4,32,512]{2,1,0:T(8,128)S(1)} %pad_maximum_fusion.6), channel_id=1, source_target_pairs={{0,8},{1,9},{2,10},{3,11},{4,12},{5,13},{6,14},{7,15},{8,0},{9,1},... | collective-permute-start | bytes 786440 | tf_op jit(solution)/shard_map/ppermute | solution.py:47
  26.1 1.0 %copy-start.1 = (f32[512,128]{1,0:T(8,128)S(1)}, f32[512,128]{1,0:T(8,128)}, u32[]{:S(2)}) copy-start(f32[512,128]{1,0:T(8,128)} %param.8) | copy-start | bytes 786436
  29.8 3.4 %collective-permute-start.8 = (f32[512,512]{1,0:T(8,128)S(1)}, f32[512,512]{1,0:T(8,128)S(1)}, u32[]{:S(2)}, u32[]{:S(2)}) collective-permute-start(f32[512,512]{1,0:T(8,128)S(1)} %convolution_add_fusion), channel_id=1, source_target_pairs={{0,4},{1,5},{2,6},{3,7},{4,0},{5,1},{6,2},{7,3},{8,12},{9,13},{10,... | collective-permute-start | bytes 3145736 | tf_op jit(solution)/shard_map/ppermute | solution.py:47
  30.8 1.6 %collective-permute-start.9 = (f32[1,512]{1,0:T(1,128)S(1)}, f32[1,512]{1,0:T(1,128)S(1)}, u32[]{:S(2)}, u32[]{:S(2)}) collective-permute-start(f32[1,512]{1,0:T(1,128)S(1)} %slice_add_fusion), channel_id=1, source_target_pairs={{0,4},{1,5},{2,6},{3,7},{4,0},{5,1},{6,2},{7,3},{8,12},{9,13},{10,... | collective-permute-start | bytes 6152 | tf_op jit(solution)/shard_map/ppermute | solution.py:47
  31.5 6.8 %collective-permute-start.12 = (f32[2,4,32,512]{3,2,0,1:T(8,128)S(1)}, f32[2,4,32,512]{3,2,0,1:T(8,128)S(1)}, u32[]{:S(2)}, u32[]{:S(2)}) collective-permute-start(f32[2,4,32,512]{3,2,0,1:T(8,128)S(1)} %pad_maximum_fusion.4), channel_id=1, source_target_pairs={{0,4},{1,5},{2,6},{3,7},{4,0},{5,1},{6,2},{7,3},{8,12},{9,13},{10,... | collective-permute-start | bytes 1572872 | tf_op jit(solution)/shard_map/ppermute | solution.py:47
  33.0 1.2 %copy-start.3 = (f32[512]{0:T(512)S(1)}, f32[512]{0:T(512)}, u32[]{:S(2)}) copy-start(f32[512]{0:T(512)} %param.12) | copy-start | bytes 6148
  33.0 1.2 %collective-permute-start.10 = (f32[1,512]{1,0:T(1,128)S(1)}, f32[1,512]{1,0:T(1,128)S(1)}, u32[]{:S(2)}, u32[]{:S(2)}) collective-permute-start(f32[1,512]{1,0:T(1,128)S(1)} %convolution_add_fusion.11), channel_id=1, source_target_pairs={{0,4},{1,5},{2,6},{3,7},{4,0},{5,1},{6,2},{7,3},{8,12},{9,13},{10,... | collective-permute-start | bytes 6152 | tf_op jit(solution)/shard_map/ppermute | solution.py:47
  34.8 5.0 %collective-permute-start.11 = (f32[1,512]{1,0:T(1,128)S(1)}, f32[1,512]{1,0:T(1,128)S(1)}, u32[]{:S(2)}, u32[]{:S(2)}) collective-permute-start(f32[1,512]{1,0:T(1,128)S(1)} %convolution_add_fusion.12), channel_id=1, source_target_pairs={{0,8},{1,9},{2,10},{3,11},{4,12},{5,13},{6,14},{7,15}} | collective-permute-start | bytes 6152 | tf_op jit(solution)/shard_map/ppermute | solution.py:47
  38.5 1.1 %copy-start.4 = (f32[2,128]{1,0:T(2,128)S(1)}, f32[2,128]{1,0:T(2,128)}, u32[]{:S(2)}) copy-start(f32[2,128]{1,0:T(2,128)} %param.10) | copy-start | bytes 3076
  40.3 2.7 %collective-permute-start.13 = (f32[1,512]{1,0:T(1,128)S(1)}, f32[1,512]{1,0:T(1,128)S(1)}, u32[]{:S(2)}, u32[]{:S(2)}) collective-permute-start(f32[1,512]{1,0:T(1,128)S(1)} %convolution_add_fusion.10), channel_id=1, source_target_pairs={{8,16},{9,17},{10,18},{11,19},{12,20},{13,21},{14,22},{15,23}} | collective-permute-start | bytes 6152 | tf_op jit(solution)/shard_map/ppermute | solution.py:47
  43.5 3.2 %collective-permute-start.14 = (f32[1,512]{1,0:T(1,128)S(1)}, f32[1,512]{1,0:T(1,128)S(1)}, u32[]{:S(2)}, u32[]{:S(2)}) collective-permute-start(f32[1,512]{1,0:T(1,128)S(1)} %convolution_add_fusion.9), channel_id=1, source_target_pairs={{16,24},{17,25},{18,26},{19,27},{20,28},{21,29},{22,30},{23,31}} | collective-permute-start | bytes 6152 | tf_op jit(solution)/shard_map/ppermute | solution.py:47
  44.4 1.6 %collective-permute-start.16 = (f32[2,128]{1,0:T(2,128)S(1)}, f32[2,128]{1,0:T(2,128)S(1)}, u32[]{:S(2)}, u32[]{:S(2)}) collective-permute-start(f32[2,128]{1,0:T(2,128)S(1)} %add_select_fusion), channel_id=1, source_target_pairs={{0,4},{1,5},{2,6},{3,7},{4,0},{5,1},{6,2},{7,3},{8,12},{9,13},{10,... | collective-permute-start | bytes 3080 | tf_op jit(solution)/shard_map/ppermute | solution.py:47
  44.5 2.0 %collective-permute-start.15 = (f32[256,512]{1,0:T(8,128)S(1)}, f32[256,512]{1,0:T(8,128)S(1)}, u32[]{:S(2)}, u32[]{:S(2)}) collective-permute-start(f32[256,512]{1,0:T(8,128)S(1)} %convolution_select_fusion), channel_id=1, source_target_pairs={{0,4},{1,5},{2,6},{3,7},{4,0},{5,1},{6,2},{7,3},{8,12},{9,13},{10,... | collective-permute-start | bytes 1572872 | tf_op jit(solution)/shard_map/ppermute | solution.py:47
  47.5 7.7 %collective-permute-start.19 = (f32[4,512]{1,0:T(4,128)S(1)}, f32[4,512]{1,0:T(4,128)S(1)}, u32[]{:S(2)}, u32[]{:S(2)}) collective-permute-start(f32[4,512]{1,0:T(4,128)S(1)} %fusion.32), channel_id=1, source_target_pairs={{24,0},{25,1},{26,2},{27,3},{28,4},{29,5},{30,6},{31,7}} | collective-permute-start | bytes 24584 | tf_op jit(solution)/shard_map/ppermute | solution.py:47
  48.8 6.6 %collective-permute-start.18 = (f32[4,512]{1,0:T(4,128)S(1)}, f32[4,512]{1,0:T(4,128)S(1)}, u32[]{:S(2)}, u32[]{:S(2)}) collective-permute-start(f32[4,512]{1,0:T(4,128)S(1)} %fusion.32), channel_id=1, source_target_pairs={{16,0},{17,1},{18,2},{19,3},{20,4},{21,5},{22,6},{23,7},{24,8},{25... | collective-permute-start | bytes 24584 | tf_op jit(solution)/shard_map/ppermute | solution.py:47
  50.1 5.6 %collective-permute-start.17 = (f32[4,512]{1,0:T(4,128)S(1)}, f32[4,512]{1,0:T(4,128)S(1)}, u32[]{:S(2)}, u32[]{:S(2)}) collective-permute-start(f32[4,512]{1,0:T(4,128)S(1)} %fusion.32), channel_id=1, source_target_pairs={{8,0},{9,1},{10,2},{11,3},{12,4},{13,5},{14,6},{15,7},{16,8},{17,9... | collective-permute-start | bytes 24584 | tf_op jit(solution)/shard_map/ppermute | solution.py:47

commit v7 on v6

--- a/solution.py
+++ b/solution.py
@@ -59,7 +59,7 @@
 
         weights = present.astype(jnp.float32)
         drive = weights[:, None] * by(gain, observations)
-        taken = [-weights[e] * gain for e in range(epochs)]
+        taken = lax.optimization_barrier([-weights[e] * gain for e in range(epochs)])
 
         share = part_rows // 4
         own_share = lax.dynamic_slice_in_dim(smoother_gain, place % 4 * share, share, 0)
@@ -120,7 +120,7 @@
         def second_work(ahead):
             powers[-1], seen[:] = after((powers[-1], seen), ahead)
             powers.append(mm(powers[-1], powers[-1]))
-            moved = [mm(seen[0], else_map), by(seen[0], else_offset).reshape(seen[1].shape) + seen[1]]
+            moved = [rowwise(mm(seen[0], else_map)), by(seen[0], else_offset).reshape(seen[1].shape) + seen[1]]
             seen[:] = [jnp.where(odd, a, b) for a, b in zip(moved, seen)]
 
         def third_work(ahead):

time: 58.9 us -> 58.9 us (level)
  waiting for transfers between devices: 11.5 us -> 10.4 us
  other arithmetic: 2.5 us -> 3.5 us
    ppermute x20, waiting for transfers between devices: 11.5 us -> 10.4 us  [send(): return lax.ppermute(a, AXES, perm)]
    mul x0 -> x1, other arithmetic: none -> 0.99 us  [on_device(): -weights[e] * gain]
  transfers between devices with their start and end apart: 20 -> 20, of which waited for: 10 -> 10; matrix products, arithmetic and copies ran while one was open for 28% -> 30% of each run, Pallas kernels for 0% -> 0%
where the time goes in v7:
time: 58.9 us; the launch traced here: 58.6 us
  starting transfers between devices  23.3 us (40%)
  matrix products  17 us (29%)
  waiting for transfers between devices  10.4 us (18%)
  other arithmetic  3.5 us (6%)
  between operations  2.45 us (4%)
  local copies, waits for them, and re-layouts  1.91 us (3%)
    ppermute x20, starting transfers between devices, send(): return lax.ppermute(a, AXES, perm)  23.3 us
    ppermute x20, waiting for transfers between devices, send(): return lax.ppermute(a, AXES, perm)  10.4 us
    dot_general x18, matrix products, by(): lax.dot_general(rows, matrix, (((1,), (1,)), ((), ())), precision=HIGH)  9.08 us
    dot_general x10, matrix products, mm(): return jnp.dot(a, b, precision=HIGH)  7.93 us
  transfers between devices with their start and end apart: 20, of which 10 were waited for; matrix products, arithmetic and copies ran while one was open for 30% of the time, Pallas kernels for 0%

profile of v7, /device:TPU:0, one launch (start us, length us, event | category | flops | bytes accessed | tf_op | source)
XLA Modules:
  0.0 58.6 jit_solution(13625447358614065045)
XLA Ops:
  0.6 3.0 %collective-permute-start = (f32[2,128,512]{2,1,0:T(8,128)}, f32[2,128,512]{2,1,0:T(8,128)S(1)}, u32[]{:S(2)}, u32[]{:S(2)}) collective-permute-start(f32[2,128,512]{2,1,0:T(8,128)} %param.7), channel_id=1, source_target_pairs={{0,2},{1,3},{2,0},{3,1},{4,6},{5,7},{6,4},{7,5},{8,10},{9,11},{10,... | collective-permute-start | bytes 1572872 | tf_op jit(solution)/shard_map/ppermute | solution.py:47
  3.7 1.5 %collective-permute-start.2 = (f32[2,128,512]{2,1,0:T(8,128)}, f32[2,128,512]{2,1,0:T(8,128)S(1)}, u32[]{:S(2)}, u32[]{:S(2)}) collective-permute-start(f32[2,128,512]{2,1,0:T(8,128)} %param.7), channel_id=1, source_target_pairs={{0,1},{1,0},{2,3},{3,2},{4,5},{5,4},{6,7},{7,6},{8,9},{9,8},{10,11... | collective-permute-start | bytes 1572872 | tf_op jit(solution)/shard_map/ppermute | solution.py:47
  5.2 0.7 %convert_element_type.11 = f32[2]{0:T(128)S(1)} convert(s32[2]{0:T(128)} %param.11) | non-fusion elementwise | flops 2 | bytes 16 | tf_op jit(solution)/shard_map/convert_element_type | solution.py:60
  5.8 1.2 %convolution_multiply_fusion = f32[2,512]{1,0:T(2,128)S(1)} fusion(f32[2,128]{1,0:T(2,128)} %param.10, f32[512,128]{1,0:T(8,128)} %param.8, f32[2]{0:T(128)S(1)} %convert_element_type.11), kind=kOutput, calls=%fused_computation.10 | convolution fusion | flops 787456 | bytes 267272 | tf_op jit(solution)/shard_map/dot_general | solution.py:16
  7.0 0.9 %constant_dynamic-slice_fusion = f32[32,512]{1,0:T(8,128)S(1)} fusion(f32[128,512]{1,0:T(8,128)} %param.13, s32[]{:T(128)S(6)} %select_n.230), kind=kLoop, calls=%fused_computation.97 | loop fusion | bytes 131076 | tf_op jit(solution)/shard_map/dynamic_slice | solution.py:65
  7.9 0.5 collective-permute-start.6
  8.5 2.9 %collective-permute-start.4 = (f32[32,512]{1,0:T(8,128)S(1)}, f32[32,512]{1,0:T(8,128)S(1)}, u32[]{:S(2)}, u32[]{:S(2)}) collective-permute-start(f32[32,512]{1,0:T(8,128)S(1)} %constant_dynamic-slice_fusion), channel_id=1, source_target_pairs={{0,3},{1,2},{2,1},{3,0},{4,7},{5,6},{6,5},{7,4},{8,11},{9,10},{10,... | collective-permute-start | bytes 196616 | tf_op jit(solution)/shard_map/ppermute | solution.py:47
  11.4 0.6 fusion.35
  13.3 1.0 %broadcast_multiply_fusion.2 = (f32[512,128]{1,0:T(8,128)S(1)}, f32[512,128]{1,0:T(8,128)S(1)}) fusion(f32[512,128]{1,0:T(8,128)} %param.8, f32[]{:T(128)} %bitcast.7, f32[]{:T(128)} %bitcast.6), kind=kLoop, calls=%fused_computation.50 | loop fusion | flops 131072 | bytes 786440 | tf_op jit(solution)/shard_map/mul | solution.py:62
  14.3 2.2 %collective-permute-done = f32[2,128,512]{2,1,0:T(8,128)S(1)} collective-permute-done((f32[2,128,512]{2,1,0:T(8,128)}, f32[2,128,512]{2,1,0:T(8,128)S(1)}, u32[]{:S(2)}, u32[]{:S(2)}) %collective-permute-start) | collective-permute-done | bytes 524320 | tf_op jit(solution)/shard_map/ppermute | solution.py:47
  16.5 1.8 %collective-permute-start.1 = (f32[1,128,512]{2,1,0:T(8,128)S(1)}, f32[1,128,512]{2,1,0:T(8,128)S(1)}, u32[]{:S(2)}, u32[]{:S(2)}) collective-permute-start(f32[1,128,512]{2,1,0:T(8,128)S(1)} %slice.67), channel_id=1, source_target_pairs={{0,1},{1,0},{2,3},{3,2},{4,5},{5,4},{6,7},{7,6},{8,9},{9,8},{10,11... | collective-permute-start | bytes 786440 | tf_op jit(solution)/shard_map/ppermute | solution.py:47
  18.8 1.2 %collective-permute-start.3 = (f32[1,128,512]{2,1,0:T(8,128)S(1)}, f32[1,128,512]{2,1,0:T(8,128)S(1)}, u32[]{:S(2)}, u32[]{:S(2)}) collective-permute-start(f32[1,128,512]{2,1,0:T(8,128)S(1)} %slice.68), channel_id=1, source_target_pairs={{0,2},{1,3},{2,0},{3,1},{4,6},{5,7},{6,4},{7,5},{8,10},{9,11},{10,... | collective-permute-start | bytes 786440 | tf_op jit(solution)/shard_map/ppermute | solution.py:47
  20.1 0.9 %collective-permute-done.4 = f32[32,512]{1,0:T(8,128)S(1)} collective-permute-done((f32[32,512]{1,0:T(8,128)S(1)}, f32[32,512]{1,0:T(8,128)S(1)}, u32[]{:S(2)}, u32[]{:S(2)}) %collective-permute-start.4) | collective-permute-done | bytes 65568 | tf_op jit(solution)/shard_map/ppermute | solution.py:47
  21.1 2.0 %collective-permute-start.7 = (f32[4,32,512]{2,1,0:T(8,128)S(1)}, f32[4,32,512]{2,1,0:T(8,128)S(1)}, u32[]{:S(2)}, u32[]{:S(2)}) collective-permute-start(f32[4,32,512]{2,1,0:T(8,128)S(1)} %pad_maximum_fusion.6), channel_id=1, source_target_pairs={{0,8},{1,9},{2,10},{3,11},{4,12},{5,13},{6,14},{7,15},{8,0},{9,1},... | collective-permute-start | bytes 786440 | tf_op jit(solution)/shard_map/ppermute | solution.py:47
  23.0 2.6 %collective-permute-done.1 = f32[1,128,512]{2,1,0:T(8,128)S(1)} collective-permute-done((f32[1,128,512]{2,1,0:T(8,128)S(1)}, f32[1,128,512]{2,1,0:T(8,128)S(1)}, u32[]{:S(2)}, u32[]{:S(2)}) %collective-permute-start.1) | collective-permute-done | bytes 262176 | tf_op jit(solution)/shard_map/ppermute | solution.py:47
  26.7 0.6 %convolution_add_fusion.1 = f32[512,512]{1,0:T(8,128)S(1)} fusion(f32[512,128]{1,0:T(8,128)S(1)} %get-tuple-element.44, f32[128,512]{1,0:T(8,128)S(1)} %convolution_bitcast_fusion.1, f32[2,512,512]{2,1,0:T(8,128)S(1)} %pad_maximum_fusion), kind=kOutput, calls=%fused_computation.2 | convolution fusion | flops 201588736 | bytes 2621440 | tf_op jit(solution)/shard_map/dot_general | solution.py:12
  27.3 1.0 %fusion.6 = f32[512,512]{1,0:T(8,128)S(1)} fusion(f32[512,512]{1,0:T(8,128)S(1)} %convolution_add_fusion.1, f32[2,512,512]{2,1,0:T(8,128)S(1)} %pad_maximum_fusion), kind=kOutput, calls=%fused_computation.28 | convolution fusion | flops 805306368 | bytes 3145728 | tf_op jit(solution)/shard_map/dot_general | solution.py:12
  28.8 0.6 convolution_add_fusion
  29.5 0.5 fusion.5
  30.5 0.6 collective-permute-start.9
  31.2 0.9 %collective-permute-done.9 = f32[1,512]{1,0:T(1,128)S(1)} collective-permute-done((f32[1,512]{1,0:T(1,128)S(1)}, f32[1,512]{1,0:T(1,128)S(1)}, u32[]{:S(2)}, u32[]{:S(2)}) %collective-permute-start.9) | collective-permute-done | bytes 2080 | tf_op jit(solution)/shard_map/ppermute | solution.py:47
  32.2 0.5 convolution_add_fusion.11
  32.9 1.0 %fusion.2 = f32[512,512]{1,0:T(8,128)S(1)} fusion(f32[512,512]{1,0:T(8,128)S(1)} %collective-permute-done.8, f32[512,512]{1,0:T(8,128)S(1)} %convolution_add_fusion, pred[]{:T(512)S(6)} %eq.19), kind=kOutput, calls=%fused_computation.24 | convolution fusion | flops 805830656 | bytes 3145729 | tf_op jit(solution)/shard_map/dot_general | solution.py:12
  33.9 0.5 convolution_add_fusion.12
  34.5 3.5 %collective-permute-start.11 = (f32[1,512]{1,0:T(1,128)S(1)}, f32[1,512]{1,0:T(1,128)S(1)}, u32[]{:S(2)}, u32[]{:S(2)}) collective-permute-start(f32[1,512]{1,0:T(1,128)S(1)} %convolution_add_fusion.12), channel_id=1, source_target_pairs={{0,8},{1,9},{2,10},{3,11},{4,12},{5,13},{6,14},{7,15}} | collective-permute-start | bytes 6152 | tf_op jit(solution)/shard_map/ppermute | solution.py:47
  38.2 1.0 %fusion.36 = f32[512,512]{1,0:T(8,128)S(1)} fusion(f32[512,512]{1,0:T(8,128)S(1)} %bitcast.133), kind=kOutput, calls=%fused_computation.103 | convolution fusion | flops 805306368 | bytes 2097152 | tf_op jit(solution)/shard_map/dot_general | solution.py:12
  39.4 0.5 convolution_add_fusion.10
  40.0 0.7 %collective-permute-start.13 = (f32[1,512]{1,0:T(1,128)S(1)}, f32[1,512]{1,0:T(1,128)S(1)}, u32[]{:S(2)}, u32[]{:S(2)}) collective-permute-start(f32[1,512]{1,0:T(1,128)S(1)} %convolution_add_fusion.10), channel_id=1, source_target_pairs={{8,16},{9,17},{10,18},{11,19},{12,20},{13,21},{14,22},{15,23}} | collective-permute-start | bytes 6152 | tf_op jit(solution)/shard_map/ppermute | solution.py:47
  40.6 1.0 %fusion.37 = f32[512,512]{1,0:T(8,128)S(1)} fusion(f32[512,512]{1,0:T(8,128)S(1)} %fusion.36), kind=kOutput, calls=%fused_computation.104 | convolution fusion | flops 805306368 | bytes 2097152 | tf_op jit(solution)/shard_map/dot_general | solution.py:12
  41.7 0.7 %convolution_select_fusion = f32[256,512]{1,0:T(8,128)S(1)} fusion(f32[256,512]{1,0:T(8,128)S(1)} %pad_maximum_fusion.5, f32[512,512]{1,0:T(8,128)S(1)} %collective-permute-done.8, pred[]{:T(512)S(6)} %eq.19), kind=kOutput, calls=%fused_computation.3 | convolution fusion | flops 402784256 | bytes 2097153 | tf_op jit(solution)/shard_map/dot_general | solution.py:12
  42.7 0.5 convolution_add_fusion.9
  43.2 0.8 %collective-permute-start.14 = (f32[1,512]{1,0:T(1,128)S(1)}, f32[1,512]{1,0:T(1,128)S(1)}, u32[]{:S(2)}, u32[]{:S(2)}) collective-permute-start(f32[1,512]{1,0:T(1,128)S(1)} %convolution_add_fusion.9), channel_id=1, source_target_pairs={{16,24},{17,25},{18,26},{19,27},{20,28},{21,29},{22,30},{23,31}} | collective-permute-start | bytes 6152 | tf_op jit(solution)/shard_map/ppermute | solution.py:47
  44.6 1.0 %fusion.38 = f32[512,512]{1,0:T(8,128)S(1)} fusion(f32[512,512]{1,0:T(8,128)S(1)} %fusion.37), kind=kOutput, calls=%fused_computation.105 | convolution fusion | flops 805306368 | bytes 2097152 | tf_op jit(solution)/shard_map/dot_general | solution.py:12
  45.7 0.5 collective-permute-done.15
  46.4 0.5 fusion.14
  47.5 1.3 %collective-permute-start.19 = (f32[4,512]{1,0:T(4,128)S(1)}, f32[4,512]{1,0:T(4,128)S(1)}, u32[]{:S(2)}, u32[]{:S(2)}) collective-permute-start(f32[4,512]{1,0:T(4,128)S(1)} %fusion.25), channel_id=1, source_target_pairs={{24,0},{25,1},{26,2},{27,3},{28,4},{29,5},{30,6},{31,7}} | collective-permute-start | bytes 24584 | tf_op jit(solution)/shard_map/ppermute | solution.py:47
  48.8 1.3 %collective-permute-start.18 = (f32[4,512]{1,0:T(4,128)S(1)}, f32[4,512]{1,0:T(4,128)S(1)}, u32[]{:S(2)}, u32[]{:S(2)}) collective-permute-start(f32[4,512]{1,0:T(4,128)S(1)} %fusion.25), channel_id=1, source_target_pairs={{16,0},{17,1},{18,2},{19,3},{20,4},{21,5},{22,6},{23,7},{24,8},{25... | collective-permute-start | bytes 24584 | tf_op jit(solution)/shard_map/ppermute | solution.py:47
  50.1 1.3 %collective-permute-start.17 = (f32[4,512]{1,0:T(4,128)S(1)}, f32[4,512]{1,0:T(4,128)S(1)}, u32[]{:S(2)}, u32[]{:S(2)}) collective-permute-start(f32[4,512]{1,0:T(4,128)S(1)} %fusion.25), channel_id=1, source_target_pairs={{8,0},{9,1},{10,2},{11,3},{12,4},{13,5},{14,6},{15,7},{16,8},{17,9... | collective-permute-start | bytes 24584 | tf_op jit(solution)/shard_map/ppermute | solution.py:47
  51.4 0.5 fusion.1
  51.9 0.6 convolution_add_fusion.7
  52.5 0.6 convolution_add_fusion.6
  53.0 1.9 %collective-permute-done.19 = f32[4,512]{1,0:T(4,128)S(1)} collective-permute-done((f32[4,512]{1,0:T(4,128)S(1)}, f32[4,512]{1,0:T(4,128)S(1)}, u32[]{:S(2)}, u32[]{:S(2)}) %collective-permute-start.19) | collective-permute-done | bytes 8224 | tf_op jit(solution)/shard_map/ppermute | solution.py:47
  54.9 0.5 collective-permute-done.18
  55.7 0.5 convolution_add_fusion.5
  56.3 0.5 convolution_add_fusion.4
  56.8 0.5 convolution_add_fusion.3
  57.4 0.5 convolution_add_fusion.2
  57.9 0.6 %fusion.12 = (f32[2,512]{1,0:T(2,128)}, f32[2,512]{1,0:T(2,128)}) fusion(f32[4,512]{1,0:T(4,128)S(1)} %fusion.25, f32[16,512]{1,0:T(8,128)S(1)} %convolution_add_fusion.2, pred[]{:T(512)S(6)} %eq.19, f32[1,512]{1,0:T(1,128)S(1)} %convolution_add_fusion.6, f32[1,512]{1,0:T(1,128)S(1)} %convolution_add_fusion.7), kind=kLoop, calls=%fused_computation.66 | loop fusion | flops 5120 | bytes 28673 | tf_op jit(solution)/shard_map/sub | solution.py:162
  (65 shorter events, 5.4 us)
Async XLA Ops:
  0.6 25.6 %copy-start = (f32[128,512]{1,0:T(8,128)S(1)}, f32[128,512]{1,0:T(8,128)}, u32[]{:S(2)}) copy-start(f32[128,512]{1,0:T(8,128)} %param.9) | copy-start | bytes 786436
  0.6 15.9 %collective-permute-start = (f32[2,128,512]{2,1,0:T(8,128)}, f32[2,128,512]{2,1,0:T(8,128)S(1)}, u32[]{:S(2)}, u32[]{:S(2)}) collective-permute-start(f32[2,128,512]{2,1,0:T(8,128)} %param.7), channel_id=1, source_target_pairs={{0,2},{1,3},{2,0},{3,1},{4,6},{5,7},{6,4},{7,5},{8,10},{9,11},{10,... | collective-permute-start | bytes 1572872 | tf_op jit(solution)/shard_map/ppermute | solution.py:47
  3.7 15.1 %collective-permute-start.2 = (f32[2,128,512]{2,1,0:T(8,128)}, f32[2,128,512]{2,1,0:T(8,128)S(1)}, u32[]{:S(2)}, u32[]{:S(2)}) collective-permute-start(f32[2,128,512]{2,1,0:T(8,128)} %param.7), channel_id=1, source_target_pairs={{0,1},{1,0},{2,3},{3,2},{4,5},{5,4},{6,7},{7,6},{8,9},{9,8},{10,11... | collective-permute-start | bytes 1572872 | tf_op jit(solution)/shard_map/ppermute | solution.py:47
  7.0 18.7 %copy-start.2 = (f32[2,128,512]{2,1,0:T(8,128)S(1)}, f32[2,128,512]{2,1,0:T(8,128)}, u32[]{:S(2)}) copy-start(f32[2,128,512]{2,1,0:T(8,128)} %param.7) | copy-start | bytes 1572868
  7.9 12.2 %collective-permute-start.6 = (f32[32,512]{1,0:T(8,128)S(1)}, f32[32,512]{1,0:T(8,128)S(1)}, u32[]{:S(2)}, u32[]{:S(2)}) collective-permute-start(f32[32,512]{1,0:T(8,128)S(1)} %constant_dynamic-slice_fusion), channel_id=1, source_target_pairs={{0,1},{1,0},{2,3},{3,2},{4,5},{5,4},{6,7},{7,6},{8,9},{9,8},{10,11... | collective-permute-start | bytes 196616 | tf_op jit(solution)/shard_map/ppermute | solution.py:47
  8.5 11.7 %collective-permute-start.5 = (f32[32,512]{1,0:T(8,128)S(1)}, f32[32,512]{1,0:T(8,128)S(1)}, u32[]{:S(2)}, u32[]{:S(2)}) collective-permute-start(f32[32,512]{1,0:T(8,128)S(1)} %constant_dynamic-slice_fusion), channel_id=1, source_target_pairs={{0,2},{1,3},{2,0},{3,1},{4,6},{5,7},{6,4},{7,5},{8,10},{9,11},{10,... | collective-permute-start | bytes 196616 | tf_op jit(solution)/shard_map/ppermute | solution.py:47
  8.5 12.5 %collective-permute-start.4 = (f32[32,512]{1,0:T(8,128)S(1)}, f32[32,512]{1,0:T(8,128)S(1)}, u32[]{:S(2)}, u32[]{:S(2)}) collective-permute-start(f32[32,512]{1,0:T(8,128)S(1)} %constant_dynamic-slice_fusion), channel_id=1, source_target_pairs={{0,3},{1,2},{2,1},{3,0},{4,7},{5,6},{6,5},{7,4},{8,11},{9,10},{10,... | collective-permute-start | bytes 196616 | tf_op jit(solution)/shard_map/ppermute | solution.py:47
  16.5 9.2 %collective-permute-start.1 = (f32[1,128,512]{2,1,0:T(8,128)S(1)}, f32[1,128,512]{2,1,0:T(8,128)S(1)}, u32[]{:S(2)}, u32[]{:S(2)}) collective-permute-start(f32[1,128,512]{2,1,0:T(8,128)S(1)} %slice.67), channel_id=1, source_target_pairs={{0,1},{1,0},{2,3},{3,2},{4,5},{5,4},{6,7},{7,6},{8,9},{9,8},{10,11... | collective-permute-start | bytes 786440 | tf_op jit(solution)/shard_map/ppermute | solution.py:47
  18.8 6.9 %collective-permute-start.3 = (f32[1,128,512]{2,1,0:T(8,128)S(1)}, f32[1,128,512]{2,1,0:T(8,128)S(1)}, u32[]{:S(2)}, u32[]{:S(2)}) collective-permute-start(f32[1,128,512]{2,1,0:T(8,128)S(1)} %slice.68), channel_id=1, source_target_pairs={{0,2},{1,3},{2,0},{3,1},{4,6},{5,7},{6,4},{7,5},{8,10},{9,11},{10,... | collective-permute-start | bytes 786440 | tf_op jit(solution)/shard_map/ppermute | solution.py:47
  21.1 8.3 %collective-permute-start.7 = (f32[4,32,512]{2,1,0:T(8,128)S(1)}, f32[4,32,512]{2,1,0:T(8,128)S(1)}, u32[]{:S(2)}, u32[]{:S(2)}) collective-permute-start(f32[4,32,512]{2,1,0:T(8,128)S(1)} %pad_maximum_fusion.6), channel_id=1, source_target_pairs={{0,8},{1,9},{2,10},{3,11},{4,12},{5,13},{6,14},{7,15},{8,0},{9,1},... | collective-permute-start | bytes 786440 | tf_op jit(solution)/shard_map/ppermute | solution.py:47
  29.4 3.4 %collective-permute-start.8 = (f32[512,512]{1,0:T(8,128)S(1)}, f32[512,512]{1,0:T(8,128)S(1)}, u32[]{:S(2)}, u32[]{:S(2)}) collective-permute-start(f32[512,512]{1,0:T(8,128)S(1)} %convolution_add_fusion), channel_id=1, source_target_pairs={{0,4},{1,5},{2,6},{3,7},{4,0},{5,1},{6,2},{7,3},{8,12},{9,13},{10,... | collective-permute-start | bytes 3145736 | tf_op jit(solution)/shard_map/ppermute | solution.py:47
  30.5 1.6 %collective-permute-start.9 = (f32[1,512]{1,0:T(1,128)S(1)}, f32[1,512]{1,0:T(1,128)S(1)}, u32[]{:S(2)}, u32[]{:S(2)}) collective-permute-start(f32[1,512]{1,0:T(1,128)S(1)} %slice_add_fusion), channel_id=1, source_target_pairs={{0,4},{1,5},{2,6},{3,7},{4,0},{5,1},{6,2},{7,3},{8,12},{9,13},{10,... | collective-permute-start | bytes 6152 | tf_op jit(solution)/shard_map/ppermute | solution.py:47
  31.2 6.8 %collective-permute-start.12 = (f32[2,4,32,512]{3,2,0,1:T(8,128)S(1)}, f32[2,4,32,512]{3,2,0,1:T(8,128)S(1)}, u32[]{:S(2)}, u32[]{:S(2)}) collective-permute-start(f32[2,4,32,512]{3,2,0,1:T(8,128)S(1)} %pad_maximum_fusion.4), channel_id=1, source_target_pairs={{0,4},{1,5},{2,6},{3,7},{4,0},{5,1},{6,2},{7,3},{8,12},{9,13},{10,... | collective-permute-start | bytes 1572872 | tf_op jit(solution)/shard_map/ppermute | solution.py:47
  32.7 1.2 %copy-start.3 = (f32[512]{0:T(512)S(1)}, f32[512]{0:T(512)}, u32[]{:S(2)}) copy-start(f32[512]{0:T(512)} %param.12) | copy-start | bytes 6148
  32.7 1.2 %collective-permute-start.10 = (f32[1,512]{1,0:T(1,128)S(1)}, f32[1,512]{1,0:T(1,128)S(1)}, u32[]{:S(2)}, u32[]{:S(2)}) collective-permute-start(f32[1,512]{1,0:T(1,128)S(1)} %convolution_add_fusion.11), channel_id=1, source_target_pairs={{0,4},{1,5},{2,6},{3,7},{4,0},{5,1},{6,2},{7,3},{8,12},{9,13},{10,... | collective-permute-start | bytes 6152 | tf_op jit(solution)/shard_map/ppermute | solution.py:47
  34.5 5.0 %collective-permute-start.11 = (f32[1,512]{1,0:T(1,128)S(1)}, f32[1,512]{1,0:T(1,128)S(1)}, u32[]{:S(2)}, u32[]{:S(2)}) collective-permute-start(f32[1,512]{1,0:T(1,128)S(1)} %convolution_add_fusion.12), channel_id=1, source_target_pairs={{0,8},{1,9},{2,10},{3,11},{4,12},{5,13},{6,14},{7,15}} | collective-permute-start | bytes 6152 | tf_op jit(solution)/shard_map/ppermute | solution.py:47
  38.2 1.1 %copy-start.4 = (f32[2,128]{1,0:T(2,128)S(1)}, f32[2,128]{1,0:T(2,128)}, u32[]{:S(2)}) copy-start(f32[2,128]{1,0:T(2,128)} %param.10) | copy-start | bytes 3076
  40.0 2.7 %collective-permute-start.13 = (f32[1,512]{1,0:T(1,128)S(1)}, f32[1,512]{1,0:T(1,128)S(1)}, u32[]{:S(2)}, u32[]{:S(2)}) collective-permute-start(f32[1,512]{1,0:T(1,128)S(1)} %convolution_add_fusion.10), channel_id=1, source_target_pairs={{8,16},{9,17},{10,18},{11,19},{12,20},{13,21},{14,22},{15,23}} | collective-permute-start | bytes 6152 | tf_op jit(solution)/shard_map/ppermute | solution.py:47
  43.2 3.2 %collective-permute-start.14 = (f32[1,512]{1,0:T(1,128)S(1)}, f32[1,512]{1,0:T(1,128)S(1)}, u32[]{:S(2)}, u32[]{:S(2)}) collective-permute-start(f32[1,512]{1,0:T(1,128)S(1)} %convolution_add_fusion.9), channel_id=1, source_target_pairs={{16,24},{17,25},{18,26},{19,27},{20,28},{21,29},{22,30},{23,31}} | collective-permute-start | bytes 6152 | tf_op jit(solution)/shard_map/ppermute | solution.py:47
  44.1 1.6 %collective-permute-start.16 = (f32[2,128]{1,0:T(2,128)S(1)}, f32[2,128]{1,0:T(2,128)S(1)}, u32[]{:S(2)}, u32[]{:S(2)}) collective-permute-start(f32[2,128]{1,0:T(2,128)S(1)} %add_select_fusion), channel_id=1, source_target_pairs={{0,4},{1,5},{2,6},{3,7},{4,0},{5,1},{6,2},{7,3},{8,12},{9,13},{10,... | collective-permute-start | bytes 3080 | tf_op jit(solution)/shard_map/ppermute | solution.py:47
  44.2 2.0 %collective-permute-start.15 = (f32[256,512]{1,0:T(8,128)S(1)}, f32[256,512]{1,0:T(8,128)S(1)}, u32[]{:S(2)}, u32[]{:S(2)}) collective-permute-start(f32[256,512]{1,0:T(8,128)S(1)} %convolution_select_fusion), channel_id=1, source_target_pairs={{0,4},{1,5},{2,6},{3,7},{4,0},{5,1},{6,2},{7,3},{8,12},{9,13},{10,... | collective-permute-start | bytes 1572872 | tf_op jit(solution)/shard_map/ppermute | solution.py:47
  46.3 1.0 %copy-start.1 = (f32[512,128]{1,0:T(8,128)S(1)}, f32[512,128]{1,0:T(8,128)}, u32[]{:S(2)}) copy-start(f32[512,128]{1,0:T(8,128)} %param.8) | copy-start | bytes 786436
  47.5 7.4 %collective-permute-start.19 = (f32[4,512]{1,0:T(4,128)S(1)}, f32[4,512]{1,0:T(4,128)S(1)}, u32[]{:S(2)}, u32[]{:S(2)}) collective-permute-start(f32[4,512]{1,0:T(4,128)S(1)} %fusion.25), channel_id=1, source_target_pairs={{24,0},{25,1},{26,2},{27,3},{28,4},{29,5},{30,6},{31,7}} | collective-permute-start | bytes 24584 | tf_op jit(solution)/shard_map/ppermute | solution.py:47
  48.8 6.6 %collective-permute-start.18 = (f32[4,512]{1,0:T(4,128)S(1)}, f32[4,512]{1,0:T(4,128)S(1)}, u32[]{:S(2)}, u32[]{:S(2)}) collective-permute-start(f32[4,512]{1,0:T(4,128)S(1)} %fusion.25), channel_id=1, source_target_pairs={{16,0},{17,1},{18,2},{19,3},{20,4},{21,5},{22,6},{23,7},{24,8},{25... | collective-permute-start | bytes 24584 | tf_op jit(solution)/shard_map/ppermute | solution.py:47
  50.1 5.6 %collective-permute-start.17 = (f32[4,512]{1,0:T(4,128)S(1)}, f32[4,512]{1,0:T(4,128)S(1)}, u32[]{:S(2)}, u32[]{:S(2)}) collective-permute-start(f32[4,512]{1,0:T(4,128)S(1)} %fusion.25), channel_id=1, source_target_pairs={{8,0},{9,1},{10,2},{11,3},{12,4},{13,5},{14,6},{15,7},{16,8},{17,9... | collective-permute-start | bytes 24584 | tf_op jit(solution)/shard_map/ppermute | solution.py:47

commit v8 on v7

--- a/solution.py
+++ b/solution.py
@@ -122,11 +122,12 @@
             powers.append(mm(powers[-1], powers[-1]))
             moved = [rowwise(mm(seen[0], else_map)), by(seen[0], else_offset).reshape(seen[1].shape) + seen[1]]
             seen[:] = [jnp.where(odd, a, b) for a, b in zip(moved, seen)]
+            seen.extend([other_core(a) for a in seen])
 
         def third_work(ahead):
             powers[-1], seen[:] = after((powers[-1], seen), ahead)
             seen[:] = [
-                lax.concatenate(in_order([a, other_core(a)], place % 2), 0) for a in seen
+                lax.concatenate(in_order(list(a), place % 2), 0) for a in zip(seen[:2], seen[2:])
             ]
             while 2 ** len(powers) < count:
                 powers.append(mm(powers[-1], powers[-1]))

time: 58.9 us -> 58.5 us (level)
  transfers between devices with their start and end apart: 20 -> 20, of which waited for: 10 -> 8; matrix products, arithmetic and copies ran while one was open for 30% -> 30% of each run, Pallas kernels for 0% -> 0%
where the time goes in v8:
time: 58.5 us; the launch traced here: 58.1 us
  starting transfers between devices  23.3 us (40%)
  matrix products  17 us (29%)
  waiting for transfers between devices  9.96 us (17%)
  other arithmetic  3.5 us (6%)
  between operations  2.46 us (4%)
  local copies, waits for them, and re-layouts  1.89 us (3%)
    ppermute x20, starting transfers between devices, send(): return lax.ppermute(a, AXES, perm)  23.3 us
    ppermute x20, waiting for transfers between devices, send(): return lax.ppermute(a, AXES, perm)  9.96 us
    dot_general x18, matrix products, by(): lax.dot_general(rows, matrix, (((1,), (1,)), ((), ())), precision=HIGH)  9.08 us
    dot_general x10, matrix products, mm(): return jnp.dot(a, b, precision=HIGH)  7.94 us
  transfers between devices with their start and end apart: 20, of which 8 were waited for; matrix products, arithmetic and copies ran while one was open for 30% of the time, Pallas kernels for 0%

profile of v8, /device:TPU:0, one launch (start us, length us, event | category | flops | bytes accessed | tf_op | source)
XLA Modules:
  0.0 58.1 jit_solution(4543446997279638928)
XLA Ops:
  0.6 3.0 %collective-permute-start = (f32[2,128,512]{2,1,0:T(8,128)}, f32[2,128,512]{2,1,0:T(8,128)S(1)}, u32[]{:S(2)}, u32[]{:S(2)}) collective-permute-start(f32[2,128,512]{2,1,0:T(8,128)} %param.7), channel_id=1, source_target_pairs={{0,2},{1,3},{2,0},{3,1},{4,6},{5,7},{6,4},{7,5},{8,10},{9,11},{10,... | collective-permute-start | bytes 1572872 | tf_op jit(solution)/shard_map/ppermute | solution.py:47
  3.7 1.5 %collective-permute-start.2 = (f32[2,128,512]{2,1,0:T(8,128)}, f32[2,128,512]{2,1,0:T(8,128)S(1)}, u32[]{:S(2)}, u32[]{:S(2)}) collective-permute-start(f32[2,128,512]{2,1,0:T(8,128)} %param.7), channel_id=1, source_target_pairs={{0,1},{1,0},{2,3},{3,2},{4,5},{5,4},{6,7},{7,6},{8,9},{9,8},{10,11... | collective-permute-start | bytes 1572872 | tf_op jit(solution)/shard_map/ppermute | solution.py:47
  5.2 0.7 %convert_element_type.11 = f32[2]{0:T(128)S(1)} convert(s32[2]{0:T(128)} %param.11) | non-fusion elementwise | flops 2 | bytes 16 | tf_op jit(solution)/shard_map/convert_element_type | solution.py:60
  5.8 1.2 %convolution_multiply_fusion = f32[2,512]{1,0:T(2,128)S(1)} fusion(f32[2,128]{1,0:T(2,128)} %param.10, f32[512,128]{1,0:T(8,128)} %param.8, f32[2]{0:T(128)S(1)} %convert_element_type.11), kind=kOutput, calls=%fused_computation.10 | convolution fusion | flops 787456 | bytes 267272 | tf_op jit(solution)/shard_map/dot_general | solution.py:16
  7.0 0.9 %constant_dynamic-slice_fusion = f32[32,512]{1,0:T(8,128)S(1)} fusion(f32[128,512]{1,0:T(8,128)} %param.13, s32[]{:T(128)S(6)} %select_n.230), kind=kLoop, calls=%fused_computation.97 | loop fusion | bytes 131076 | tf_op jit(solution)/shard_map/dynamic_slice | solution.py:65
  7.9 0.5 collective-permute-start.6
  8.5 2.9 %collective-permute-start.4 = (f32[32,512]{1,0:T(8,128)S(1)}, f32[32,512]{1,0:T(8,128)S(1)}, u32[]{:S(2)}, u32[]{:S(2)}) collective-permute-start(f32[32,512]{1,0:T(8,128)S(1)} %constant_dynamic-slice_fusion), channel_id=1, source_target_pairs={{0,3},{1,2},{2,1},{3,0},{4,7},{5,6},{6,5},{7,4},{8,11},{9,10},{10,... | collective-permute-start | bytes 196616 | tf_op jit(solution)/shard_map/ppermute | solution.py:47
  11.4 0.6 %fusion.35 = (f32[1]{0:T(128)}, f32[1]{0:T(128)}) fusion(f32[2]{0:T(128)S(1)} %convert_element_type.11), kind=kLoop, calls=%fused_computation.102 | loop fusion | bytes 16 | tf_op jit(solution)/shard_map/slice | solution.py:62
  13.3 1.0 %broadcast_multiply_fusion.2 = (f32[512,128]{1,0:T(8,128)S(1)}, f32[512,128]{1,0:T(8,128)S(1)}) fusion(f32[512,128]{1,0:T(8,128)} %param.8, f32[]{:T(128)} %bitcast.7, f32[]{:T(128)} %bitcast.6), kind=kLoop, calls=%fused_computation.50 | loop fusion | flops 131072 | bytes 786440 | tf_op jit(solution)/shard_map/mul | solution.py:62
  14.3 2.2 %collective-permute-done = f32[2,128,512]{2,1,0:T(8,128)S(1)} collective-permute-done((f32[2,128,512]{2,1,0:T(8,128)}, f32[2,128,512]{2,1,0:T(8,128)S(1)}, u32[]{:S(2)}, u32[]{:S(2)}) %collective-permute-start) | collective-permute-done | bytes 524320 | tf_op jit(solution)/shard_map/ppermute | solution.py:47
  16.5 1.8 %collective-permute-start.1 = (f32[1,128,512]{2,1,0:T(8,128)S(1)}, f32[1,128,512]{2,1,0:T(8,128)S(1)}, u32[]{:S(2)}, u32[]{:S(2)}) collective-permute-start(f32[1,128,512]{2,1,0:T(8,128)S(1)} %slice.67), channel_id=1, source_target_pairs={{0,1},{1,0},{2,3},{3,2},{4,5},{5,4},{6,7},{7,6},{8,9},{9,8},{10,11... | collective-permute-start | bytes 786440 | tf_op jit(solution)/shard_map/ppermute | solution.py:47
  18.8 1.2 %collective-permute-start.3 = (f32[1,128,512]{2,1,0:T(8,128)S(1)}, f32[1,128,512]{2,1,0:T(8,128)S(1)}, u32[]{:S(2)}, u32[]{:S(2)}) collective-permute-start(f32[1,128,512]{2,1,0:T(8,128)S(1)} %slice.68), channel_id=1, source_target_pairs={{0,2},{1,3},{2,0},{3,1},{4,6},{5,7},{6,4},{7,5},{8,10},{9,11},{10,... | collective-permute-start | bytes 786440 | tf_op jit(solution)/shard_map/ppermute | solution.py:47
  20.1 0.9 %collective-permute-done.4 = f32[32,512]{1,0:T(8,128)S(1)} collective-permute-done((f32[32,512]{1,0:T(8,128)S(1)}, f32[32,512]{1,0:T(8,128)S(1)}, u32[]{:S(2)}, u32[]{:S(2)}) %collective-permute-start.4) | collective-permute-done | bytes 65568 | tf_op jit(solution)/shard_map/ppermute | solution.py:47
  21.1 2.0 %collective-permute-start.7 = (f32[4,32,512]{2,1,0:T(8,128)S(1)}, f32[4,32,512]{2,1,0:T(8,128)S(1)}, u32[]{:S(2)}, u32[]{:S(2)}) collective-permute-start(f32[4,32,512]{2,1,0:T(8,128)S(1)} %pad_maximum_fusion.6), channel_id=1, source_target_pairs={{0,8},{1,9},{2,10},{3,11},{4,12},{5,13},{6,14},{7,15},{8,0},{9,1},... | collective-permute-start | bytes 786440 | tf_op jit(solution)/shard_map/ppermute | solution.py:47
  23.0 2.6 %collective-permute-done.1 = f32[1,128,512]{2,1,0:T(8,128)S(1)} collective-permute-done((f32[1,128,512]{2,1,0:T(8,128)S(1)}, f32[1,128,512]{2,1,0:T(8,128)S(1)}, u32[]{:S(2)}, u32[]{:S(2)}) %collective-permute-start.1) | collective-permute-done | bytes 262176 | tf_op jit(solution)/shard_map/ppermute | solution.py:47
  26.2 0.4 convolution_bitcast_fusion.1
  26.7 0.6 %convolution_add_fusion.1 = f32[512,512]{1,0:T(8,128)S(1)} fusion(f32[512,128]{1,0:T(8,128)S(1)} %get-tuple-element.48, f32[128,512]{1,0:T(8,128)S(1)} %convolution_bitcast_fusion.1, f32[2,512,512]{2,1,0:T(8,128)S(1)} %pad_maximum_fusion), kind=kOutput, calls=%fused_computation.2 | convolution fusion | flops 201588736 | bytes 2621440 | tf_op jit(solution)/shard_map/dot_general | solution.py:12
  27.3 1.0 %fusion.6 = f32[512,512]{1,0:T(8,128)S(1)} fusion(f32[512,512]{1,0:T(8,128)S(1)} %convolution_add_fusion.1, f32[2,512,512]{2,1,0:T(8,128)S(1)} %pad_maximum_fusion), kind=kOutput, calls=%fused_computation.28 | convolution fusion | flops 805306368 | bytes 3145728 | tf_op jit(solution)/shard_map/dot_general | solution.py:12
  28.8 0.6 convolution_add_fusion
  29.5 0.5 fusion.5
  30.5 0.6 collective-permute-start.9
  31.2 0.9 %collective-permute-done.9 = f32[1,512]{1,0:T(1,128)S(1)} collective-permute-done((f32[1,512]{1,0:T(1,128)S(1)}, f32[1,512]{1,0:T(1,128)S(1)}, u32[]{:S(2)}, u32[]{:S(2)}) %collective-permute-start.9) | collective-permute-done | bytes 2080 | tf_op jit(solution)/shard_map/ppermute | solution.py:47
  32.2 0.5 convolution_add_fusion.11
  32.9 1.0 %fusion.2 = f32[512,512]{1,0:T(8,128)S(1)} fusion(f32[512,512]{1,0:T(8,128)S(1)} %collective-permute-done.8, f32[512,512]{1,0:T(8,128)S(1)} %convolution_add_fusion, pred[]{:T(512)S(6)} %eq.19), kind=kOutput, calls=%fused_computation.24 | convolution fusion | flops 805830656 | bytes 3145729 | tf_op jit(solution)/shard_map/dot_general | solution.py:12
  33.9 0.5 convolution_add_fusion.12
  34.5 3.5 %collective-permute-start.11 = (f32[1,512]{1,0:T(1,128)S(1)}, f32[1,512]{1,0:T(1,128)S(1)}, u32[]{:S(2)}, u32[]{:S(2)}) collective-permute-start(f32[1,512]{1,0:T(1,128)S(1)} %convolution_add_fusion.12), channel_id=1, source_target_pairs={{0,8},{1,9},{2,10},{3,11},{4,12},{5,13},{6,14},{7,15}} | collective-permute-start | bytes 6152 | tf_op jit(solution)/shard_map/ppermute | solution.py:47
  38.2 1.0 %fusion.36 = f32[512,512]{1,0:T(8,128)S(1)} fusion(f32[512,512]{1,0:T(8,128)S(1)} %bitcast.133), kind=kOutput, calls=%fused_computation.103 | convolution fusion | flops 805306368 | bytes 2097152 | tf_op jit(solution)/shard_map/dot_general | solution.py:12
  39.4 0.5 convolution_add_fusion.10
  40.0 0.7 %collective-permute-start.13 = (f32[1,512]{1,0:T(1,128)S(1)}, f32[1,512]{1,0:T(1,128)S(1)}, u32[]{:S(2)}, u32[]{:S(2)}) collective-permute-start(f32[1,512]{1,0:T(1,128)S(1)} %convolution_add_fusion.10), channel_id=1, source_target_pairs={{8,16},{9,17},{10,18},{11,19},{12,20},{13,21},{14,22},{15,23}} | collective-permute-start | bytes 6152 | tf_op jit(solution)/shard_map/ppermute | solution.py:47
  40.6 0.7 %convolution_select_fusion = f32[256,512]{1,0:T(8,128)S(1)} fusion(f32[256,512]{1,0:T(8,128)S(1)} %pad_maximum_fusion.5, f32[512,512]{1,0:T(8,128)S(1)} %collective-permute-done.8, pred[]{:T(512)S(6)} %eq.19), kind=kOutput, calls=%fused_computation.3 | convolution fusion | flops 402784256 | bytes 2097153 | tf_op jit(solution)/shard_map/dot_general | solution.py:12
  41.8 0.5 collective-permute-start.15
  42.3 1.0 %fusion.37 = f32[512,512]{1,0:T(8,128)S(1)} fusion(f32[512,512]{1,0:T(8,128)S(1)} %fusion.36), kind=kOutput, calls=%fused_computation.104 | convolution fusion | flops 805306368 | bytes 2097152 | tf_op jit(solution)/shard_map/dot_general | solution.py:12
  43.4 0.5 convolution_add_fusion.9
  43.9 0.8 %collective-permute-start.16 = (f32[1,512]{1,0:T(1,128)S(1)}, f32[1,512]{1,0:T(1,128)S(1)}, u32[]{:S(2)}, u32[]{:S(2)}) collective-permute-start(f32[1,512]{1,0:T(1,128)S(1)} %convolution_add_fusion.9), channel_id=1, source_target_pairs={{16,24},{17,25},{18,26},{19,27},{20,28},{21,29},{22,30},{23,31}} | collective-permute-start | bytes 6152 | tf_op jit(solution)/shard_map/ppermute | solution.py:47
  44.7 1.0 %fusion.38 = f32[512,512]{1,0:T(8,128)S(1)} fusion(f32[512,512]{1,0:T(8,128)S(1)} %fusion.37), kind=kOutput, calls=%fused_computation.105 | convolution fusion | flops 805306368 | bytes 2097152 | tf_op jit(solution)/shard_map/dot_general | solution.py:12
  46.1 0.5 fusion.14
  47.1 1.3 %collective-permute-start.19 = (f32[4,512]{1,0:T(4,128)S(1)}, f32[4,512]{1,0:T(4,128)S(1)}, u32[]{:S(2)}, u32[]{:S(2)}) collective-permute-start(f32[4,512]{1,0:T(4,128)S(1)} %fusion.25), channel_id=1, source_target_pairs={{24,0},{25,1},{26,2},{27,3},{28,4},{29,5},{30,6},{31,7}} | collective-permute-start | bytes 24584 | tf_op jit(solution)/shard_map/ppermute | solution.py:47
  48.4 1.3 %collective-permute-start.18 = (f32[4,512]{1,0:T(4,128)S(1)}, f32[4,512]{1,0:T(4,128)S(1)}, u32[]{:S(2)}, u32[]{:S(2)}) collective-permute-start(f32[4,512]{1,0:T(4,128)S(1)} %fusion.25), channel_id=1, source_target_pairs={{16,0},{17,1},{18,2},{19,3},{20,4},{21,5},{22,6},{23,7},{24,8},{25... | collective-permute-start | bytes 24584 | tf_op jit(solution)/shard_map/ppermute | solution.py:47
  49.7 1.3 %collective-permute-start.17 = (f32[4,512]{1,0:T(4,128)S(1)}, f32[4,512]{1,0:T(4,128)S(1)}, u32[]{:S(2)}, u32[]{:S(2)}) collective-permute-start(f32[4,512]{1,0:T(4,128)S(1)} %fusion.25), channel_id=1, source_target_pairs={{8,0},{9,1},{10,2},{11,3},{12,4},{13,5},{14,6},{15,7},{16,8},{17,9... | collective-permute-start | bytes 24584 | tf_op jit(solution)/shard_map/ppermute | solution.py:47
  51.0 0.5 fusion.1
  51.5 0.6 convolution_add_fusion.7
  52.1 0.6 convolution_add_fusion.6
  52.6 2.3 %collective-permute-done.19 = f32[4,512]{1,0:T(4,128)S(1)} collective-permute-done((f32[4,512]{1,0:T(4,128)S(1)}, f32[4,512]{1,0:T(4,128)S(1)}, u32[]{:S(2)}, u32[]{:S(2)}) %collective-permute-start.19) | collective-permute-done | bytes 8224 | tf_op jit(solution)/shard_map/ppermute | solution.py:47
  55.3 0.5 convolution_add_fusion.5
  55.9 0.5 convolution_add_fusion.4
  56.4 0.5 convolution_add_fusion.3
  57.0 0.5 convolution_add_fusion.2
  57.5 0.6 %fusion.12 = (f32[2,512]{1,0:T(2,128)}, f32[2,512]{1,0:T(2,128)}) fusion(f32[4,512]{1,0:T(4,128)S(1)} %fusion.25, f32[16,512]{1,0:T(8,128)S(1)} %convolution_add_fusion.2, pred[]{:T(512)S(6)} %eq.19, f32[1,512]{1,0:T(1,128)S(1)} %convolution_add_fusion.6, f32[1,512]{1,0:T(1,128)S(1)} %convolution_add_fusion.7), kind=kLoop, calls=%fused_computation.66 | loop fusion | flops 5120 | bytes 28673 | tf_op jit(solution)/shard_map/sub | solution.py:163
  (65 shorter events, 4.6 us)
Async XLA Ops:
  0.6 25.6 %copy-start = (f32[128,512]{1,0:T(8,128)S(1)}, f32[128,512]{1,0:T(8,128)}, u32[]{:S(2)}) copy-start(f32[128,512]{1,0:T(8,128)} %param.9) | copy-start | bytes 786436
  0.6 15.9 %collective-permute-start = (f32[2,128,512]{2,1,0:T(8,128)}, f32[2,128,512]{2,1,0:T(8,128)S(1)}, u32[]{:S(2)}, u32[]{:S(2)}) collective-permute-start(f32[2,128,512]{2,1,0:T(8,128)} %param.7), channel_id=1, source_target_pairs={{0,2},{1,3},{2,0},{3,1},{4,6},{5,7},{6,4},{7,5},{8,10},{9,11},{10,... | collective-permute-start | bytes 1572872 | tf_op jit(solution)/shard_map/ppermute | solution.py:47
  3.7 15.1 %collective-permute-start.2 = (f32[2,128,512]{2,1,0:T(8,128)}, f32[2,128,512]{2,1,0:T(8,128)S(1)}, u32[]{:S(2)}, u32[]{:S(2)}) collective-permute-start(f32[2,128,512]{2,1,0:T(8,128)} %param.7), channel_id=1, source_target_pairs={{0,1},{1,0},{2,3},{3,2},{4,5},{5,4},{6,7},{7,6},{8,9},{9,8},{10,11... | collective-permute-start | bytes 1572872 | tf_op jit(solution)/shard_map/ppermute | solution.py:47
  7.0 18.7 %copy-start.2 = (f32[2,128,512]{2,1,0:T(8,128)S(1)}, f32[2,128,512]{2,1,0:T(8,128)}, u32[]{:S(2)}) copy-start(f32[2,128,512]{2,1,0:T(8,128)} %param.7) | copy-start | bytes 1572868
  7.9 12.2 %collective-permute-start.6 = (f32[32,512]{1,0:T(8,128)S(1)}, f32[32,512]{1,0:T(8,128)S(1)}, u32[]{:S(2)}, u32[]{:S(2)}) collective-permute-start(f32[32,512]{1,0:T(8,128)S(1)} %constant_dynamic-slice_fusion), channel_id=1, source_target_pairs={{0,1},{1,0},{2,3},{3,2},{4,5},{5,4},{6,7},{7,6},{8,9},{9,8},{10,11... | collective-permute-start | bytes 196616 | tf_op jit(solution)/shard_map/ppermute | solution.py:47
  8.5 11.7 %collective-permute-start.5 = (f32[32,512]{1,0:T(8,128)S(1)}, f32[32,512]{1,0:T(8,128)S(1)}, u32[]{:S(2)}, u32[]{:S(2)}) collective-permute-start(f32[32,512]{1,0:T(8,128)S(1)} %constant_dynamic-slice_fusion), channel_id=1, source_target_pairs={{0,2},{1,3},{2,0},{3,1},{4,6},{5,7},{6,4},{7,5},{8,10},{9,11},{10,... | collective-permute-start | bytes 196616 | tf_op jit(solution)/shard_map/ppermute | solution.py:47
  8.5 12.5 %collective-permute-start.4 = (f32[32,512]{1,0:T(8,128)S(1)}, f32[32,512]{1,0:T(8,128)S(1)}, u32[]{:S(2)}, u32[]{:S(2)}) collective-permute-start(f32[32,512]{1,0:T(8,128)S(1)} %constant_dynamic-slice_fusion), channel_id=1, source_target_pairs={{0,3},{1,2},{2,1},{3,0},{4,7},{5,6},{6,5},{7,4},{8,11},{9,10},{10,... | collective-permute-start | bytes 196616 | tf_op jit(solution)/shard_map/ppermute | solution.py:47
  16.5 9.2 %collective-permute-start.1 = (f32[1,128,512]{2,1,0:T(8,128)S(1)}, f32[1,128,512]{2,1,0:T(8,128)S(1)}, u32[]{:S(2)}, u32[]{:S(2)}) collective-permute-start(f32[1,128,512]{2,1,0:T(8,128)S(1)} %slice.67), channel_id=1, source_target_pairs={{0,1},{1,0},{2,3},{3,2},{4,5},{5,4},{6,7},{7,6},{8,9},{9,8},{10,11... | collective-permute-start | bytes 786440 | tf_op jit(solution)/shard_map/ppermute | solution.py:47
  18.8 6.9 %collective-permute-start.3 = (f32[1,128,512]{2,1,0:T(8,128)S(1)}, f32[1,128,512]{2,1,0:T(8,128)S(1)}, u32[]{:S(2)}, u32[]{:S(2)}) collective-permute-start(f32[1,128,512]{2,1,0:T(8,128)S(1)} %slice.68), channel_id=1, source_target_pairs={{0,2},{1,3},{2,0},{3,1},{4,6},{5,7},{6,4},{7,5},{8,10},{9,11},{10,... | collective-permute-start | bytes 786440 | tf_op jit(solution)/shard_map/ppermute | solution.py:47
  21.1 8.3 %collective-permute-start.7 = (f32[4,32,512]{2,1,0:T(8,128)S(1)}, f32[4,32,512]{2,1,0:T(8,128)S(1)}, u32[]{:S(2)}, u32[]{:S(2)}) collective-permute-start(f32[4,32,512]{2,1,0:T(8,128)S(1)} %pad_maximum_fusion.6), channel_id=1, source_target_pairs={{0,8},{1,9},{2,10},{3,11},{4,12},{5,13},{6,14},{7,15},{8,0},{9,1},... | collective-permute-start | bytes 786440 | tf_op jit(solution)/shard_map/ppermute | solution.py:47
  29.4 3.4 %collective-permute-start.8 = (f32[512,512]{1,0:T(8,128)S(1)}, f32[512,512]{1,0:T(8,128)S(1)}, u32[]{:S(2)}, u32[]{:S(2)}) collective-permute-start(f32[512,512]{1,0:T(8,128)S(1)} %convolution_add_fusion), channel_id=1, source_target_pairs={{0,4},{1,5},{2,6},{3,7},{4,0},{5,1},{6,2},{7,3},{8,12},{9,13},{10,... | collective-permute-start | bytes 3145736 | tf_op jit(solution)/shard_map/ppermute | solution.py:47
  30.5 1.6 %collective-permute-start.9 = (f32[1,512]{1,0:T(1,128)S(1)}, f32[1,512]{1,0:T(1,128)S(1)}, u32[]{:S(2)}, u32[]{:S(2)}) collective-permute-start(f32[1,512]{1,0:T(1,128)S(1)} %slice_add_fusion), channel_id=1, source_target_pairs={{0,4},{1,5},{2,6},{3,7},{4,0},{5,1},{6,2},{7,3},{8,12},{9,13},{10,... | collective-permute-start | bytes 6152 | tf_op jit(solution)/shard_map/ppermute | solution.py:47
  31.2 6.8 %collective-permute-start.12 = (f32[2,4,32,512]{3,2,0,1:T(8,128)S(1)}, f32[2,4,32,512]{3,2,0,1:T(8,128)S(1)}, u32[]{:S(2)}, u32[]{:S(2)}) collective-permute-start(f32[2,4,32,512]{3,2,0,1:T(8,128)S(1)} %pad_maximum_fusion.4), channel_id=1, source_target_pairs={{0,4},{1,5},{2,6},{3,7},{4,0},{5,1},{6,2},{7,3},{8,12},{9,13},{10,... | collective-permute-start | bytes 1572872 | tf_op jit(solution)/shard_map/ppermute | solution.py:47
  32.7 1.2 %copy-start.3 = (f32[512]{0:T(512)S(1)}, f32[512]{0:T(512)}, u32[]{:S(2)}) copy-start(f32[512]{0:T(512)} %param.12) | copy-start | bytes 6148
  32.7 1.2 %collective-permute-start.10 = (f32[1,512]{1,0:T(1,128)S(1)}, f32[1,512]{1,0:T(1,128)S(1)}, u32[]{:S(2)}, u32[]{:S(2)}) collective-permute-start(f32[1,512]{1,0:T(1,128)S(1)} %convolution_add_fusion.11), channel_id=1, source_target_pairs={{0,4},{1,5},{2,6},{3,7},{4,0},{5,1},{6,2},{7,3},{8,12},{9,13},{10,... | collective-permute-start | bytes 6152 | tf_op jit(solution)/shard_map/ppermute | solution.py:47
  34.5 5.0 %collective-permute-start.11 = (f32[1,512]{1,0:T(1,128)S(1)}, f32[1,512]{1,0:T(1,128)S(1)}, u32[]{:S(2)}, u32[]{:S(2)}) collective-permute-start(f32[1,512]{1,0:T(1,128)S(1)} %convolution_add_fusion.12), channel_id=1, source_target_pairs={{0,8},{1,9},{2,10},{3,11},{4,12},{5,13},{6,14},{7,15}} | collective-permute-start | bytes 6152 | tf_op jit(solution)/shard_map/ppermute | solution.py:47
  38.2 1.1 %copy-start.4 = (f32[2,128]{1,0:T(2,128)S(1)}, f32[2,128]{1,0:T(2,128)}, u32[]{:S(2)}) copy-start(f32[2,128]{1,0:T(2,128)} %param.10) | copy-start | bytes 3076
  40.0 3.4 %collective-permute-start.13 = (f32[1,512]{1,0:T(1,128)S(1)}, f32[1,512]{1,0:T(1,128)S(1)}, u32[]{:S(2)}, u32[]{:S(2)}) collective-permute-start(f32[1,512]{1,0:T(1,128)S(1)} %convolution_add_fusion.10), channel_id=1, source_target_pairs={{8,16},{9,17},{10,18},{11,19},{12,20},{13,21},{14,22},{15,23}} | collective-permute-start | bytes 6152 | tf_op jit(solution)/shard_map/ppermute | solution.py:47
  41.3 2.0 %collective-permute-start.14 = (f32[256,512]{1,0:T(8,128)S(1)}, f32[256,512]{1,0:T(8,128)S(1)}, u32[]{:S(2)}, u32[]{:S(2)}) collective-permute-start(f32[256,512]{1,0:T(8,128)S(1)} %convolution_select_fusion), channel_id=1, source_target_pairs={{0,4},{1,5},{2,6},{3,7},{4,0},{5,1},{6,2},{7,3},{8,12},{9,13},{10,... | collective-permute-start | bytes 1572872 | tf_op jit(solution)/shard_map/ppermute | solution.py:47
  41.8 1.5 %collective-permute-start.15 = (f32[2,128]{1,0:T(2,128)S(1)}, f32[2,128]{1,0:T(2,128)S(1)}, u32[]{:S(2)}, u32[]{:S(2)}) collective-permute-start(f32[2,128]{1,0:T(2,128)S(1)} %add_select_fusion), channel_id=1, source_target_pairs={{0,4},{1,5},{2,6},{3,7},{4,0},{5,1},{6,2},{7,3},{8,12},{9,13},{10,... | collective-permute-start | bytes 3080 | tf_op jit(solution)/shard_map/ppermute | solution.py:47
  43.9 2.1 %collective-permute-start.16 = (f32[1,512]{1,0:T(1,128)S(1)}, f32[1,512]{1,0:T(1,128)S(1)}, u32[]{:S(2)}, u32[]{:S(2)}) collective-permute-start(f32[1,512]{1,0:T(1,128)S(1)} %convolution_add_fusion.9), channel_id=1, source_target_pairs={{16,24},{17,25},{18,26},{19,27},{20,28},{21,29},{22,30},{23,31}} | collective-permute-start | bytes 6152 | tf_op jit(solution)/shard_map/ppermute | solution.py:47
  45.9 1.0 %copy-start.1 = (f32[512,128]{1,0:T(8,128)S(1)}, f32[512,128]{1,0:T(8,128)}, u32[]{:S(2)}) copy-start(f32[512,128]{1,0:T(8,128)} %param.8) | copy-start | bytes 786436
  47.1 7.8 %collective-permute-start.19 = (f32[4,512]{1,0:T(4,128)S(1)}, f32[4,512]{1,0:T(4,128)S(1)}, u32[]{:S(2)}, u32[]{:S(2)}) collective-permute-start(f32[4,512]{1,0:T(4,128)S(1)} %fusion.25), channel_id=1, source_target_pairs={{24,0},{25,1},{26,2},{27,3},{28,4},{29,5},{30,6},{31,7}} | collective-permute-start | bytes 24584 | tf_op jit(solution)/shard_map/ppermute | solution.py:47
  48.4 6.5 %collective-permute-start.18 = (f32[4,512]{1,0:T(4,128)S(1)}, f32[4,512]{1,0:T(4,128)S(1)}, u32[]{:S(2)}, u32[]{:S(2)}) collective-permute-start(f32[4,512]{1,0:T(4,128)S(1)} %fusion.25), channel_id=1, source_target_pairs={{16,0},{17,1},{18,2},{19,3},{20,4},{21,5},{22,6},{23,7},{24,8},{25... | collective-permute-start | bytes 24584 | tf_op jit(solution)/shard_map/ppermute | solution.py:47
  49.7 5.6 %collective-permute-start.17 = (f32[4,512]{1,0:T(4,128)S(1)}, f32[4,512]{1,0:T(4,128)S(1)}, u32[]{:S(2)}, u32[]{:S(2)}) collective-permute-start(f32[4,512]{1,0:T(4,128)S(1)} %fusion.25), channel_id=1, source_target_pairs={{8,0},{9,1},{10,2},{11,3},{12,4},{13,5},{14,6},{15,7},{16,8},{17,9... | collective-permute-start | bytes 24584 | tf_op jit(solution)/shard_map/ppermute | solution.py:47
